TPU v7x, 512 devices: a whole 4x4x16 slice. The times are simulated.
512 devices in a mesh: domain: 64 (over x, y, z_lo), member: 8 (over z_hi, core).
Axes of the slice: x: 4, y: 4, z: 16 (z_hi: 4, z_lo: 4; z = z_hi * 4 + z_lo), core: 2. Of those that a mesh axis runs over, the one named last changes fastest.
Arguments:
- inputs: bfloat16 [16, 12288, 1024], P('member', 'domain')
- norm_gain: bfloat16 [1024], P('member'), may hold values from 0.099609375 to 1.8984375
- w_query: bfloat16 [1024, 512], P('member')
- w_key: bfloat16 [1024, 512], P('member')
- w_value: bfloat16 [1024, 512], P('member'), may hold values from -0.1875 to 0.1875
- w_out: bfloat16 [512, 1024], P('member'), may hold values from -0.75 to 0.75
- neighbors: int32 [192, 9], P('domain'), may hold values from 0 to 191, as said below
- slot_valid: int32 [192, 9], P('domain'), may hold values from 0 to 1, as said below
- output_cotangent: bfloat16 [16, 12288, 1024], P('member', 'domain'), may hold values from -1.5 to 1.5
Outputs:
- attn_out: bfloat16 [16, 12288, 1024], P('member', 'domain')
- d_input: bfloat16 [16, 12288, 1024], P('member', 'domain')
- grad_wout: float32 [512, 1024], P('member')
Inputs may be any that keep to these rules, and one draw needn't show every extreme that they name: `neighbors`: slot 0 of block b names b. The blocks named by the valid slots of b are distinct and lie within blocks (b // 3 - 1) * 3 to (b // 3 + 2) * 3 - 1. An invalid slot names b. `slot_valid`: slot 0 is always 1.
All inputs are finite; a program needn't handle non-finite values.
Results may differ from a plain program's by a relative error of at most 0.019.
Values may be sent and summed in bfloat16 or wider, within the bound.
No kernel may reach another device: no remote copies, remote signals or barrier semaphores. Data moves between devices by JAX's collectives and lax.ppermute only.
A program may use at most 128 MiB of HBM per device.

v0:
```python
import jax
import jax.numpy as jnp
from jax import lax
from jax.sharding import PartitionSpec as P

HEAD_DIM = 64


EPSILON = 1e-06
MASKED = -1e30


def extended_2(value, sides, width):
    for axis, dim in sides:
        peers, length = (lax.axis_size(axis), value.shape[dim])
        up = [(i, (i + 1) % peers) for i in range(peers - 1)]
        down = [(j, i) for i, j in up]
        last = lax.slice_in_dim(value, length - width, length, axis=dim)
        initial = lax.slice_in_dim(value, 0, width, axis=dim)
        before = lax.ppermute(last, axis, up)
        after = lax.ppermute(initial, axis, down)
        value = jnp.concatenate([before, value, after], axis=dim)
    return value


def pair_columns(field, pair_index, pair_width):
    return lax.dynamic_slice_in_dim(field, pair_index * pair_width, pair_width, field.ndim - 1)


def shards(
    inputs, norm_gain, w_query, w_key, w_value, w_out, neighbors, slot_valid, output_cotangent
):
    samples, length, model_width = inputs.shape
    block_count, slot_count = neighbors.shape
    block_len = length // block_count
    window_blocks = 3 * block_count
    full_gain, complete_query, complete_key, complete_value, complete_output = (
        lax.all_gather(norm_gain, "member", axis=0, tiled=True),
        lax.all_gather(w_query, "member", axis=0, tiled=True),
        lax.all_gather(w_key, "member", axis=0, tiled=True),
        lax.all_gather(w_value, "member", axis=0, tiled=True),
        lax.all_gather(w_out, "member", axis=0, tiled=True),
    )
    hidden_width = complete_query.shape[1]
    pair_width = 2 * HEAD_DIM
    pair_count = hidden_width // pair_width
    score_scale = HEAD_DIM ** (-0.5)
    inputs_float = inputs.astype(jnp.float32)
    inverse_rms = lax.rsqrt(jnp.mean(inputs_float * inputs_float, axis=-1, keepdims=True) + EPSILON)
    gain_float = full_gain.astype(jnp.float32)
    normalized_input = (inputs_float * inverse_rms * gain_float).astype(jnp.bfloat16)
    query = jnp.einsum(
        "fbi,iy->fby", normalized_input, complete_query, preferred_element_type=jnp.float32
    ).astype(jnp.bfloat16)
    key_rows = jnp.einsum(
        "fbi,iy->fby", normalized_input, complete_key, preferred_element_type=jnp.float32
    ).astype(jnp.bfloat16)
    value_rows = jnp.einsum(
        "fbi,iy->fby", normalized_input, complete_value, preferred_element_type=jnp.float32
    ).astype(jnp.bfloat16)
    key_value = jnp.concatenate([key_rows, value_rows], axis=-1)
    extended = extended_2(key_value, (("domain", 1),), length)
    domain_rank = lax.axis_index("domain")
    local_index = neighbors - (domain_rank - 1) * block_count
    present = slot_valid > 0
    window_ids = jnp.arange(window_blocks, dtype=jnp.int32)
    key_all = extended[..., :hidden_width]
    value_all = extended[..., hidden_width:]
    score_spec = "sbqgd,skgd->sbgqk"
    mix_spec = "sbgqk,skgd->sbqgd"
    back_spec = "sbgqk,sbqgd->skgd"
    matches = jnp.logical_and(
        local_index[:, :, None] == window_ids[None, None, :], present[:, :, None]
    )
    included = jnp.any(matches, axis=1)
    key_mask = jnp.repeat(included, block_len, axis=1)

    def pair_keys(pair_index):
        key_pair = pair_columns(key_all, pair_index, pair_width).reshape(
            samples, window_blocks * block_len, 2, HEAD_DIM
        )
        value_pair = pair_columns(value_all, pair_index, pair_width).reshape(
            samples, window_blocks * block_len, 2, HEAD_DIM
        )
        return (key_pair, value_pair)

    def to_window(grad_keys):
        return grad_keys.reshape(samples, window_blocks * block_len, pair_width)

    def pair_probability(pair_index):
        query_pair = pair_columns(query, pair_index, pair_width).reshape(
            samples, block_count, block_len, 2, HEAD_DIM
        )
        key_pair, value_pair = pair_keys(pair_index)
        scores = (
            jnp.einsum(score_spec, query_pair, key_pair, preferred_element_type=jnp.float32)
            * score_scale
        )
        scores = jnp.where(key_mask[None, :, None, None, :], scores, MASKED)
        row_max = jnp.max(scores, axis=-1, keepdims=True)
        shifted = jnp.exp(scores - row_max)
        probability = shifted / jnp.sum(shifted, axis=-1, keepdims=True)
        return (query_pair, key_pair, value_pair, probability)

    def forward_pair(pair_index):
        query_pair, key_pair, value_pair, probability = pair_probability(pair_index)
        prob_bf = probability.astype(jnp.bfloat16)
        mixed_pair = jnp.einsum(mix_spec, prob_bf, value_pair, preferred_element_type=jnp.float32)
        return mixed_pair.astype(jnp.bfloat16).reshape(samples, length, pair_width)

    attention_pairs = lax.map(forward_pair, jnp.arange(pair_count))
    neighbour_attention = jnp.transpose(attention_pairs, (1, 2, 0, 3)).reshape(
        samples, length, hidden_width
    )
    attn_out = jnp.einsum(
        "qny,yb->qnb", neighbour_attention, complete_output, preferred_element_type=jnp.float32
    ).astype(jnp.bfloat16)
    d_attention = jnp.einsum(
        "yjz,bz->yjb", output_cotangent, complete_output, preferred_element_type=jnp.float32
    ).astype(jnp.bfloat16)
    row_share = hidden_width // lax.axis_size("member")
    member_total = samples * lax.axis_size("member")
    incomplete_gradient = jnp.einsum(
        "rfe,rfu->eu", neighbour_attention, output_cotangent, preferred_element_type=jnp.float32
    )
    total_grad = lax.psum(incomplete_gradient, ("domain", "member"))
    grad_mine = lax.dynamic_slice_in_dim(
        total_grad, lax.axis_index("member") * row_share, row_share, 0
    )
    grad_wout = grad_mine / member_total

    def backward_pair(pair_index):
        query_pair, key_pair, value_pair, probability = pair_probability(pair_index)
        prob_bf = probability.astype(jnp.bfloat16)
        grad_pair = pair_columns(d_attention, pair_index, pair_width).reshape(
            samples, block_count, block_len, 2, HEAD_DIM
        )
        d_prob = jnp.einsum(score_spec, grad_pair, value_pair, preferred_element_type=jnp.float32)
        delta = jnp.sum(probability * d_prob, axis=-1, keepdims=True)
        d_score = (probability * (d_prob - delta) * score_scale).astype(jnp.bfloat16)
        d_query_pair = jnp.einsum(mix_spec, d_score, key_pair, preferred_element_type=jnp.float32)
        d_query_pair = d_query_pair.astype(jnp.bfloat16).reshape(samples, length, pair_width)
        d_key_pair = jnp.einsum(back_spec, d_score, query_pair, preferred_element_type=jnp.float32)
        d_value_pair = jnp.einsum(back_spec, prob_bf, grad_pair, preferred_element_type=jnp.float32)
        return (d_query_pair, to_window(d_key_pair), to_window(d_value_pair))

    query_grads, key_grads, value_grads = lax.map(backward_pair, jnp.arange(pair_count))
    query_cotangent = jnp.transpose(query_grads, (1, 2, 0, 3)).reshape(
        samples, length, hidden_width
    )
    key_ext = jnp.transpose(key_grads, (1, 2, 0, 3)).reshape(samples, 3 * length, hidden_width)
    value_ext = jnp.transpose(value_grads, (1, 2, 0, 3)).reshape(samples, 3 * length, hidden_width)
    ext_grad = jnp.concatenate([key_ext, value_ext], axis=-1)
    lower_rim = ext_grad[:, :length]
    own_part = ext_grad[:, length : 2 * length]
    upper_rim = ext_grad[:, 2 * length :]
    rims_half = jnp.concatenate([lower_rim, upper_rim], axis=1).astype(jnp.bfloat16)
    returned = extended_2(rims_half, (("domain", 1),), length)
    from_below = returned[:, :length].astype(jnp.float32)
    from_above = returned[:, 3 * length :].astype(jnp.float32)
    kv_total = own_part + from_below + from_above
    kv_grad = kv_total.astype(jnp.bfloat16)
    key_cotangent = kv_grad[..., :hidden_width]
    value_cotangent = kv_grad[..., hidden_width:]
    normed_cotangent = jnp.einsum(
        "qja,ga->qjg", query_cotangent, complete_query, preferred_element_type=jnp.float32
    )
    normed_cotangent = normed_cotangent + jnp.einsum(
        "qja,ga->qjg", key_cotangent, complete_key, preferred_element_type=jnp.float32
    )
    normed_cotangent = normed_cotangent + jnp.einsum(
        "qja,ga->qjg", value_cotangent, complete_value, preferred_element_type=jnp.float32
    )
    scaled_grad = normed_cotangent * gain_float
    inner_mean = jnp.mean(scaled_grad * inputs_float, axis=-1, keepdims=True)
    d_input = inverse_rms * scaled_grad - inputs_float * inverse_rms**3 * inner_mean
    return (attn_out, d_input.astype(jnp.bfloat16), grad_wout)


def solution(mesh):
    placed = (
        P("member", "domain", None),
        P("member"),
        P("member", None),
        P("member", None),
        P("member", None),
        P("member", None),
        P("domain", None),
        P("domain", None),
        P("member", "domain", None),
    )
    return jax.shard_map(
        shards,
        mesh=mesh,
        in_specs=placed,
        out_specs=(P("member", "domain", None), P("member", "domain", None), P("member", None)),
        check_vma=False,
    )
```

profile of v0, /device:TPU:1, one launch (start us, length us, event | category | flops | bytes accessed | tf_op | source)
XLA Modules:
  0.0 901.7 jit_solution(3319372591805515954)
XLA Ops:
  11.5 22.8 %all-gather = bf16[8,1,128]{2,1,0:T(2,128)(2,1)S(1)} all-gather(bf16[1,1,128]{2,1,0:T(2,128)(2,1)} %bitcast.205), channel_id=1, replica_groups=mesh['domain'=64,'member'=8] {'member'}, dimensions={0}, use_global_device_ids=true | all-gather | bytes 2304 | tf_op jit(solution)/shard_map/all_gather | solution.py:38
  35.0 28.1 %all-gather.8.cloned.1.call-done = bf16[1024,512]{1,0:T(8,128)(2,1)} async-done(((bf16[128,512]{1,0:T(8,128)(2,1)}), bf16[1024,512]{1,0:T(8,128)(2,1)}) %all-gather.8.cloned.1.call-update) | async-done | bytes 1048592 | tf_op jit(solution)/shard_map/all_gather | solution.py:41
  65.2 42.2 %all-gather.6.cloned.1.call-done = bf16[1024,512]{1,0:T(8,128)(2,1)} async-done(((bf16[128,512]{1,0:T(8,128)(2,1)}), bf16[1024,512]{1,0:T(8,128)(2,1)}) %all-gather.6.cloned.1.call-update) | async-done | bytes 1048592 | tf_op jit(solution)/shard_map/all_gather | solution.py:40
  111.5 4.9 collective-permute-start
  116.7 37.4 %all-gather.12.cloned.1.call-done = bf16[512,1024]{1,0:T(8,128)(2,1)} async-done(((bf16[64,1024]{1,0:T(8,128)(2,1)}), bf16[512,1024]{1,0:T(8,128)(2,1)}) %all-gather.12.cloned.1.call-update) | async-done | bytes 1048592 | tf_op jit(solution)/shard_map/all_gather | solution.py:42
  154.0 2.6 convolution_convert_fusion.2
  156.6 59.6 %all-gather.10.cloned.1.call-done = bf16[1024,512]{1,0:T(8,128)(2,1)} async-done(((bf16[128,512]{1,0:T(8,128)(2,1)}), bf16[1024,512]{1,0:T(8,128)(2,1)}) %all-gather.10.cloned.1.call-update) | async-done | bytes 1048592 | tf_op jit(solution)/shard_map/all_gather | solution.py:39
  216.2 2.6 convolution_convert_fusion.3
  224.2 34.7 %while.26 = (s32[]{:T(128)}, bf16[4,2,192,128]{3,2,1,0:T(8,128)(2,1)}, s32[4]{0:T(128)S(1)}, bf16[2,576,512]{1,2,0:T(8,128)(2,1)}, bf16[2,576,512]{1,2,0:T(8,128...) while((s32[]{:T(128)}, ...), condition=%wide.region_5.6_spmd.clone, body=%wide.region_2.5_spmd.clone.sunk | while | flops 117278592 | bytes 8469142 | solution.py:111
  259.7 121.8 %while.27 = (s32[]{:T(128)}, bf16[4,2,192,128]{3,2,1,0:T(8,128)(2,1)}, f32[4,2,576,128]{2,3,1,0:T(8,128)}, f32[4,2,576,128]{2,3,1,0:T(8,128)}, s32[4]{0:T(128)S(...) while((s32[]{:T(128)}, ...), condition=%wide.region_10.11_spmd.clone, body=%wide.region_6.0_spmd.clone.sunk | while | flops 293343744 | bytes 26301140 | solution.py:147
  269.1 7.8 fusion.143
  278.8 2.4 fusion.144
  281.2 7.7 fusion.145
  299.5 7.8 fusion.143
  309.2 2.4 fusion.144
  311.6 7.7 fusion.145
  329.9 7.8 fusion.143
  339.6 2.4 fusion.144
  342.0 7.7 fusion.145
  360.4 7.8 fusion.143
  370.1 2.4 fusion.144
  372.5 7.7 fusion.145
  381.4 3.2 copy.65
  386.8 3.5 constant_dynamic-update-slice_fusion.5
  390.2 2.6 copy.66
  392.8 2.7 reshape.82
  397.3 2.7 convert.6
  402.3 4.9 collective-permute-start.2
  409.3 2.8 convolution_convert_fusion.1
  412.7 9.3 %collective-permute-done.3 = bf16[2,192,1024]{2,1,0:T(8,128)(2,1)} collective-permute-done((bf16[2,192,1024]{2,1,0:T(8,128)(2,1)}, bf16[2,192,1024]{2,1,0:T(8,128)(2,1)}, u32[]{:S(2)}, u32[]{:S(2)}) %collective-permute-start.3) | collective-permute-done | bytes 786464 | tf_op jit(solution)/shard_map/ppermute | solution.py:21
  422.6 2.2 fusion.58
  428.5 465.0 %all-reduce.2.cloned.1.call-done = f32[512,1024]{1,0:T(8,128)} async-done(((f32[512,1024]{1,0:T(8,128)}), f32[512,1024]{1,0:T(8,128)}) %all-reduce.2.cloned.1.call-update) | async-done | bytes 2097168 | tf_op jit(solution)/shard_map/psum | solution.py:126
  (198 shorter events, 111.2 us)
Async XLA Ops:
  7.2 146.9 %copy-start = (bf16[2,192,1024]{2,1,0:T(8,128)(2,1)S(1)}, bf16[2,192,1024]{2,1,0:T(8,128)(2,1)}, u32[]{:S(2)}) copy-start(bf16[2,192,1024]{2,1,0:T(8,128)(2,1)} %param.21) | copy-start | bytes 2359300
  7.2 55.9 %all-gather.8.cloned.1.call-start = ((), (), s32[]{:S(2)}) async-start(), calls=%async_computation.1 | async-start | bytes 1179648 | tf_op jit(solution)/shard_map/all_gather | solution.py:41
  7.9 99.4 %all-gather.6.cloned.1.call-start = ((), (), s32[]{:S(2)}) async-start(), calls=%async_computation | async-start | bytes 1179648 | tf_op jit(solution)/shard_map/all_gather | solution.py:40
  8.7 145.4 %all-gather.12.cloned.1.call-start = ((), (), s32[]{:S(2)}) async-start(), calls=%async_computation.3 | async-start | bytes 1179648 | tf_op jit(solution)/shard_map/all_gather | solution.py:42
  9.4 206.8 %all-gather.10.cloned.1.call-start = ((), (), s32[]{:S(2)}) async-start(), calls=%async_computation.2 | async-start | bytes 1179648 | tf_op jit(solution)/shard_map/all_gather | solution.py:39
  10.0 97.4 %copy-start.2 = (bf16[2,192,1024]{2,1,0:T(8,128)(2,1)S(1)}, bf16[2,192,1024]{2,1,0:T(8,128)(2,1)}, u32[]{:S(2)}) copy-start(bf16[2,192,1024]{2,1,0:T(8,128)(2,1)} %param.13) | copy-start | bytes 2359300
  10.0 883.5 %all-reduce.2.cloned.1.call-start = ((), (), s32[]{:S(2)}) async-start(), calls=%async_computation.4 | async-start | bytes 4194304 | tf_op jit(solution)/shard_map/psum | solution.py:126
  65.1 51.2 %copy-start.10 = (s32[3,9]{1,0:T(4,128)S(1)}, s32[3,9]{1,0:T(4,128)}, u32[]{:S(2)}) copy-start(s32[3,9]{1,0:T(4,128)} %param.20) | copy-start | bytes 328
  110.2 108.6 %collective-permute-start.1 = (bf16[2,192,1024]{2,1,0:T(8,128)(2,1)}, bf16[2,192,1024]{2,1,0:T(8,128)(2,1)S(1)}, u32[]{:S(2)}, u32[]{:S(2)}) collective-permute-start(bf16[2,192,1024]{2,1,0:T(8,128)(2,1)} %pad_maximum_fusion.1), channel_id=1, source_target_pairs={{8,0},{16,8},{24,16},{32,24},{40,32},{48,40},{56,48},{64,56},{72,6... | collective-permute-start | bytes 2359304 | tf_op jit(solution)/shard_map/ppermute | solution.py:21
  111.5 107.3 %collective-permute-start = (bf16[2,192,1024]{2,1,0:T(8,128)(2,1)}, bf16[2,192,1024]{2,1,0:T(8,128)(2,1)}, u32[]{:S(2)}, u32[]{:S(2)}) collective-permute-start(bf16[2,192,1024]{2,1,0:T(8,128)(2,1)} %pad_maximum_fusion.1), channel_id=1, source_target_pairs={{0,8},{8,16},{16,24},{24,32},{32,40},{40,48},{48,56},{56,64},{64,7... | collective-permute-start | bytes 2359304 | tf_op jit(solution)/shard_map/ppermute | solution.py:20
  281.2 7.7 copy-start.1
  311.6 7.7 copy-start.1
  342.0 7.7 copy-start.1
  372.5 7.7 copy-start.1
  386.8 3.5 copy-start.4
  400.0 7.2 copy-start.5
  401.0 21.0 %collective-permute-start.3 = (bf16[2,192,1024]{2,1,0:T(8,128)(2,1)}, bf16[2,192,1024]{2,1,0:T(8,128)(2,1)}, u32[]{:S(2)}, u32[]{:S(2)}) collective-permute-start(bf16[2,192,1024]{2,1,0:T(8,128)(2,1)} %get-tuple-element.247), channel_id=1, source_target_pairs={{8,0},{16,8},{24,16},{32,24},{40,32},{48,40},{56,48},{64,56},{72,6... | collective-permute-start | bytes 2359304 | tf_op jit(solution)/shard_map/ppermute | solution.py:21
  402.3 20.3 %collective-permute-start.2 = (bf16[2,192,1024]{2,1,0:T(8,128)(2,1)S(1)}, bf16[2,192,1024]{2,1,0:T(8,128)(2,1)}, u32[]{:S(2)}, u32[]{:S(2)}) collective-permute-start(bf16[2,192,1024]{2,1,0:T(8,128)(2,1)S(1)} %get-tuple-element.246), channel_id=1, source_target_pairs={{0,8},{8,16},{16,24},{24,32},{32,40},{40,48},{48,56},{56,64},{64,7... | collective-permute-start | bytes 2359304 | tf_op jit(solution)/shard_map/ppermute | solution.py:20
  409.3 2.8 copy-start.6
  409.3 2.8 copy-start.8
  412.7 12.2 %copy-start.7 = (bf16[1024,512]{1,0:T(8,128)(2,1)S(1)}, bf16[1024,512]{1,0:T(8,128)(2,1)}, u32[]{:S(2)}) copy-start(bf16[1024,512]{1,0:T(8,128)(2,1)} %all-gather.6.cloned.1.call-done) | copy-start | bytes 3145732
  424.9 1.1 copy-start.3
  424.9 1.5 copy-start.9
Sparse Core Ops, SparseCore 0:
  10.1 52.8 all-gather.7
  65.2 42.0 all-gather.5
  109.5 44.4 all-gather.11
  156.0 60.1 all-gather.9
  409.4 484.0 all-reduce.1
where the time goes:
time: 903 us; the launch traced here: 902 us
  waiting for transfers between devices  645 us (71%)
  matrix products  106 us (12%)
  local copies, waits for them, and re-layouts  73.6 us (8%)
  blocking collectives  22.8 us (3%)
  other arithmetic  22.2 us (2%)
  between operations  14 us (2%)
  starting transfers between devices  12.5 us (1%)
    psum x1, waiting for transfers between devices, shards(): total_grad = lax.psum(incomplete_gradient, ('domain', 'member'))  465 us
    all_gather x1, waiting for transfers between devices, shards(): lax.all_gather(w_query, 'member', axis=0, tiled=True)  59.6 us
    all_gather x1, waiting for transfers between devices, shards(): lax.all_gather(w_key, 'member', axis=0, tiled=True)  42.2 us
    all_gather x1, waiting for transfers between devices, shards(): lax.all_gather(w_out, 'member', axis=0, tiled=True)  37.4 us
    dot_general x4, matrix products, backward_pair(): jnp.einsum(mix_spec, d_score, key_pair, preferred_element_type=jnp.float32)  31.3 us
    dot_general x4, matrix products, backward_pair(): jnp.einsum(back_spec, d_score, query_pair, preferred_element_type=jnp.flo...  30.7 us
    all_gather x1, waiting for transfers between devices, shards(): lax.all_gather(w_value, 'member', axis=0, tiled=True)  28.1 us
    dynamic_slice x24, local copies, waits for them, and re-layouts, pair_columns(): lax.dynamic_slice_in_dim(field, pair_index * pair_width, pair_width, fiel...  23.5 us
  transfers between devices with their start and end apart: 9, of which 7 were waited for; matrix products, arithmetic and copies ran while one was open for 3% of the time, Pallas kernels for 0%

commit v1 on v0

v1 whole, which is shorter than its diff:
```python
import jax
import jax.numpy as jnp
from jax import lax
from jax.experimental import pallas as pl
from jax.experimental.pallas import tpu as pltpu
from jax.sharding import Mesh
from jax.sharding import PartitionSpec as P


HEAD_DIM = 64
PAIR = 2 * HEAD_DIM
EPSILON = 1e-06
MASKED = -1e30
X, Y, ZL, ZH, CORE = "x", "y", "zl", "zh", "core"
DOMAIN = (X, Y, ZL)
MEMBER = (ZH, CORE)
PLANE = (X, Y)
COLUMN = (ZL, ZH)
BF16, F32 = jnp.bfloat16, jnp.float32


def contract(a, b, da, db):
    return lax.dot_general(a, b, (((da,), (db,)), ((), ())), preferred_element_type=F32)


def attention_kernel(
    bias_ref, q_ref, k_ref, v_ref, g_ref, att_ref, dq_ref, low_ref, own_ref, high_ref
):
    rows = q_ref.shape[1]
    span = k_ref.shape[1]
    near = lax.broadcasted_iota(jnp.int32, (1, PAIR), 1) < HEAD_DIM

    def stacked(both):
        zero = jnp.zeros_like(both)
        return jnp.concatenate([jnp.where(near, both, zero), jnp.where(near, zero, both)], axis=0)

    def merged(columns):
        both = columns.T
        return jnp.where(near, both[:rows], both[rows:])

    query, key, value, grad = (stacked(q_ref[0]), k_ref[0], v_ref[0], stacked(g_ref[0]))
    blocks = bias_ref.shape[0]
    scores = contract(key, query, 1, 1).reshape(blocks, span // blocks, 2 * rows)
    scores = (scores + bias_ref[...]).reshape(span, 2 * rows)
    shifted = jnp.exp(scores - jnp.max(scores, axis=0, keepdims=True))
    prob = shifted * (1.0 / jnp.sum(shifted, axis=0, keepdims=True))
    prob_bf = prob.astype(BF16)
    att_ref[0] = merged(contract(value, prob_bf, 0, 0)).astype(BF16)
    d_prob = contract(value, grad, 1, 1)
    delta = jnp.sum(prob * d_prob, axis=0, keepdims=True)
    d_score = (prob * (d_prob - delta)).astype(BF16)
    dq_ref[0] = (merged(contract(key, d_score, 0, 0)) * HEAD_DIM**-0.5).astype(BF16)
    third = span // 3
    for part, total in enumerate((contract(d_score, query, 1, 0), contract(prob_bf, grad, 1, 0))):
        low_ref[part, 0] = total[:third].astype(BF16)
        own_ref[part, 0] = total[third : 2 * third]
        high_ref[part, 0] = total[2 * third :].astype(BF16)


def attention(bias, query, key_value, grad):
    samples, rows, width = query.shape
    span = key_value.shape[1]
    pairs = width // PAIR
    shape = jax.ShapeDtypeStruct
    narrow = pl.BlockSpec((1, rows, PAIR), lambda s, h: (s, 0, h))
    split = pl.BlockSpec((2, 1, rows, PAIR), lambda s, h: (0, s, 0, h))
    return pl.pallas_call(
        attention_kernel,
        grid=(samples, pairs),
        in_specs=[
            pl.BlockSpec(bias.shape, lambda s, h: (0, 0, 0)),
            narrow,
            pl.BlockSpec((1, span, PAIR), lambda s, h: (s, 0, h)),
            pl.BlockSpec((1, span, PAIR), lambda s, h: (s, 0, h + pairs)),
            narrow,
        ],
        out_specs=[narrow, narrow, split, split, split],
        out_shape=[
            shape((samples, rows, width), BF16),
            shape((samples, rows, width), BF16),
            shape((2, samples, rows, width), BF16),
            shape((2, samples, rows, width), F32),
            shape((2, samples, rows, width), BF16),
        ],
        cost_estimate=pl.CostEstimate(
            flops=12 * samples * rows * span * width,
            transcendentals=samples * rows * span * width // HEAD_DIM,
            bytes_accessed=16 * samples * rows * width,
        ),
        compiler_params=pltpu.CompilerParams(vmem_limit_bytes=48 * 2**20),
    )(bias, query, key_value, key_value, grad)


def column_gather(part):
    count = lax.axis_size(ZH)
    place = lax.axis_index(ZH)
    pieces = [part] + [
        lax.ppermute(part, ZH, [(i, (i + step) % count) for i in range(count)])
        for step in range(1, count)
    ]
    turned = jnp.stack(pieces[::-1] * 2)
    return lax.dynamic_slice_in_dim(turned, count - 1 - place, count, 0)


def other_core(value):
    return lax.ppermute(value, CORE, [(0, 1), (1, 0)])


def both_cores(mine):
    theirs = other_core(mine)
    first = lax.axis_index(CORE) == 0
    return jnp.stack([jnp.where(first, mine, theirs), jnp.where(first, theirs, mine)])


def plane_gather(piece):
    count = lax.axis_size(PLANE)
    copies = jnp.broadcast_to(piece[None], (count,) + piece.shape)
    return lax.all_to_all(copies, PLANE, 0, 0, tiled=True)


def gathered_weights(norm_gain, w_query, w_key, w_value, w_out):
    nx, ny, nz = (lax.axis_size(X), lax.axis_size(Y), lax.axis_size(ZH))
    xi, yi = (lax.axis_index(X), lax.axis_index(Y))
    depth, hidden_width = w_query.shape
    out_depth, model_width = w_out.shape
    rows = depth // (nx * ny)
    start = (xi * ny + yi) * rows
    out_rows, out_columns = (out_depth // nx, model_width // ny)
    out_part = lax.dynamic_slice(w_out, (xi * out_rows, yi * out_columns), (out_rows, out_columns))
    folds = out_rows // rows
    part = [lax.dynamic_slice_in_dim(w, start, rows, 0) for w in (w_query, w_key, w_value)]
    part += [out_part[i * rows : (i + 1) * rows] for i in range(folds)]
    part += [jnp.broadcast_to(norm_gain[None], (rows, depth))]
    part = column_gather(jnp.concatenate(part, axis=1))
    width = 3 * hidden_width + folds * out_columns
    gain = both_cores(part[:, :, width:])[:, :, 0]
    gain = jnp.swapaxes(gain, 0, 1).reshape(-1)
    whole = plane_gather(part[:, :, :width])
    whole = both_cores(whole)
    joint = jnp.transpose(whole[..., : 3 * hidden_width], (2, 0, 1, 3, 4))
    joint = joint.reshape(2 * nz * depth, 3 * hidden_width)
    whole = whole.reshape(2, nx, ny, nz, rows, width)
    bands = []
    for i in range(folds):
        begin = 3 * hidden_width + i * out_columns
        bands.append(jnp.transpose(whole[..., begin : begin + out_columns], (2, 3, 0, 1, 4, 5)))
    bands = jnp.stack(bands, axis=4).reshape(ny, 2 * nz * out_depth, out_columns)
    out_whole = jnp.concatenate([bands[i] for i in range(ny)], axis=1)
    return gain, joint, out_whole


def halved_gradient(attended, cotangent):
    nz = lax.axis_size(ZH)
    partial = jnp.einsum("sre,sru->eu", attended, cotangent, preferred_element_type=F32)
    width, model_width = partial.shape
    partial = partial.reshape(nz, 2, width // (2 * nz), model_width)
    first = lax.axis_index(CORE) == 0
    kept = jnp.where(first, partial[:, 0], partial[:, 1])
    sent = jnp.where(first, partial[:, 1], partial[:, 0])
    return (kept + other_core(sent)).astype(BF16)


def summed_gradient(half, total_samples):
    nx, ny, nz, nl = (lax.axis_size(X), lax.axis_size(Y), lax.axis_size(ZH), lax.axis_size(ZL))
    _, share, model_width = half.shape
    rows, columns = (share // nx, model_width // ny)
    half = jnp.stack([half[:, :, i * columns : (i + 1) * columns] for i in range(ny)])
    half = jnp.swapaxes(half.reshape(ny, nz, nx, rows, columns), 1, 2)
    half = half.reshape(ny * nx, nz, rows, columns)
    half = lax.all_to_all(half, (Y, X), 0, 0, tiled=True)
    part = jnp.sum(half.astype(F32), axis=0)
    part = jnp.broadcast_to(part[None], (nl, nz, rows, columns)).reshape(nl * nz, rows, columns)
    part = lax.all_to_all(part, COLUMN, 0, 0, tiled=True)
    part = jnp.sum(part, axis=0) / total_samples
    whole = plane_gather(part).reshape(nx, ny, rows, columns)
    return jnp.concatenate([whole[:, i].reshape(share, columns) for i in range(ny)], axis=1)


def shards(
    inputs, norm_gain, w_query, w_key, w_value, w_out, neighbors, slot_valid, output_cotangent
):
    samples, length, _ = inputs.shape
    block_count, _ = neighbors.shape
    block_len = length // block_count
    window_blocks = 3 * block_count
    groups = lax.axis_size(DOMAIN)
    up = [(i, i + 1) for i in range(groups - 1)]
    down = [(j, i) for i, j in up]
    below = lax.ppermute(inputs, DOMAIN, up)
    above = lax.ppermute(inputs, DOMAIN, down)
    gain, w_joint, w_full_out = gathered_weights(norm_gain, w_query, w_key, w_value, w_out)
    hidden_width = w_query.shape[1]
    gain_float = gain.astype(F32)

    def normalized(rows):
        rows = rows.astype(F32)
        inverse = lax.rsqrt(jnp.mean(rows * rows, axis=-1, keepdims=True) + EPSILON)
        return inverse, (rows * inverse * gain_float).astype(BF16)

    inverse_rms, normed = normalized(inputs)
    _, window = normalized(jnp.concatenate([below, inputs, above], axis=1))
    query = jnp.einsum(
        "sti,iy->sty", normed, w_joint[:, :hidden_width], preferred_element_type=F32
    ).astype(BF16) * jnp.asarray(HEAD_DIM**-0.5, BF16)
    key_value = jnp.einsum(
        "sti,iy->sty", window, w_joint[:, hidden_width:], preferred_element_type=F32
    ).astype(BF16)
    d_attention = jnp.einsum(
        "stz,yz->sty", output_cotangent, w_full_out, preferred_element_type=F32
    ).astype(BF16)

    group = lax.axis_index(DOMAIN)
    local_index = neighbors - (group - 1) * block_count
    matches = jnp.logical_and(
        local_index[:, :, None] == jnp.arange(window_blocks, dtype=jnp.int32)[None, None, :],
        (slot_valid > 0)[:, :, None],
    )
    bias = jnp.where(jnp.any(matches, axis=1).T, 0.0, MASKED).astype(F32)
    bias = jnp.tile(jnp.repeat(bias, block_len, axis=1), (1, 2))[:, None, :]

    attended, d_query, low, own, high = attention(bias, query, key_value, d_attention)
    half = halved_gradient(attended, output_cotangent)
    half, low, high, attended = lax.optimization_barrier((half, low, high, attended))
    from_below = lax.ppermute(high, DOMAIN, up)
    from_above = lax.ppermute(low, DOMAIN, down)
    attn_out = jnp.einsum(
        "sty,yb->stb", attended, w_full_out, preferred_element_type=F32
    ).astype(BF16)
    members = lax.axis_size(MEMBER)
    grad_wout = summed_gradient(half, samples * members)
    d_key_value = (own + from_below.astype(F32) + from_above.astype(F32)).astype(BF16)
    d_joint = jnp.concatenate([d_query, d_key_value[0], d_key_value[1]], axis=-1)
    d_normed = jnp.einsum("sty,iy->sti", d_joint, w_joint, preferred_element_type=F32)
    inputs_float = inputs.astype(F32)
    scaled = d_normed * gain_float
    inner = jnp.mean(scaled * inputs_float, axis=-1, keepdims=True)
    d_input = inverse_rms * scaled - inputs_float * inverse_rms**3 * inner
    return attn_out, d_input.astype(BF16), grad_wout


def solution(mesh):
    fine = Mesh(mesh.devices.reshape(4, 4, 4, 4, 2), (X, Y, ZL, ZH, CORE))
    placed = (
        P(MEMBER, DOMAIN, None),
        P(MEMBER),
        P(MEMBER, None),
        P(MEMBER, None),
        P(MEMBER, None),
        P(MEMBER, None),
        P(DOMAIN, None),
        P(DOMAIN, None),
        P(MEMBER, DOMAIN, None),
    )

    return jax.shard_map(
        shards,
        mesh=fine,
        in_specs=placed,
        out_specs=(P(MEMBER, DOMAIN, None), P(MEMBER, DOMAIN, None), P(MEMBER, None)),
        check_vma=False,
    )
```

time: 903 us -> 222 us (0.25)
  the two profiles are of different devices: /device:TPU:1 before, /device:TPU:32 now
where the time goes in v1:
time: 222 us; the launch traced here: 221 us
  starting transfers between devices  73.7 us (33%)
  waiting for transfers between devices  68.2 us (31%)
  blocking collectives  33.7 us (15%)
  Pallas kernels  14.6 us (7%)
  other arithmetic  11 us (5%)
  matrix products  10.1 us (5%)
  local copies, waits for them, and re-layouts  8.46 us (4%)
    all_to_all x1, blocking collectives, plane_gather(): return lax.all_to_all(copies, PLANE, 0, 0, tiled=True)  33.7 us
    ppermute x3, starting transfers between devices, column_gather(): lax.ppermute(part, ZH, [(i, (i + step) % count) for i in range(count)])  24.6 us
    all_to_all x1, starting transfers between devices, summed_gradient(): part = lax.all_to_all(part, COLUMN, 0, 0, tiled=True)  23 us
    ppermute x1, waiting for transfers between devices, shards(): above = lax.ppermute(inputs, DOMAIN, down)  17.9 us
    all_to_all x1, waiting for transfers between devices, summed_gradient(): part = lax.all_to_all(part, COLUMN, 0, 0, tiled=True)  15.4 us
    pallas_call x1, Pallas kernels, attention(): pl.pallas_call(attention_kernel, grid=(samples, pairs), in_specs=[pl.Bloc...  14.6 us
    ppermute x1, waiting for transfers between devices, shards(): below = lax.ppermute(inputs, DOMAIN, up)  11.6 us
    all_to_all x1, waiting for transfers between devices, summed_gradient(): half = lax.all_to_all(half, (Y, X), 0, 0, tiled=True)  8.92 us
  transfers between devices with their start and end apart: 13, of which 8 were waited for; matrix products, arithmetic and copies ran while one was open for 6% of the time, Pallas kernels for 0%

profile of v1, /device:TPU:32, one launch (start us, length us, event | category | flops | bytes accessed | tf_op | source)
XLA Modules:
  0.0 221.0 jit_solution(139674404218422932)
XLA Ops:
  0.7 0.8 constant_dynamic-update-slice_fusion.5
  4.9 11.8 %collective-permute-start = (bf16[8,2176]{1,0:T(8,128)(2,1)S(1)}, bf16[8,2176]{1,0:T(8,128)(2,1)S(1)}, u32[]{:S(2)}, u32[]{:S(2)}) collective-permute-start(bf16[8,2176]{1,0:T(8,128)(2,1)S(1)} %constant_dynamic-update-slice_fusion), channel_id=1, source_target_pairs={{0,6},{2,0},{4,2},{6,4},{1,7},{3,1},{5,3},{7,5},{8,14},{10,8},{12,... | collective-permute-start | bytes 104456 | tf_op jit(solution)/shard_map/ppermute | solution.py:98
  16.7 1.9 collective-permute-start.2
  18.6 10.8 %collective-permute-start.1 = (bf16[8,2176]{1,0:T(8,128)(2,1)S(1)}, bf16[8,2176]{1,0:T(8,128)(2,1)S(1)}, u32[]{:S(2)}, u32[]{:S(2)}) collective-permute-start(bf16[8,2176]{1,0:T(8,128)(2,1)S(1)} %constant_dynamic-update-slice_fusion), channel_id=1, source_target_pairs={{0,4},{2,6},{4,0},{6,2},{1,5},{3,7},{5,1},{7,3},{8,12},{10,14},{12... | collective-permute-start | bytes 104456 | tf_op jit(solution)/shard_map/ppermute | solution.py:98
  29.5 3.8 %collective-permute-done.1 = bf16[8,2176]{1,0:T(8,128)(2,1)S(1)} collective-permute-done((bf16[8,2176]{1,0:T(8,128)(2,1)S(1)}, bf16[8,2176]{1,0:T(8,128)(2,1)S(1)}, u32[]{:S(2)}, u32[]{:S(2)}) %collective-permute-start.1) | collective-permute-done | bytes 34848 | tf_op jit(solution)/shard_map/ppermute | solution.py:98
  33.7 33.7 %all_to_all.20 = bf16[16,4,8,2048]{3,2,1,0:T(8,128)(2,1)} all-to-all(bf16[16,4,8,2048]{3,2,1,0:T(8,128)(2,1)S(1)} %broadcast_in_dim.22), channel_id=1, replica_groups=mesh['x'=4,'y'=4,'zl'=4,'zh'=4,'core'=2] {'x','y'}, dimensions={0} | all-to-all | bytes 4194304 | tf_op jit(solution)/shard_map/all_to_all | solution.py:118
  67.4 1.9 collective-permute-start.4
  69.3 2.9 %collective-permute-start.5 = (bf16[2,192,1024]{2,1,0:T(8,128)(2,1)S(1)}, bf16[2,192,1024]{2,1,0:T(8,128)(2,1)S(1)}, u32[]{:S(2)}, u32[]{:S(2)}) collective-permute-start(bf16[2,192,1024]{2,1,0:T(8,128)(2,1)S(1)} %copy-done.3), channel_id=1, source_target_pairs={{0,8},{8,16},{16,24},{24,32},{32,40},{40,48},{48,56},{56,64},{64,7... | collective-permute-start | bytes 2359304 | tf_op jit(solution)/shard_map/ppermute | solution.py:189
  72.3 2.9 %collective-permute-start.6 = (bf16[2,192,1024]{2,1,0:T(8,128)(2,1)S(1)}, bf16[2,192,1024]{2,1,0:T(8,128)(2,1)S(1)}, u32[]{:S(2)}, u32[]{:S(2)}) collective-permute-start(bf16[2,192,1024]{2,1,0:T(8,128)(2,1)S(1)} %copy-done.3), channel_id=1, source_target_pairs={{8,0},{16,8},{24,16},{32,24},{40,32},{48,40},{56,48},{64,56},{72,6... | collective-permute-start | bytes 2359304 | tf_op jit(solution)/shard_map/ppermute | solution.py:190
  76.4 1.9 collective-permute-start.3
  79.5 11.6 %collective-permute-done.5 = bf16[2,192,1024]{2,1,0:T(8,128)(2,1)S(1)} collective-permute-done((bf16[2,192,1024]{2,1,0:T(8,128)(2,1)S(1)}, bf16[2,192,1024]{2,1,0:T(8,128)(2,1)S(1)}, u32[]{:S(2)}, u32[]{:S(2)}) %collective-permute-start.5) | collective-permute-done | bytes 786464 | tf_op jit(solution)/shard_map/ppermute | solution.py:189
  91.2 17.9 %collective-permute-done.6 = bf16[2,192,1024]{2,1,0:T(8,128)(2,1)S(1)} collective-permute-done((bf16[2,192,1024]{2,1,0:T(8,128)(2,1)S(1)}, bf16[2,192,1024]{2,1,0:T(8,128)(2,1)S(1)}, u32[]{:S(2)}, u32[]{:S(2)}) %collective-permute-start.6) | collective-permute-done | bytes 786464 | tf_op jit(solution)/shard_map/ppermute | solution.py:190
  109.6 2.5 %broadcast_select_fusion.1 = (bf16[16,4,8,2048]{3,2,1,0:T(8,128)(2,1)S(1)}, bf16[16,4,8,2048]{3,2,1,0:T(8,128)(2,1)S(1)}) fusion(bf16[16,4,8,2048]{3,2,1,0:T(8,128)(2,1)} %all_to_all.20, bf16[16,4,8,2048]{3,2,1,0:T(8,128)(2,1)} %collective-permute-done.4, pred[]{:T(512)S(6)} %eq.8), kind=kLoop, calls=%fused_computation.17 | loop fusion | flops 2097152 | bytes 8388609 | tf_op jit(solution)/shard_map/jit(_where)/select_n | solution.py:112
  115.0 3.9 %fusion.8.k_ref.v_ref = bf16[2,576,1024]{2,1,0:T(8,128)(2,1)} fusion(bf16[1024,1536]{1,0:T(8,128)(2,1)S(1)} %bitcast.115, f32[1024]{0:T(1024)S(1)} %bitcast.133, f32[2,576]{1,0:T(2,128)S(1)} %add_rsqrt_fusion, bf16[2,192,1024]{2,1,0:T(8,128)(2,1)S(1)} %collective-permute-done.6, bf16[2,192,1024]{2,1,0:T(8,128)(2,1)S(1)} %copy-done.3, ...), kind=kOutput, calls=%fused_computation.18 | convolution fusion | flops 2427715584 | bytes 6824960 | tf_op jit(solution)/shard_map/sti,iy->sty/dot_general | solution.py:205
  118.9 14.6 %shard_map.112 = (bf16[2,192,512]{2,1,0:T(8,128)(2,1)S(1)}, bf16[2,192,512]{2,1,0:T(8,128)(2,1)S(1)}, bf16[2,2,192,512]{3,2,1,0:T(8,128)(2,1)S(1)}, f32[2,2,192,...) custom-call(f32[9,1,384]{2,1,0:T(1,128)S(1)} %tile.11.bias_ref, bf16[2,192,512]{2,1,0:T(8,128)(2,1)S(1)} %fusion.19.q_ref, ...), custom_call_target="tpu_custom_call" | custom-call | flops 1358954496 | bytes 3145728 | tf_op jit(solution)/shard_map/pallas_call | solution.py:67
  134.4 2.0 collective-permute-start.7
  136.4 2.6 %collective-permute-done.7 = f32[4,64,1024]{2,1,0:T(8,128)S(1)} collective-permute-done((f32[4,64,1024]{2,1,0:T(8,128)S(1)}, f32[4,64,1024]{2,1,0:T(8,128)S(1)}, u32[]{:S(2)}, u32[]{:S(2)}) %collective-permute-start.7) | collective-permute-done | bytes 1048608 | tf_op jit(solution)/shard_map/ppermute | solution.py:106
  139.4 2.5 %collective-permute-start.8 = (bf16[2,2,192,512]{3,2,1,0:T(8,128)(2,1)}, bf16[2,2,192,512]{3,2,1,0:T(8,128)(2,1)}, u32[]{:S(2)}, u32[]{:S(2)}) collective-permute-start(bf16[2,2,192,512]{3,2,1,0:T(8,128)(2,1)} %get-tuple-element.18), channel_id=1, source_target_pairs={{0,8},{8,16},{16,24},{24,32},{32,40},{40,48},{48,56},{56,64},{64,7... | collective-permute-start | bytes 2359304 | tf_op jit(solution)/shard_map/ppermute | solution.py:224
  141.9 4.2 %collective-permute-start.9 = (bf16[2,2,192,512]{3,2,1,0:T(8,128)(2,1)S(1)}, bf16[2,2,192,512]{3,2,1,0:T(8,128)(2,1)}, u32[]{:S(2)}, u32[]{:S(2)}) collective-permute-start(bf16[2,2,192,512]{3,2,1,0:T(8,128)(2,1)S(1)} %get-tuple-element.19), channel_id=1, source_target_pairs={{8,0},{16,8},{24,16},{32,24},{40,32},{48,40},{56,48},{64,56},{72,6... | collective-permute-start | bytes 2359304 | tf_op jit(solution)/shard_map/ppermute | solution.py:225
  146.3 0.9 pad_maximum_fusion.6
  147.1 4.2 %all-to-all-start.1 = ((bf16[16,4,16,256]{3,2,1,0:T(8,128)(2,1)}), bf16[16,4,16,256]{3,2,1,0:T(8,128)(2,1)}, u32[]{:S(2)}, u32[]{:S(2)}) async-start(bf16[16,4,16,256]{3,2,1,0:T(8,128)(2,1)} %bitcast.117), calls=%async_computation.1 | async-start | bytes 1048576 | tf_op jit(solution)/shard_map/all_to_all | solution.py:170
  151.4 2.6 %convolution_convert_fusion = bf16[2,192,1024]{2,1,0:T(8,128)(2,1)} fusion(bf16[2,192,512]{2,1,0:T(8,128)(2,1)S(1)} %get-tuple-element.15, bf16[512,256]{1,0:T(8,128)(2,1)} %bitcast.124, bf16[512,256]{1,0:T(8,128)(2,1)} %bitcast.126, bf16[512,256]{1,0:T(8,128)(2,1)} %bitcast.122, bf16[512,256]{1,0:T(8,128)(2,1)} %bitcast.120), kind=kOutput, calls=%fused_computation.28 | convolution fusion | flops 407240704 | bytes 2228224 | tf_op jit(solution)/shard_map/sty,yb->stb/dot_general | solution.py:226
  154.0 8.9 %all-to-all-done.1 = bf16[16,4,16,256]{3,2,1,0:T(8,128)(2,1)} async-done(((bf16[16,4,16,256]{3,2,1,0:T(8,128)(2,1)}), bf16[16,4,16,256]{3,2,1,0:T(8,128)(2,1)}, u32[]{:S(2)}, u32[]{:S(2)}) %all-to-all-start.1) | async-done | bytes 524320 | tf_op jit(solution)/shard_map/all_to_all | solution.py:170
  163.0 1.1 convert_reduce_fusion
  164.8 23.0 %all-to-all-start.2 = ((f32[16,16,256]{2,1,0:T(8,128)}), f32[16,16,256]{2,1,0:T(8,128)S(1)}, u32[]{:S(2)}, u32[]{:S(2)}) async-start(f32[16,16,256]{2,1,0:T(8,128)} %bitcast.45), calls=%async_computation.2 | async-start | bytes 524288 | tf_op jit(solution)/shard_map/all_to_all | solution.py:173
  187.9 1.9 add_convert_fusion
  189.8 0.8 copy-done.6
  190.6 1.5 fusion.17
  192.1 15.4 %all-to-all-done.2 = f32[16,16,256]{2,1,0:T(8,128)S(1)} async-done(((f32[16,16,256]{2,1,0:T(8,128)}), f32[16,16,256]{2,1,0:T(8,128)S(1)}, u32[]{:S(2)}, u32[]{:S(2)}) %all-to-all-start.2) | async-done | bytes 262176 | tf_op jit(solution)/shard_map/all_to_all | solution.py:173
  208.3 3.5 %all-to-all-start.3 = ((f32[16,16,256]{2,1,0:T(8,128)}), f32[16,16,256]{2,1,0:T(8,128)S(1)}, u32[]{:S(2)}, u32[]{:S(2)}) async-start(f32[16,16,256]{2,1,0:T(8,128)} %broadcast_in_dim.24), calls=%async_computation.3 | async-start | bytes 524288 | tf_op jit(solution)/shard_map/all_to_all | solution.py:118
  211.8 1.2 fusion.16
  213.1 7.2 %all-to-all-done.3 = f32[16,16,256]{2,1,0:T(8,128)S(1)} async-done(((f32[16,16,256]{2,1,0:T(8,128)}), f32[16,16,256]{2,1,0:T(8,128)S(1)}, u32[]{:S(2)}, u32[]{:S(2)}) %all-to-all-start.3) | async-done | bytes 262176 | tf_op jit(solution)/shard_map/all_to_all | solution.py:118
  (96 shorter events, 13.0 us)
Async XLA Ops:
  0.6 113.7 %copy-start = (bf16[2,192,1024]{2,1,0:T(8,128)(2,1)S(1)}, bf16[2,192,1024]{2,1,0:T(8,128)(2,1)}, u32[]{:S(2)}) copy-start(bf16[2,192,1024]{2,1,0:T(8,128)(2,1)} %param.17) | copy-start | bytes 2359300
  4.9 24.6 %collective-permute-start = (bf16[8,2176]{1,0:T(8,128)(2,1)S(1)}, bf16[8,2176]{1,0:T(8,128)(2,1)S(1)}, u32[]{:S(2)}, u32[]{:S(2)}) collective-permute-start(bf16[8,2176]{1,0:T(8,128)(2,1)S(1)} %constant_dynamic-update-slice_fusion), channel_id=1, source_target_pairs={{0,6},{2,0},{4,2},{6,4},{1,7},{3,1},{5,3},{7,5},{8,14},{10,8},{12,... | collective-permute-start | bytes 104456 | tf_op jit(solution)/shard_map/ppermute | solution.py:98
  16.7 16.6 %collective-permute-start.2 = (bf16[8,2176]{1,0:T(8,128)(2,1)S(1)}, bf16[8,2176]{1,0:T(8,128)(2,1)S(1)}, u32[]{:S(2)}, u32[]{:S(2)}) collective-permute-start(bf16[8,2176]{1,0:T(8,128)(2,1)S(1)} %constant_dynamic-update-slice_fusion), channel_id=1, source_target_pairs={{0,2},{2,4},{4,6},{6,0},{1,3},{3,5},{5,7},{7,1},{8,10},{10,12},{12... | collective-permute-start | bytes 104456 | tf_op jit(solution)/shard_map/ppermute | solution.py:98
  18.6 14.7 %collective-permute-start.1 = (bf16[8,2176]{1,0:T(8,128)(2,1)S(1)}, bf16[8,2176]{1,0:T(8,128)(2,1)S(1)}, u32[]{:S(2)}, u32[]{:S(2)}) collective-permute-start(bf16[8,2176]{1,0:T(8,128)(2,1)S(1)} %constant_dynamic-update-slice_fusion), channel_id=1, source_target_pairs={{0,4},{2,6},{4,0},{6,2},{1,5},{3,7},{5,1},{7,3},{8,12},{10,14},{12... | collective-permute-start | bytes 104456 | tf_op jit(solution)/shard_map/ppermute | solution.py:98
  33.6 35.7 %copy-start.3 = (bf16[2,192,1024]{2,1,0:T(8,128)(2,1)S(1)}, bf16[2,192,1024]{2,1,0:T(8,128)(2,1)}, u32[]{:S(2)}) copy-start(bf16[2,192,1024]{2,1,0:T(8,128)(2,1)} %param.9) | copy-start | bytes 2359300
  33.7 41.6 %copy-start.16 = (s32[3,9]{1,0:T(4,128)S(1)}, s32[3,9]{1,0:T(4,128)}, u32[]{:S(2)}) copy-start(s32[3,9]{1,0:T(4,128)} %param.16) | copy-start | bytes 328
  33.7 41.7 %copy-start.17 = (s32[3,9]{1,0:T(4,128)S(1)}, s32[3,9]{1,0:T(4,128)}, u32[]{:S(2)}) copy-start(s32[3,9]{1,0:T(4,128)} %param.15) | copy-start | bytes 328
  67.4 42.2 %collective-permute-start.4 = (bf16[16,4,8,2048]{3,2,1,0:T(8,128)(2,1)}, bf16[16,4,8,2048]{3,2,1,0:T(8,128)(2,1)}, u32[]{:S(2)}, u32[]{:S(2)}) collective-permute-start(bf16[16,4,8,2048]{3,2,1,0:T(8,128)(2,1)} %all_to_all.20), channel_id=1, source_target_pairs={{0,1},{1,0},{2,3},{3,2},{4,5},{5,4},{6,7},{7,6},{8,9},{9,8},{10,11... | collective-permute-start | bytes 6291464 | tf_op jit(solution)/shard_map/ppermute | solution.py:106
  69.3 21.8 %collective-permute-start.5 = (bf16[2,192,1024]{2,1,0:T(8,128)(2,1)S(1)}, bf16[2,192,1024]{2,1,0:T(8,128)(2,1)S(1)}, u32[]{:S(2)}, u32[]{:S(2)}) collective-permute-start(bf16[2,192,1024]{2,1,0:T(8,128)(2,1)S(1)} %copy-done.3), channel_id=1, source_target_pairs={{0,8},{8,16},{16,24},{24,32},{32,40},{40,48},{48,56},{56,64},{64,7... | collective-permute-start | bytes 2359304 | tf_op jit(solution)/shard_map/ppermute | solution.py:189
  72.3 36.8 %collective-permute-start.6 = (bf16[2,192,1024]{2,1,0:T(8,128)(2,1)S(1)}, bf16[2,192,1024]{2,1,0:T(8,128)(2,1)S(1)}, u32[]{:S(2)}, u32[]{:S(2)}) collective-permute-start(bf16[2,192,1024]{2,1,0:T(8,128)(2,1)S(1)} %copy-done.3), channel_id=1, source_target_pairs={{8,0},{16,8},{24,16},{32,24},{40,32},{48,40},{56,48},{64,56},{72,6... | collective-permute-start | bytes 2359304 | tf_op jit(solution)/shard_map/ppermute | solution.py:190
  76.3 36.9 %copy-start.12 = (f32[2,192]{1,0:T(2,128)}, f32[2,192]{1,0:T(2,128)S(1)}, u32[]{:S(2)}) copy-start(f32[2,192]{1,0:T(2,128)S(1)} %get-tuple-element.46) | copy-start | bytes 4612
  76.4 3.1 %collective-permute-start.3 = (bf16[4,8,128]{2,1,0:T(8,128)(2,1)S(1)}, bf16[4,8,128]{2,1,0:T(8,128)(2,1)S(1)}, u32[]{:S(2)}, u32[]{:S(2)}) collective-permute-start(bf16[4,8,128]{2,1,0:T(8,128)(2,1)S(1)} %constant_dynamic-slice_fusion), channel_id=1, source_target_pairs={{0,1},{1,0},{2,3},{3,2},{4,5},{5,4},{6,7},{7,6},{8,9},{9,8},{10,11... | collective-permute-start | bytes 24584 | tf_op jit(solution)/shard_map/ppermute | solution.py:106
  79.5 35.4 %copy-start.14 = (f32[4,2,128]{2,1,0:T(2,128)}, f32[4,2,128]{2,1,0:T(2,128)S(1)}, u32[]{:S(2)}) copy-start(f32[4,2,128]{2,1,0:T(2,128)S(1)} %copy.41) | copy-start | bytes 12292
  112.8 2.2 copy-start.5
  113.2 1.1 copy-start.9
  113.2 1.2 copy-start.10
  113.2 1.8 copy-start.7
  113.2 1.8 copy-start.8
  133.5 0.9 copy-start.1
  134.4 4.6 %collective-permute-start.7 = (f32[4,64,1024]{2,1,0:T(8,128)S(1)}, f32[4,64,1024]{2,1,0:T(8,128)S(1)}, u32[]{:S(2)}, u32[]{:S(2)}) collective-permute-start(f32[4,64,1024]{2,1,0:T(8,128)S(1)} %select_bitcast_fusion), channel_id=1, source_target_pairs={{0,1},{1,0},{2,3},{3,2},{4,5},{5,4},{6,7},{7,6},{8,9},{9,8},{10,11... | collective-permute-start | bytes 3145736 | tf_op jit(solution)/shard_map/ppermute | solution.py:106
  139.4 48.4 %collective-permute-start.8 = (bf16[2,2,192,512]{3,2,1,0:T(8,128)(2,1)}, bf16[2,2,192,512]{3,2,1,0:T(8,128)(2,1)}, u32[]{:S(2)}, u32[]{:S(2)}) collective-permute-start(bf16[2,2,192,512]{3,2,1,0:T(8,128)(2,1)} %get-tuple-element.18), channel_id=1, source_target_pairs={{0,8},{8,16},{16,24},{24,32},{32,40},{40,48},{48,56},{56,64},{64,7... | collective-permute-start | bytes 2359304 | tf_op jit(solution)/shard_map/ppermute | solution.py:224
  141.9 45.9 %collective-permute-start.9 = (bf16[2,2,192,512]{3,2,1,0:T(8,128)(2,1)S(1)}, bf16[2,2,192,512]{3,2,1,0:T(8,128)(2,1)}, u32[]{:S(2)}, u32[]{:S(2)}) collective-permute-start(bf16[2,2,192,512]{3,2,1,0:T(8,128)(2,1)S(1)} %get-tuple-element.19), channel_id=1, source_target_pairs={{8,0},{16,8},{24,16},{32,24},{40,32},{48,40},{56,48},{64,56},{72,6... | collective-permute-start | bytes 2359304 | tf_op jit(solution)/shard_map/ppermute | solution.py:225
  147.1 15.8 %all-to-all-start.1 = ((bf16[16,4,16,256]{3,2,1,0:T(8,128)(2,1)}), bf16[16,4,16,256]{3,2,1,0:T(8,128)(2,1)}, u32[]{:S(2)}, u32[]{:S(2)}) async-start(bf16[16,4,16,256]{3,2,1,0:T(8,128)(2,1)} %bitcast.117), calls=%async_computation.1 | async-start | bytes 1048576 | tf_op jit(solution)/shard_map/all_to_all | solution.py:170
  164.8 42.7 %all-to-all-start.2 = ((f32[16,16,256]{2,1,0:T(8,128)}), f32[16,16,256]{2,1,0:T(8,128)S(1)}, u32[]{:S(2)}, u32[]{:S(2)}) async-start(f32[16,16,256]{2,1,0:T(8,128)} %bitcast.45), calls=%async_computation.2 | async-start | bytes 524288 | tf_op jit(solution)/shard_map/all_to_all | solution.py:173
  187.8 2.0 copy-start.2
  187.9 2.0 copy-start.4
  187.9 2.7 %copy-start.6 = (bf16[4,2,16,8,1536]{4,3,2,1,0:T(8,128)(2,1)S(1)}, bf16[4,2,16,8,1536]{4,3,2,1,0:T(8,128)(2,1)}, u32[]{:S(2)}) copy-start(bf16[4,2,16,8,1536]{4,3,2,1,0:T(8,128)(2,1)} %copy-done.5) | copy-start | bytes 9437188
  187.9 2.7 %copy-start.15 = (f32[4,2,128]{2,1,0:T(2,128)S(1)}, f32[4,2,128]{2,1,0:T(2,128)}, u32[]{:S(2)}) copy-start(f32[4,2,128]{2,1,0:T(2,128)} %copy-done.14) | copy-start | bytes 12292
  190.6 21.2 %copy-start.11 = (f32[2,192]{1,0:T(2,128)S(1)}, f32[2,192]{1,0:T(2,128)}, u32[]{:S(2)}) copy-start(f32[2,192]{1,0:T(2,128)} %get-tuple-element.45) | copy-start | bytes 4612
  190.6 21.2 %copy-start.13 = (f32[2,192]{1,0:T(2,128)S(1)}, f32[2,192]{1,0:T(2,128)}, u32[]{:S(2)}) copy-start(f32[2,192]{1,0:T(2,128)} %copy-done.12) | copy-start | bytes 4612
  208.3 12.0 %all-to-all-start.3 = ((f32[16,16,256]{2,1,0:T(8,128)}), f32[16,16,256]{2,1,0:T(8,128)S(1)}, u32[]{:S(2)}, u32[]{:S(2)}) async-start(f32[16,16,256]{2,1,0:T(8,128)} %broadcast_in_dim.24), calls=%async_computation.3 | async-start | bytes 524288 | tf_op jit(solution)/shard_map/all_to_all | solution.py:118

commit v2 on v1

--- a/solution.py
+++ b/solution.py
@@ -23,29 +23,48 @@
     return lax.dot_general(a, b, (((da,), (db,)), ((), ())), preferred_element_type=F32)
 
 
-def attention_kernel(
-    bias_ref, q_ref, k_ref, v_ref, g_ref, att_ref, dq_ref, low_ref, own_ref, high_ref
+def head_lanes():
+    return lax.broadcasted_iota(jnp.int32, (1, PAIR), 1) < HEAD_DIM
+
+
+def stacked(both):
+    near = head_lanes()
+    zero = jnp.zeros_like(both)
+    return jnp.concatenate([jnp.where(near, both, zero), jnp.where(near, zero, both)], axis=0)
+
+
+def merged(columns):
+    both = columns.T
+    rows = both.shape[0] // 2
+    return jnp.where(head_lanes(), both[:rows], both[rows:])
+
+
+def masked_scores(bias_ref, key, query):
+    blocks = bias_ref.shape[0]
+    span, columns = (key.shape[0], query.shape[0])
+    scores = contract(key, query, 1, 1).reshape(blocks, span // blocks, columns)
+    return (scores + bias_ref[...]).reshape(span, columns)
+
+
+def forward_kernel(bias_ref, q_ref, k_ref, v_ref, att_ref, stat_ref):
+    scores = masked_scores(bias_ref, k_ref[0], stacked(q_ref[0]))
+    row_max = jnp.max(scores, axis=0, keepdims=True)
+    shifted = jnp.exp(scores - row_max)
+    inverse = 1.0 / jnp.sum(shifted, axis=0, keepdims=True)
+    prob_bf = (shifted * inverse).astype(BF16)
+    att_ref[0] = merged(contract(v_ref[0], prob_bf, 0, 0)).astype(BF16)
+    stat_ref[0, 0, 0:1, :] = row_max
+    stat_ref[0, 0, 1:2, :] = inverse
+
+
+def backward_kernel(
+    bias_ref, q_ref, k_ref, v_ref, g_ref, stat_ref, dq_ref, low_ref, own_ref, high_ref
 ):
-    rows = q_ref.shape[1]
-    span = k_ref.shape[1]
-    near = lax.broadcasted_iota(jnp.int32, (1, PAIR), 1) < HEAD_DIM
-
-    def stacked(both):
-        zero = jnp.zeros_like(both)
-        return jnp.concatenate([jnp.where(near, both, zero), jnp.where(near, zero, both)], axis=0)
-
-    def merged(columns):
-        both = columns.T
-        return jnp.where(near, both[:rows], both[rows:])
-
     query, key, value, grad = (stacked(q_ref[0]), k_ref[0], v_ref[0], stacked(g_ref[0]))
-    blocks = bias_ref.shape[0]
-    scores = contract(key, query, 1, 1).reshape(blocks, span // blocks, 2 * rows)
-    scores = (scores + bias_ref[...]).reshape(span, 2 * rows)
-    shifted = jnp.exp(scores - jnp.max(scores, axis=0, keepdims=True))
-    prob = shifted * (1.0 / jnp.sum(shifted, axis=0, keepdims=True))
+    span = key.shape[0]
+    scores = masked_scores(bias_ref, key, query)
+    prob = jnp.exp(scores - stat_ref[0, 0, 0:1, :]) * stat_ref[0, 0, 1:2, :]
     prob_bf = prob.astype(BF16)
-    att_ref[0] = merged(contract(value, prob_bf, 0, 0)).astype(BF16)
     d_prob = contract(value, grad, 1, 1)
     delta = jnp.sum(prob * d_prob, axis=0, keepdims=True)
     d_score = (prob * (d_prob - delta)).astype(BF16)
@@ -57,48 +76,112 @@
         high_ref[part, 0] = total[2 * third :].astype(BF16)
 
 
-def attention(bias, query, key_value, grad):
+def attention_specs(bias, query, key_value):
     samples, rows, width = query.shape
     span = key_value.shape[1]
     pairs = width // PAIR
+    narrow = pl.BlockSpec((1, rows, PAIR), lambda s, h: (s, 0, h))
+    given = [
+        pl.BlockSpec(bias.shape, lambda s, h: (0, 0, 0)),
+        narrow,
+        pl.BlockSpec((1, span, PAIR), lambda s, h: (s, 0, h)),
+        pl.BlockSpec((1, span, PAIR), lambda s, h: (s, 0, h + pairs)),
+    ]
+    stat = pl.BlockSpec((1, 1, 2, 2 * rows), lambda s, h: (s, h, 0, 0))
+    stat_shape = jax.ShapeDtypeStruct((samples, pairs, 2, 2 * rows), F32)
+    return (samples, pairs), given, narrow, stat, stat_shape
+
+
+def attention_cost(query, key_value, products):
+    samples, rows, width = query.shape
+    span = key_value.shape[1]
+    return pl.CostEstimate(
+        flops=2 * products * samples * rows * span * width,
+        transcendentals=samples * rows * span * width // HEAD_DIM,
+        bytes_accessed=3 * products * samples * rows * width,
+    )
+
+
+def forward_attention(bias, query, key_value):
+    grid, given, narrow, stat, stat_shape = attention_specs(bias, query, key_value)
+    return pl.pallas_call(
+        forward_kernel,
+        grid=grid,
+        in_specs=given,
+        out_specs=[narrow, stat],
+        out_shape=[jax.ShapeDtypeStruct(query.shape, BF16), stat_shape],
+        cost_estimate=attention_cost(query, key_value, 2),
+        compiler_params=pltpu.CompilerParams(vmem_limit_bytes=40 * 2**20),
+    )(bias, query, key_value, key_value)
+
+
+def backward_attention(bias, query, key_value, grad, stats):
+    grid, given, narrow, stat, _ = attention_specs(bias, query, key_value)
+    samples, rows, width = query.shape
     shape = jax.ShapeDtypeStruct
-    narrow = pl.BlockSpec((1, rows, PAIR), lambda s, h: (s, 0, h))
     split = pl.BlockSpec((2, 1, rows, PAIR), lambda s, h: (0, s, 0, h))
     return pl.pallas_call(
-        attention_kernel,
-        grid=(samples, pairs),
-        in_specs=[
-            pl.BlockSpec(bias.shape, lambda s, h: (0, 0, 0)),
-            narrow,
-            pl.BlockSpec((1, span, PAIR), lambda s, h: (s, 0, h)),
-            pl.BlockSpec((1, span, PAIR), lambda s, h: (s, 0, h + pairs)),
-            narrow,
-        ],
-        out_specs=[narrow, narrow, split, split, split],
+        backward_kernel,
+        grid=grid,
+        in_specs=given + [narrow, stat],
+        out_specs=[narrow, split, split, split],
         out_shape=[
-            shape((samples, rows, width), BF16),
             shape((samples, rows, width), BF16),
             shape((2, samples, rows, width), BF16),
             shape((2, samples, rows, width), F32),
             shape((2, samples, rows, width), BF16),
         ],
-        cost_estimate=pl.CostEstimate(
-            flops=12 * samples * rows * span * width,
-            transcendentals=samples * rows * span * width // HEAD_DIM,
-            bytes_accessed=16 * samples * rows * width,
+        cost_estimate=attention_cost(query, key_value, 5),
+        compiler_params=pltpu.CompilerParams(vmem_limit_bytes=40 * 2**20),
+    )(bias, query, key_value, key_value, grad, stats)
+
+
+def slice_kernel(place_ref, q_ref, k_ref, v_ref, out_ref, gain_ref, part_ref):
+    rows, width = q_ref.shape
+    columns = out_ref.shape[1]
+    folds = out_ref.shape[0] // rows
+    for i, ref in enumerate((q_ref, k_ref, v_ref)):
+        part_ref[:, i * width : (i + 1) * width] = ref[...]
+    for i in range(folds):
+        begin = 3 * width + i * columns
+        part_ref[:, begin : begin + columns] = out_ref[i * rows : (i + 1) * rows, :]
+    begin = 3 * width + folds * columns
+    part_ref[:, begin:] = jnp.broadcast_to(gain_ref[...], (rows, gain_ref.shape[1]))
+
+
+def own_slices(norm_gain, w_query, w_key, w_value, w_out, rows, out_rows, out_columns):
+    depth, width = w_query.shape
+    xi, yi = (lax.axis_index(X), lax.axis_index(Y))
+    place = jnp.stack([xi * lax.axis_size(Y) + yi, xi, yi])
+    band = pl.BlockSpec((rows, width), lambda i, place: (place[0], 0))
+    total = 3 * width + out_rows // rows * out_columns + depth
+    return pl.pallas_call(
+        slice_kernel,
+        grid_spec=pltpu.PrefetchScalarGridSpec(
+            num_scalar_prefetch=1,
+            grid=(1,),
+            in_specs=[
+                band,
+                band,
+                band,
+                pl.BlockSpec((out_rows, out_columns), lambda i, place: (place[1], place[2])),
+                pl.BlockSpec((1, depth), lambda i, place: (0, 0)),
+            ],
+            out_specs=pl.BlockSpec((rows, total), lambda i, place: (0, 0)),
         ),
-        compiler_params=pltpu.CompilerParams(vmem_limit_bytes=48 * 2**20),
-    )(bias, query, key_value, key_value, grad)
+        out_shape=jax.ShapeDtypeStruct((rows, total), BF16),
+    )(place, w_query, w_key, w_value, w_out, norm_gain[None])
 
 
 def column_gather(part):
     count = lax.axis_size(ZH)
     place = lax.axis_index(ZH)
-    pieces = [part] + [
-        lax.ppermute(part, ZH, [(i, (i + step) % count) for i in range(count)])
-        for step in range(1, count)
-    ]
-    turned = jnp.stack(pieces[::-1] * 2)
+    up = [(i, (i + 1) % count) for i in range(count)]
+    down = [(j, i) for i, j in up]
+    first = lax.ppermute(part, ZH, up)
+    third = lax.ppermute(part, ZH, down)
+    second = lax.ppermute(first, ZH, up)
+    turned = jnp.stack([third, second, first, part] * 2)
     return lax.dynamic_slice_in_dim(turned, count - 1 - place, count, 0)
 
 
@@ -120,18 +203,13 @@
 
 def gathered_weights(norm_gain, w_query, w_key, w_value, w_out):
     nx, ny, nz = (lax.axis_size(X), lax.axis_size(Y), lax.axis_size(ZH))
-    xi, yi = (lax.axis_index(X), lax.axis_index(Y))
     depth, hidden_width = w_query.shape
     out_depth, model_width = w_out.shape
     rows = depth // (nx * ny)
-    start = (xi * ny + yi) * rows
     out_rows, out_columns = (out_depth // nx, model_width // ny)
-    out_part = lax.dynamic_slice(w_out, (xi * out_rows, yi * out_columns), (out_rows, out_columns))
     folds = out_rows // rows
-    part = [lax.dynamic_slice_in_dim(w, start, rows, 0) for w in (w_query, w_key, w_value)]
-    part += [out_part[i * rows : (i + 1) * rows] for i in range(folds)]
-    part += [jnp.broadcast_to(norm_gain[None], (rows, depth))]
-    part = column_gather(jnp.concatenate(part, axis=1))
+    part = own_slices(norm_gain, w_query, w_key, w_value, w_out, rows, out_rows, out_columns)
+    part = column_gather(part)
     width = 3 * hidden_width + folds * out_columns
     gain = both_cores(part[:, :, width:])[:, :, 0]
     gain = jnp.swapaxes(gain, 0, 1).reshape(-1)
@@ -218,16 +296,18 @@
     bias = jnp.where(jnp.any(matches, axis=1).T, 0.0, MASKED).astype(F32)
     bias = jnp.tile(jnp.repeat(bias, block_len, axis=1), (1, 2))[:, None, :]
 
-    attended, d_query, low, own, high = attention(bias, query, key_value, d_attention)
+    attended, stats = forward_attention(bias, query, key_value)
     half = halved_gradient(attended, output_cotangent)
-    half, low, high, attended = lax.optimization_barrier((half, low, high, attended))
+    half, d_attention = lax.optimization_barrier((half, d_attention))
+    members = lax.axis_size(MEMBER)
+    grad_wout = summed_gradient(half, samples * members)
+    d_query, low, own, high = backward_attention(bias, query, key_value, d_attention, stats)
     from_below = lax.ppermute(high, DOMAIN, up)
     from_above = lax.ppermute(low, DOMAIN, down)
+    attended, own = lax.optimization_barrier((attended, own))
     attn_out = jnp.einsum(
         "sty,yb->stb", attended, w_full_out, preferred_element_type=F32
     ).astype(BF16)
-    members = lax.axis_size(MEMBER)
-    grad_wout = summed_gradient(half, samples * members)
     d_key_value = (own + from_below.astype(F32) + from_above.astype(F32)).astype(BF16)
     d_joint = jnp.concatenate([d_query, d_key_value[0], d_key_value[1]], axis=-1)
     d_normed = jnp.einsum("sty,iy->sti", d_joint, w_joint, preferred_element_type=F32)

time: 222 us -> 225 us (1.014)
  Pallas kernels: 14.6 us -> 19.6 us
  waiting for transfers between devices: 68.2 us -> 64.6 us
  other arithmetic: 11 us -> 13.9 us
    pallas_call x1 -> x3, Pallas kernels: 14.6 us -> 19.6 us  [the longest x1 9.86 us: backward_attention(): pl.pallas_call(backward_kernel, grid=grid, in_specs=given + [narrow, stat...]
    ppermute x3, starting transfers between devices: 24.6 us -> 20.1 us  [the longest x1 9.08 us: column_gather(): first = lax.ppermute(part, ZH, up)]
    all_to_all x1, starting transfers between devices: 3.53 us -> 6.88 us  [plane_gather(): return lax.all_to_all(copies, PLANE, 0, 0, tiled=True)]
    unnamed x48 -> x45, local copies, waits for them, and re-layouts: 4.93 us -> 3.61 us
  transfers between devices with their start and end apart: 13 -> 13, of which waited for: 8 -> 9; matrix products, arithmetic and copies ran while one was open for 6% -> 7% of each run, Pallas kernels for 0% -> 0%
where the time goes in v2:
time: 225 us; the launch traced here: 224 us
  starting transfers between devices  73.8 us (33%)
  waiting for transfers between devices  64.6 us (29%)
  blocking collectives  33.7 us (15%)
  Pallas kernels  19.6 us (9%)
  other arithmetic  13.9 us (6%)
  matrix products  10.1 us (4%)
  local copies, waits for them, and re-layouts  7.26 us (3%)
    all_to_all x1, blocking collectives, plane_gather(): return lax.all_to_all(copies, PLANE, 0, 0, tiled=True)  33.7 us
    all_to_all x1, starting transfers between devices, summed_gradient(): part = lax.all_to_all(part, COLUMN, 0, 0, tiled=True)  24.2 us
    ppermute x1, waiting for transfers between devices, shards(): above = lax.ppermute(inputs, DOMAIN, down)  18.2 us
    all_to_all x1, waiting for transfers between devices, summed_gradient(): part = lax.all_to_all(part, COLUMN, 0, 0, tiled=True)  14.4 us
    ppermute x1, waiting for transfers between devices, shards(): below = lax.ppermute(inputs, DOMAIN, up)  11.6 us
    pallas_call x1, Pallas kernels, backward_attention(): pl.pallas_call(backward_kernel, grid=grid, in_specs=given + [narrow, stat...  9.86 us
    ppermute x1, starting transfers between devices, column_gather(): first = lax.ppermute(part, ZH, up)  9.08 us
    all_to_all x1, waiting for transfers between devices, summed_gradient(): half = lax.all_to_all(half, (Y, X), 0, 0, tiled=True)  8.92 us
  transfers between devices with their start and end apart: 13, of which 9 were waited for; matrix products, arithmetic and copies ran while one was open for 7% of the time, Pallas kernels for 0%

profile of v2, /device:TPU:32, one launch (start us, length us, event | category | flops | bytes accessed | tf_op | source)
XLA Modules:
  0.0 224.2 jit_solution(3043299874234073252)
XLA Ops:
  1.3 2.0 shard_map.112
  3.3 9.1 %collective-permute-start.1 = (bf16[8,2176]{1,0:T(8,128)(2,1)}, bf16[8,2176]{1,0:T(8,128)(2,1)S(1)}, u32[]{:S(2)}, u32[]{:S(2)}) collective-permute-start(bf16[8,2176]{1,0:T(8,128)(2,1)} %shard_map.112), channel_id=1, source_target_pairs={{0,2},{2,4},{4,6},{6,0},{1,3},{3,5},{5,7},{7,1},{8,10},{10,12},{12... | collective-permute-start | bytes 104456 | tf_op jit(solution)/shard_map/ppermute | solution.py:181
  12.4 4.7 %collective-permute-start = (bf16[8,2176]{1,0:T(8,128)(2,1)}, bf16[8,2176]{1,0:T(8,128)(2,1)S(1)}, u32[]{:S(2)}, u32[]{:S(2)}) collective-permute-start(bf16[8,2176]{1,0:T(8,128)(2,1)} %shard_map.112), channel_id=1, source_target_pairs={{2,0},{4,2},{6,4},{0,6},{3,1},{5,3},{7,5},{1,7},{10,8},{12,10},{14... | collective-permute-start | bytes 104456 | tf_op jit(solution)/shard_map/ppermute | solution.py:182
  17.4 6.4 %collective-permute-start.2 = (bf16[8,2176]{1,0:T(8,128)(2,1)S(1)}, bf16[8,2176]{1,0:T(8,128)(2,1)S(1)}, u32[]{:S(2)}, u32[]{:S(2)}) collective-permute-start(bf16[8,2176]{1,0:T(8,128)(2,1)S(1)} %collective-permute-done.1), channel_id=1, source_target_pairs={{0,2},{2,4},{4,6},{6,0},{1,3},{3,5},{5,7},{7,1},{8,10},{10,12},{12... | collective-permute-start | bytes 104456 | tf_op jit(solution)/shard_map/ppermute | solution.py:183
  23.8 3.3 %collective-permute-done.2 = bf16[8,2176]{1,0:T(8,128)(2,1)S(1)} collective-permute-done((bf16[8,2176]{1,0:T(8,128)(2,1)S(1)}, bf16[8,2176]{1,0:T(8,128)(2,1)S(1)}, u32[]{:S(2)}, u32[]{:S(2)}) %collective-permute-start.2) | collective-permute-done | bytes 34848 | tf_op jit(solution)/shard_map/ppermute | solution.py:183
  29.0 33.7 %all_to_all.20 = bf16[16,4,8,2048]{3,2,1,0:T(8,128)(2,1)} all-to-all(bf16[16,4,8,2048]{3,2,1,0:T(8,128)(2,1)S(1)} %broadcast_in_dim.22), channel_id=1, replica_groups=mesh['x'=4,'y'=4,'zl'=4,'zh'=4,'core'=2] {'x','y'}, dimensions={0} | all-to-all | bytes 4194304 | tf_op jit(solution)/shard_map/all_to_all | solution.py:201
  62.7 1.9 collective-permute-start.4
  64.6 2.8 %collective-permute-start.5 = (bf16[2,192,1024]{2,1,0:T(8,128)(2,1)S(1)}, bf16[2,192,1024]{2,1,0:T(8,128)(2,1)S(1)}, u32[]{:S(2)}, u32[]{:S(2)}) collective-permute-start(bf16[2,192,1024]{2,1,0:T(8,128)(2,1)S(1)} %copy-done.3), channel_id=1, source_target_pairs={{0,8},{8,16},{16,24},{24,32},{32,40},{40,48},{48,56},{56,64},{64,7... | collective-permute-start | bytes 2359304 | tf_op jit(solution)/shard_map/ppermute | solution.py:267
  67.4 3.1 %collective-permute-start.6 = (bf16[2,192,1024]{2,1,0:T(8,128)(2,1)S(1)}, bf16[2,192,1024]{2,1,0:T(8,128)(2,1)S(1)}, u32[]{:S(2)}, u32[]{:S(2)}) collective-permute-start(bf16[2,192,1024]{2,1,0:T(8,128)(2,1)S(1)} %copy-done.3), channel_id=1, source_target_pairs={{8,0},{16,8},{24,16},{32,24},{40,32},{48,40},{56,48},{64,56},{72,6... | collective-permute-start | bytes 2359304 | tf_op jit(solution)/shard_map/ppermute | solution.py:268
  71.8 1.9 collective-permute-start.3
  74.9 11.6 %collective-permute-done.5 = bf16[2,192,1024]{2,1,0:T(8,128)(2,1)S(1)} collective-permute-done((bf16[2,192,1024]{2,1,0:T(8,128)(2,1)S(1)}, bf16[2,192,1024]{2,1,0:T(8,128)(2,1)S(1)}, u32[]{:S(2)}, u32[]{:S(2)}) %collective-permute-start.5) | collective-permute-done | bytes 786464 | tf_op jit(solution)/shard_map/ppermute | solution.py:267
  86.5 18.2 %collective-permute-done.6 = bf16[2,192,1024]{2,1,0:T(8,128)(2,1)S(1)} collective-permute-done((bf16[2,192,1024]{2,1,0:T(8,128)(2,1)S(1)}, bf16[2,192,1024]{2,1,0:T(8,128)(2,1)S(1)}, u32[]{:S(2)}, u32[]{:S(2)}) %collective-permute-start.6) | collective-permute-done | bytes 786464 | tf_op jit(solution)/shard_map/ppermute | solution.py:268
  105.2 2.5 %broadcast_select_fusion.1 = (bf16[16,4,8,2048]{3,2,1,0:T(8,128)(2,1)S(1)}, bf16[16,4,8,2048]{3,2,1,0:T(8,128)(2,1)S(1)}) fusion(bf16[16,4,8,2048]{3,2,1,0:T(8,128)(2,1)} %all_to_all.20, bf16[16,4,8,2048]{3,2,1,0:T(8,128)(2,1)} %collective-permute-done.4, pred[]{:T(512)S(6)} %eq.21), kind=kLoop, calls=%fused_computation.17 | loop fusion | flops 2097152 | bytes 8388609 | tf_op jit(solution)/shard_map/jit(_where)/select_n | solution.py:195
  110.0 2.9 %fusion.8.k_ref.v_ref = bf16[2,576,1024]{2,1,0:T(8,128)(2,1)S(1)} fusion(bf16[1024,1536]{1,0:T(8,128)(2,1)S(1)} %bitcast.119, f32[1024]{0:T(1024)S(1)} %bitcast.137, f32[2,576]{1,0:T(2,128)S(1)} %add_rsqrt_fusion, bf16[2,192,1024]{2,1,0:T(8,128)(2,1)S(1)} %collective-permute-done.6, bf16[2,192,1024]{2,1,0:T(8,128)(2,1)S(1)} %copy-done.3, ...), kind=kOutput, calls=%fused_computation.18 | convolution fusion | flops 2427715584 | bytes 6824960 | tf_op jit(solution)/shard_map/sti,iy->sty/dot_general | solution.py:283
  112.9 7.7 %shard_map.113 = (bf16[2,192,512]{2,1,0:T(8,128)(2,1)S(1)}, f32[2,4,2,384]{3,2,1,0:T(2,128)S(1)}) custom-call(f32[9,1,384]{2,1,0:T(1,128)S(1)} %tile.11.bias_ref, bf16[2,192,512]{2,1,0:T(8,128)(2,1)S(1)} %fusion.19.q_ref, bf16[2,576,1024]{2,1,0:T(8,128)(2,1)S(1)} %fusion.8.k_ref.v_ref, bf16[2,576,1024]{2,1,0:T(8,128)(2,1)S(1)} %fusion.8.k_ref.v_ref), custom_call_target="tpu_custom_call" | custom-call | flops 452984832 | bytes 1179648 | tf_op jit(solution)/shard_map/pallas_call | solution.py:107
  121.5 1.9 collective-permute-start.7
  124.7 1.3 collective-permute-done.7
  126.4 9.9 %shard_map.114 = (bf16[2,192,512]{2,1,0:T(8,128)(2,1)S(1)}, bf16[2,2,192,512]{3,2,1,0:T(8,128)(2,1)S(1)}, f32[2,2,192,512]{3,2,1,0:T(8,128)S(1)}, bf16[2,2,192,512]{3,2,1,0:T(8,128)(2,1)}) custom-call(f32[9,1,384]{2,1,0:T(1,128)S(1)} %tile.11.bias_ref, bf16[2,192,512]{2,1,0:T(8,128)(2,1)S(1)} %fusion.19.q_ref, bf16[2,576,1024]{2,1,0:T(8,128)(2,1)S(1)} %fusion.8.k_ref.v_ref, ...), custom_call_target="tpu_custom_call" | custom-call | flops 1132462080 | bytes 2949120 | tf_op jit(solution)/shard_map/pallas_call | solution.py:123
  137.0 2.5 %collective-permute-start.8 = (bf16[2,2,192,512]{3,2,1,0:T(8,128)(2,1)}, bf16[2,2,192,512]{3,2,1,0:T(8,128)(2,1)}, u32[]{:S(2)}, u32[]{:S(2)}) collective-permute-start(bf16[2,2,192,512]{3,2,1,0:T(8,128)(2,1)} %get-tuple-element.20), channel_id=1, source_target_pairs={{0,8},{8,16},{16,24},{24,32},{32,40},{40,48},{48,56},{56,64},{64,7... | collective-permute-start | bytes 2359304 | tf_op jit(solution)/shard_map/ppermute | solution.py:305
  139.6 4.2 %collective-permute-start.9 = (bf16[2,2,192,512]{3,2,1,0:T(8,128)(2,1)S(1)}, bf16[2,2,192,512]{3,2,1,0:T(8,128)(2,1)}, u32[]{:S(2)}, u32[]{:S(2)}) collective-permute-start(bf16[2,2,192,512]{3,2,1,0:T(8,128)(2,1)S(1)} %get-tuple-element.21), channel_id=1, source_target_pairs={{8,0},{16,8},{24,16},{32,24},{40,32},{48,40},{56,48},{64,56},{72,6... | collective-permute-start | bytes 2359304 | tf_op jit(solution)/shard_map/ppermute | solution.py:306
  144.8 4.2 %all-to-all-start.1 = ((bf16[16,4,16,256]{3,2,1,0:T(8,128)(2,1)}), bf16[16,4,16,256]{3,2,1,0:T(8,128)(2,1)}, u32[]{:S(2)}, u32[]{:S(2)}) async-start(bf16[16,4,16,256]{3,2,1,0:T(8,128)(2,1)} %bitcast.121), calls=%async_computation.1 | async-start | bytes 1048576 | tf_op jit(solution)/shard_map/all_to_all | solution.py:248
  149.0 2.6 %convolution_convert_fusion = bf16[2,192,1024]{2,1,0:T(8,128)(2,1)} fusion(bf16[2,192,512]{2,1,0:T(8,128)(2,1)S(1)} %get-tuple-element.17, bf16[512,256]{1,0:T(8,128)(2,1)} %bitcast.128, bf16[512,256]{1,0:T(8,128)(2,1)} %bitcast.130, bf16[512,256]{1,0:T(8,128)(2,1)} %bitcast.126, bf16[512,256]{1,0:T(8,128)(2,1)} %bitcast.124), kind=kOutput, calls=%fused_computation.28 | convolution fusion | flops 407240704 | bytes 2228224 | tf_op jit(solution)/shard_map/sty,yb->stb/dot_general | solution.py:308
  151.7 8.9 %all-to-all-done.1 = bf16[16,4,16,256]{3,2,1,0:T(8,128)(2,1)} async-done(((bf16[16,4,16,256]{3,2,1,0:T(8,128)(2,1)}), bf16[16,4,16,256]{3,2,1,0:T(8,128)(2,1)}, u32[]{:S(2)}, u32[]{:S(2)}) %all-to-all-start.1) | async-done | bytes 524320 | tf_op jit(solution)/shard_map/all_to_all | solution.py:248
  160.6 1.1 convert_reduce_fusion
  162.4 24.2 %all-to-all-start.2 = ((f32[16,16,256]{2,1,0:T(8,128)}), f32[16,16,256]{2,1,0:T(8,128)}, u32[]{:S(2)}, u32[]{:S(2)}) async-start(f32[16,16,256]{2,1,0:T(8,128)} %bitcast.49), calls=%async_computation.2 | async-start | bytes 524288 | tf_op jit(solution)/shard_map/all_to_all | solution.py:251
  186.7 1.9 add_convert_fusion
  189.3 2.7 %fusion.17 = (f32[2,192]{1,0:T(2,128)S(1)}, f32[2,192,1024]{2,1,0:T(8,128)}) fusion(bf16[2,192,1024]{2,1,0:T(8,128)(2,1)S(1)} %copy-done.4, f32[1024]{0:T(1024)S(1)} %bitcast.138, bf16[1024,1536,1]{1,0,2:T(8,128)(2,1)S(1)} %bitcast.120, bf16[2,192,512]{2,1,0:T(8,128)(2,1)S(1)} %get-tuple-element.32, bf16[2,192,512]{2,1,0:T(8,128)(2,1)S(1)} %get-tuple-element.31, ...), kind=kOutput, calls=%fused_computation.25 | convolution fusion | flops 1213070976 | bytes 6690304 | tf_op jit(solution)/shard_map/sty,iy->sti/dot_general | solution.py:313
  192.0 14.4 %all-to-all-done.2 = f32[16,16,256]{2,1,0:T(8,128)} async-done(((f32[16,16,256]{2,1,0:T(8,128)}), f32[16,16,256]{2,1,0:T(8,128)}, u32[]{:S(2)}, u32[]{:S(2)}) %all-to-all-start.2) | async-done | bytes 262176 | tf_op jit(solution)/shard_map/all_to_all | solution.py:251
  206.4 1.0 reduce_sum.49
  208.1 6.9 %all-to-all-start.3 = ((f32[16,16,256]{2,1,0:T(8,128)}), f32[16,16,256]{2,1,0:T(8,128)S(1)}, u32[]{:S(2)}, u32[]{:S(2)}) async-start(f32[16,16,256]{2,1,0:T(8,128)} %broadcast_in_dim.24), calls=%async_computation.3 | async-start | bytes 524288 | tf_op jit(solution)/shard_map/all_to_all | solution.py:201
  215.0 2.6 %fusion.16 = bf16[2,192,1024]{2,1,0:T(8,128)(2,1)} fusion(bf16[2,192,1024]{2,1,0:T(8,128)(2,1)S(1)} %copy-done.5, f32[2,192,1024]{2,1,0:T(8,128)} %get-tuple-element.50, f32[2,192]{1,0:T(2,128)S(1)} %broadcast_multiply_fusion.1, f32[2,192]{1,0:T(2,128)S(1)} %copy-done.12, f32[2,192]{1,0:T(2,128)S(1)} %copy-done.14), kind=kLoop, calls=%fused_computation.24 | loop fusion | flops 2359296 | bytes 3150336 | tf_op jit(solution)/shard_map/convert_element_type | solution.py:318
  217.6 5.8 %all-to-all-done.3 = f32[16,16,256]{2,1,0:T(8,128)S(1)} async-done(((f32[16,16,256]{2,1,0:T(8,128)}), f32[16,16,256]{2,1,0:T(8,128)S(1)}, u32[]{:S(2)}, u32[]{:S(2)}) %all-to-all-start.3) | async-done | bytes 262176 | tf_op jit(solution)/shard_map/all_to_all | solution.py:201
  (95 shorter events, 15.1 us)
Async XLA Ops:
  0.6 120.0 %copy-start = (bf16[2,192,1024]{2,1,0:T(8,128)(2,1)S(1)}, bf16[2,192,1024]{2,1,0:T(8,128)(2,1)}, u32[]{:S(2)}) copy-start(bf16[2,192,1024]{2,1,0:T(8,128)(2,1)} %param.17) | copy-start | bytes 2359300
  3.3 14.1 %collective-permute-start.1 = (bf16[8,2176]{1,0:T(8,128)(2,1)}, bf16[8,2176]{1,0:T(8,128)(2,1)S(1)}, u32[]{:S(2)}, u32[]{:S(2)}) collective-permute-start(bf16[8,2176]{1,0:T(8,128)(2,1)} %shard_map.112), channel_id=1, source_target_pairs={{0,2},{2,4},{4,6},{6,0},{1,3},{3,5},{5,7},{7,1},{8,10},{10,12},{12... | collective-permute-start | bytes 104456 | tf_op jit(solution)/shard_map/ppermute | solution.py:181
  12.4 11.4 %collective-permute-start = (bf16[8,2176]{1,0:T(8,128)(2,1)}, bf16[8,2176]{1,0:T(8,128)(2,1)S(1)}, u32[]{:S(2)}, u32[]{:S(2)}) collective-permute-start(bf16[8,2176]{1,0:T(8,128)(2,1)} %shard_map.112), channel_id=1, source_target_pairs={{2,0},{4,2},{6,4},{0,6},{3,1},{5,3},{7,5},{1,7},{10,8},{12,10},{14... | collective-permute-start | bytes 104456 | tf_op jit(solution)/shard_map/ppermute | solution.py:182
  17.4 9.7 %collective-permute-start.2 = (bf16[8,2176]{1,0:T(8,128)(2,1)S(1)}, bf16[8,2176]{1,0:T(8,128)(2,1)S(1)}, u32[]{:S(2)}, u32[]{:S(2)}) collective-permute-start(bf16[8,2176]{1,0:T(8,128)(2,1)S(1)} %collective-permute-done.1), channel_id=1, source_target_pairs={{0,2},{2,4},{4,6},{6,0},{1,3},{3,5},{5,7},{7,1},{8,10},{10,12},{12... | collective-permute-start | bytes 104456 | tf_op jit(solution)/shard_map/ppermute | solution.py:183
  29.0 35.6 %copy-start.3 = (bf16[2,192,1024]{2,1,0:T(8,128)(2,1)S(1)}, bf16[2,192,1024]{2,1,0:T(8,128)(2,1)}, u32[]{:S(2)}) copy-start(bf16[2,192,1024]{2,1,0:T(8,128)(2,1)} %param.9) | copy-start | bytes 2359300
  29.0 41.6 %copy-start.17 = (s32[3,9]{1,0:T(4,128)S(1)}, s32[3,9]{1,0:T(4,128)}, u32[]{:S(2)}) copy-start(s32[3,9]{1,0:T(4,128)} %param.16) | copy-start | bytes 328
  29.0 41.7 %copy-start.18 = (s32[3,9]{1,0:T(4,128)S(1)}, s32[3,9]{1,0:T(4,128)}, u32[]{:S(2)}) copy-start(s32[3,9]{1,0:T(4,128)} %param.15) | copy-start | bytes 328
  62.7 42.5 %collective-permute-start.4 = (bf16[16,4,8,2048]{3,2,1,0:T(8,128)(2,1)}, bf16[16,4,8,2048]{3,2,1,0:T(8,128)(2,1)}, u32[]{:S(2)}, u32[]{:S(2)}) collective-permute-start(bf16[16,4,8,2048]{3,2,1,0:T(8,128)(2,1)} %all_to_all.20), channel_id=1, source_target_pairs={{0,1},{1,0},{2,3},{3,2},{4,5},{5,4},{6,7},{7,6},{8,9},{9,8},{10,11... | collective-permute-start | bytes 6291464 | tf_op jit(solution)/shard_map/ppermute | solution.py:189
  64.6 21.8 %collective-permute-start.5 = (bf16[2,192,1024]{2,1,0:T(8,128)(2,1)S(1)}, bf16[2,192,1024]{2,1,0:T(8,128)(2,1)S(1)}, u32[]{:S(2)}, u32[]{:S(2)}) collective-permute-start(bf16[2,192,1024]{2,1,0:T(8,128)(2,1)S(1)} %copy-done.3), channel_id=1, source_target_pairs={{0,8},{8,16},{16,24},{24,32},{32,40},{40,48},{48,56},{56,64},{64,7... | collective-permute-start | bytes 2359304 | tf_op jit(solution)/shard_map/ppermute | solution.py:267
  67.4 37.2 %collective-permute-start.6 = (bf16[2,192,1024]{2,1,0:T(8,128)(2,1)S(1)}, bf16[2,192,1024]{2,1,0:T(8,128)(2,1)S(1)}, u32[]{:S(2)}, u32[]{:S(2)}) collective-permute-start(bf16[2,192,1024]{2,1,0:T(8,128)(2,1)S(1)} %copy-done.3), channel_id=1, source_target_pairs={{8,0},{16,8},{24,16},{32,24},{40,32},{48,40},{56,48},{64,56},{72,6... | collective-permute-start | bytes 2359304 | tf_op jit(solution)/shard_map/ppermute | solution.py:268
  71.6 36.8 %copy-start.13 = (f32[2,192]{1,0:T(2,128)}, f32[2,192]{1,0:T(2,128)S(1)}, u32[]{:S(2)}) copy-start(f32[2,192]{1,0:T(2,128)S(1)} %get-tuple-element.48) | copy-start | bytes 4612
  71.8 3.1 %collective-permute-start.3 = (bf16[4,8,128]{2,1,0:T(8,128)(2,1)S(1)}, bf16[4,8,128]{2,1,0:T(8,128)(2,1)S(1)}, u32[]{:S(2)}, u32[]{:S(2)}) collective-permute-start(bf16[4,8,128]{2,1,0:T(8,128)(2,1)S(1)} %constant_dynamic-slice_fusion), channel_id=1, source_target_pairs={{0,1},{1,0},{2,3},{3,2},{4,5},{5,4},{6,7},{7,6},{8,9},{9,8},{10,11... | collective-permute-start | bytes 24584 | tf_op jit(solution)/shard_map/ppermute | solution.py:189
  74.9 34.2 %copy-start.15 = (f32[4,2,128]{2,1,0:T(2,128)}, f32[4,2,128]{2,1,0:T(2,128)S(1)}, u32[]{:S(2)}) copy-start(f32[4,2,128]{2,1,0:T(2,128)S(1)} %copy.41) | copy-start | bytes 12292
  108.4 1.6 copy-start.6
  121.5 4.6 %collective-permute-start.7 = (f32[4,64,1024]{2,1,0:T(8,128)S(1)}, f32[4,64,1024]{2,1,0:T(8,128)S(1)}, u32[]{:S(2)}, u32[]{:S(2)}) collective-permute-start(f32[4,64,1024]{2,1,0:T(8,128)S(1)} %select_bitcast_fusion), channel_id=1, source_target_pairs={{0,1},{1,0},{2,3},{3,2},{4,5},{5,4},{6,7},{7,6},{8,9},{9,8},{10,11... | collective-permute-start | bytes 3145736 | tf_op jit(solution)/shard_map/ppermute | solution.py:189
  123.8 0.7 copy-start.9
  123.8 0.8 copy-start.10
  123.8 0.9 copy-start.11
  123.8 2.6 %copy-start.8 = (bf16[1,4,2,4,2,8,256]{6,5,4,3,2,1,0:T(8,128)(2,1)}, bf16[1,4,2,4,2,8,256]{6,5,4,3,2,1,0:T(8,128)(2,1)S(1)}, u32[]{:S(2)}) copy-start(bf16[1,4,2,4,2,8,256]{6,5,4,3,2,1,0:T(8,128)(2,1)S(1)} %get-tuple-element.27) | copy-start | bytes 786436
  136.3 0.8 copy-start.1
  137.0 49.6 %collective-permute-start.8 = (bf16[2,2,192,512]{3,2,1,0:T(8,128)(2,1)}, bf16[2,2,192,512]{3,2,1,0:T(8,128)(2,1)}, u32[]{:S(2)}, u32[]{:S(2)}) collective-permute-start(bf16[2,2,192,512]{3,2,1,0:T(8,128)(2,1)} %get-tuple-element.20), channel_id=1, source_target_pairs={{0,8},{8,16},{16,24},{24,32},{32,40},{40,48},{48,56},{56,64},{64,7... | collective-permute-start | bytes 2359304 | tf_op jit(solution)/shard_map/ppermute | solution.py:305
  139.6 47.1 %collective-permute-start.9 = (bf16[2,2,192,512]{3,2,1,0:T(8,128)(2,1)S(1)}, bf16[2,2,192,512]{3,2,1,0:T(8,128)(2,1)}, u32[]{:S(2)}, u32[]{:S(2)}) collective-permute-start(bf16[2,2,192,512]{3,2,1,0:T(8,128)(2,1)S(1)} %get-tuple-element.21), channel_id=1, source_target_pairs={{8,0},{16,8},{24,16},{32,24},{40,32},{48,40},{56,48},{64,56},{72,6... | collective-permute-start | bytes 2359304 | tf_op jit(solution)/shard_map/ppermute | solution.py:306
  144.8 15.8 %all-to-all-start.1 = ((bf16[16,4,16,256]{3,2,1,0:T(8,128)(2,1)}), bf16[16,4,16,256]{3,2,1,0:T(8,128)(2,1)}, u32[]{:S(2)}, u32[]{:S(2)}) async-start(bf16[16,4,16,256]{3,2,1,0:T(8,128)(2,1)} %bitcast.121), calls=%async_computation.1 | async-start | bytes 1048576 | tf_op jit(solution)/shard_map/all_to_all | solution.py:248
  162.4 43.9 %all-to-all-start.2 = ((f32[16,16,256]{2,1,0:T(8,128)}), f32[16,16,256]{2,1,0:T(8,128)}, u32[]{:S(2)}, u32[]{:S(2)}) async-start(f32[16,16,256]{2,1,0:T(8,128)} %bitcast.49), calls=%async_computation.2 | async-start | bytes 524288 | tf_op jit(solution)/shard_map/all_to_all | solution.py:251
  186.6 2.0 copy-start.2
  186.6 2.0 copy-start.4
  186.6 2.7 %copy-start.7 = (bf16[4,2,16,8,1536]{4,3,2,1,0:T(8,128)(2,1)S(1)}, bf16[4,2,16,8,1536]{4,3,2,1,0:T(8,128)(2,1)}, u32[]{:S(2)}) copy-start(bf16[4,2,16,8,1536]{4,3,2,1,0:T(8,128)(2,1)} %copy-done.6) | copy-start | bytes 9437188
  186.6 2.7 %copy-start.16 = (f32[4,2,128]{2,1,0:T(2,128)S(1)}, f32[4,2,128]{2,1,0:T(2,128)}, u32[]{:S(2)}) copy-start(f32[4,2,128]{2,1,0:T(2,128)} %copy-done.15) | copy-start | bytes 12292
  189.3 25.6 %copy-start.5 = (bf16[2,192,1024]{2,1,0:T(8,128)(2,1)S(1)}, bf16[2,192,1024]{2,1,0:T(8,128)(2,1)}, u32[]{:S(2)}) copy-start(bf16[2,192,1024]{2,1,0:T(8,128)(2,1)} %param.9) | copy-start | bytes 2359300
  189.3 25.6 %copy-start.12 = (f32[2,192]{1,0:T(2,128)S(1)}, f32[2,192]{1,0:T(2,128)}, u32[]{:S(2)}) copy-start(f32[2,192]{1,0:T(2,128)} %get-tuple-element.47) | copy-start | bytes 4612
  189.3 25.7 %copy-start.14 = (f32[2,192]{1,0:T(2,128)S(1)}, f32[2,192]{1,0:T(2,128)}, u32[]{:S(2)}) copy-start(f32[2,192]{1,0:T(2,128)} %copy-done.13) | copy-start | bytes 4612
  208.1 15.4 %all-to-all-start.3 = ((f32[16,16,256]{2,1,0:T(8,128)}), f32[16,16,256]{2,1,0:T(8,128)S(1)}, u32[]{:S(2)}, u32[]{:S(2)}) async-start(f32[16,16,256]{2,1,0:T(8,128)} %broadcast_in_dim.24), calls=%async_computation.3 | async-start | bytes 524288 | tf_op jit(solution)/shard_map/all_to_all | solution.py:201

commit v3 on v2

--- a/solution.py
+++ b/solution.py
@@ -9,6 +9,7 @@
 
 HEAD_DIM = 64
 PAIR = 2 * HEAD_DIM
+SCALE = HEAD_DIM**-0.5
 EPSILON = 1e-06
 MASKED = -1e30
 X, Y, ZL, ZH, CORE = "x", "y", "zl", "zh", "core"
@@ -27,8 +28,9 @@
     return lax.broadcasted_iota(jnp.int32, (1, PAIR), 1) < HEAD_DIM
 
 
-def stacked(both):
+def stacked(both, scale=1.0):
     near = head_lanes()
+    both = both * jnp.asarray(scale, both.dtype)
     zero = jnp.zeros_like(both)
     return jnp.concatenate([jnp.where(near, both, zero), jnp.where(near, zero, both)], axis=0)
 
@@ -39,15 +41,15 @@
     return jnp.where(head_lanes(), both[:rows], both[rows:])
 
 
-def masked_scores(bias_ref, key, query):
-    blocks = bias_ref.shape[0]
+def masked_scores(bias, key, query):
+    blocks = bias.shape[0]
     span, columns = (key.shape[0], query.shape[0])
     scores = contract(key, query, 1, 1).reshape(blocks, span // blocks, columns)
-    return (scores + bias_ref[...]).reshape(span, columns)
+    return (scores + bias).reshape(span, columns)
 
 
 def forward_kernel(bias_ref, q_ref, k_ref, v_ref, att_ref, stat_ref):
-    scores = masked_scores(bias_ref, k_ref[0], stacked(q_ref[0]))
+    scores = masked_scores(bias_ref[...], k_ref[0], stacked(q_ref[0], SCALE))
     row_max = jnp.max(scores, axis=0, keepdims=True)
     shifted = jnp.exp(scores - row_max)
     inverse = 1.0 / jnp.sum(shifted, axis=0, keepdims=True)
@@ -57,83 +59,126 @@
     stat_ref[0, 0, 1:2, :] = inverse
 
 
-def backward_kernel(
-    bias_ref, q_ref, k_ref, v_ref, g_ref, stat_ref, dq_ref, low_ref, own_ref, high_ref
-):
-    query, key, value, grad = (stacked(q_ref[0]), k_ref[0], v_ref[0], stacked(g_ref[0]))
-    span = key.shape[0]
-    scores = masked_scores(bias_ref, key, query)
-    prob = jnp.exp(scores - stat_ref[0, 0, 0:1, :]) * stat_ref[0, 0, 1:2, :]
-    prob_bf = prob.astype(BF16)
+def query_kernel(bias_ref, q_ref, k_ref, v_ref, g_ref, stat_ref, dq_ref, own_ref, all_ref):
+    rows = q_ref.shape[1]
+    query, key, value, grad = (stacked(q_ref[0], SCALE), k_ref[0], v_ref[0], stacked(g_ref[0]))
+    row_max, inverse = (stat_ref[0, 0, 0:1, :], stat_ref[0, 0, 1:2, :])
+    prob = jnp.exp(masked_scores(bias_ref[...], key, query) - row_max) * inverse
     d_prob = contract(value, grad, 1, 1)
     delta = jnp.sum(prob * d_prob, axis=0, keepdims=True)
     d_score = (prob * (d_prob - delta)).astype(BF16)
-    dq_ref[0] = (merged(contract(key, d_score, 0, 0)) * HEAD_DIM**-0.5).astype(BF16)
-    third = span // 3
-    for part, total in enumerate((contract(d_score, query, 1, 0), contract(prob_bf, grad, 1, 0))):
-        low_ref[part, 0] = total[:third].astype(BF16)
-        own_ref[part, 0] = total[third : 2 * third]
-        high_ref[part, 0] = total[2 * third :].astype(BF16)
-
-
-def attention_specs(bias, query, key_value):
-    samples, rows, width = query.shape
-    span = key_value.shape[1]
-    pairs = width // PAIR
-    narrow = pl.BlockSpec((1, rows, PAIR), lambda s, h: (s, 0, h))
-    given = [
-        pl.BlockSpec(bias.shape, lambda s, h: (0, 0, 0)),
-        narrow,
-        pl.BlockSpec((1, span, PAIR), lambda s, h: (s, 0, h)),
-        pl.BlockSpec((1, span, PAIR), lambda s, h: (s, 0, h + pairs)),
-    ]
-    stat = pl.BlockSpec((1, 1, 2, 2 * rows), lambda s, h: (s, h, 0, 0))
-    stat_shape = jax.ShapeDtypeStruct((samples, pairs, 2, 2 * rows), F32)
-    return (samples, pairs), given, narrow, stat, stat_shape
-
-
-def attention_cost(query, key_value, products):
-    samples, rows, width = query.shape
-    span = key_value.shape[1]
-    return pl.CostEstimate(
-        flops=2 * products * samples * rows * span * width,
-        transcendentals=samples * rows * span * width // HEAD_DIM,
-        bytes_accessed=3 * products * samples * rows * width,
-    )
-
-
-def forward_attention(bias, query, key_value):
-    grid, given, narrow, stat, stat_shape = attention_specs(bias, query, key_value)
-    return pl.pallas_call(
-        forward_kernel,
-        grid=grid,
-        in_specs=given,
-        out_specs=[narrow, stat],
-        out_shape=[jax.ShapeDtypeStruct(query.shape, BF16), stat_shape],
-        cost_estimate=attention_cost(query, key_value, 2),
-        compiler_params=pltpu.CompilerParams(vmem_limit_bytes=40 * 2**20),
-    )(bias, query, key_value, key_value)
-
-
-def backward_attention(bias, query, key_value, grad, stats):
-    grid, given, narrow, stat, _ = attention_specs(bias, query, key_value)
-    samples, rows, width = query.shape
-    shape = jax.ShapeDtypeStruct
-    split = pl.BlockSpec((2, 1, rows, PAIR), lambda s, h: (0, s, 0, h))
-    return pl.pallas_call(
-        backward_kernel,
-        grid=grid,
-        in_specs=given + [narrow, stat],
-        out_specs=[narrow, split, split, split],
-        out_shape=[
-            shape((samples, rows, width), BF16),
-            shape((2, samples, rows, width), BF16),
-            shape((2, samples, rows, width), F32),
-            shape((2, samples, rows, width), BF16),
-        ],
-        cost_estimate=attention_cost(query, key_value, 5),
-        compiler_params=pltpu.CompilerParams(vmem_limit_bytes=40 * 2**20),
-    )(bias, query, key_value, key_value, grad, stats)
+    dq_ref[0] = (merged(contract(key, d_score, 0, 0)) * SCALE).astype(BF16)
+    own_ref[0, 0] = contract(d_score[rows : 2 * rows], query, 1, 0)
+    own_ref[1, 0] = contract(prob[rows : 2 * rows].astype(BF16), grad, 1, 0)
+    all_ref[0, 0, 0:1, :] = row_max
+    all_ref[0, 0, 1:2, :] = inverse
+    all_ref[0, 0, 2:3, :] = delta
+
+
+def key_kernel(
+    low_bias_ref,
+    high_bias_ref,
+    low_q_ref,
+    high_q_ref,
+    k_ref,
+    v_ref,
+    low_g_ref,
+    high_g_ref,
+    low_stat_ref,
+    high_stat_ref,
+    own_ref,
+    dk_ref,
+    dv_ref,
+):
+    key, value = (k_ref[0], v_ref[0])
+    d_key, d_value = (own_ref[0, 0], own_ref[1, 0])
+    sides = (
+        (low_bias_ref, low_q_ref, low_g_ref, low_stat_ref),
+        (high_bias_ref, high_q_ref, high_g_ref, high_stat_ref),
+    )
+    for bias_ref, q_ref, g_ref, stat_ref in sides:
+        query, grad = (stacked(q_ref[0], SCALE), stacked(g_ref[0]))
+        scores = masked_scores(bias_ref[...], key, query)
+        prob = jnp.exp(scores - stat_ref[0, 0, 0:1, :]) * stat_ref[0, 0, 1:2, :]
+        d_prob = contract(value, grad, 1, 1)
+        d_score = (prob * (d_prob - stat_ref[0, 0, 2:3, :])).astype(BF16)
+        d_key += contract(d_score, query, 1, 0)
+        d_value += contract(prob.astype(BF16), grad, 1, 0)
+    dk_ref[0] = d_key.astype(BF16)
+    dv_ref[0] = d_value.astype(BF16)
+
+
+class Plan:
+    def __init__(self, joint):
+        samples, span, width = joint.shape
+        self.rows, self.width, self.span = (span // 3, width // 3, span)
+        self.samples, self.pairs = (samples, width // 3 // PAIR)
+        self.grid = (samples, self.pairs)
+        self.narrow = pl.BlockSpec((1, self.rows, PAIR), lambda s, h: (s, 0, h))
+        self.split = pl.BlockSpec((2, 1, self.rows, PAIR), lambda s, h: (0, s, 0, h))
+
+    def joint(self, kind, third=None):
+        first = kind * self.pairs
+        if third is None:
+            return pl.BlockSpec((1, self.span, PAIR), lambda s, h: (s, 0, h + first))
+        return pl.BlockSpec((1, self.rows, PAIR), lambda s, h: (s, third, h + first))
+
+    def bias(self, bias):
+        return pl.BlockSpec(bias.shape, lambda s, h: (0, 0, 0))
+
+    def stat(self, count):
+        return pl.BlockSpec((1, 1, count, 2 * self.rows), lambda s, h: (s, h, 0, 0))
+
+    def stat_shape(self, count):
+        return jax.ShapeDtypeStruct((self.samples, self.pairs, count, 2 * self.rows), F32)
+
+    def narrow_shape(self):
+        return jax.ShapeDtypeStruct((self.samples, self.rows, self.width), BF16)
+
+    def call(self, kernel, products, in_specs, out_specs, out_shape):
+        work = self.samples * self.rows * self.span * self.width
+        return pl.pallas_call(
+            kernel,
+            grid=self.grid,
+            in_specs=in_specs,
+            out_specs=out_specs,
+            out_shape=out_shape,
+            cost_estimate=pl.CostEstimate(
+                flops=2 * products * work,
+                transcendentals=work // HEAD_DIM,
+                bytes_accessed=3 * products * self.samples * self.rows * self.width,
+            ),
+            compiler_params=pltpu.CompilerParams(vmem_limit_bytes=16 * 2**20),
+        )
+
+
+def forward_attention(bias, joint):
+    plan = Plan(joint)
+    given = [plan.bias(bias), plan.joint(0, 1), plan.joint(1), plan.joint(2)]
+    outs = ([plan.narrow, plan.stat(2)], [plan.narrow_shape(), plan.stat_shape(2)])
+    return plan.call(forward_kernel, 2, given, *outs)(bias, joint, joint, joint)
+
+
+def query_gradient(bias, joint, grad, stats):
+    plan = Plan(joint)
+    given = [plan.bias(bias), plan.joint(0, 1), plan.joint(1), plan.joint(2)]
+    given += [plan.narrow, plan.stat(2)]
+    own = jax.ShapeDtypeStruct((2, plan.samples, plan.rows, plan.width), F32)
+    outs = (
+        [plan.narrow, plan.split, plan.stat(3)],
+        [plan.narrow_shape(), own, plan.stat_shape(3)],
+    )
+    return plan.call(query_kernel, 4, given, *outs)(bias, joint, joint, joint, grad, stats)
+
+
+def key_gradient(biases, joint, grads, stats, own):
+    plan = Plan(joint)
+    given = [plan.bias(biases[0]), plan.bias(biases[1]), plan.joint(0, 0), plan.joint(0, 2)]
+    given += [plan.joint(1, 1), plan.joint(2, 1), plan.narrow, plan.narrow]
+    given += [plan.stat(3), plan.stat(3), plan.split]
+    outs = ([plan.narrow] * 2, [plan.narrow_shape()] * 2)
+    call = plan.call(key_kernel, 3, given, *outs)
+    return call(*biases, joint, joint, joint, joint, *grads, *stats, own)
 
 
 def slice_kernel(place_ref, q_ref, k_ref, v_ref, out_ref, gain_ref, part_ref):
@@ -267,22 +312,16 @@
     below = lax.ppermute(inputs, DOMAIN, up)
     above = lax.ppermute(inputs, DOMAIN, down)
     gain, w_joint, w_full_out = gathered_weights(norm_gain, w_query, w_key, w_value, w_out)
-    hidden_width = w_query.shape[1]
     gain_float = gain.astype(F32)
 
-    def normalized(rows):
+    def inverse_of(rows):
         rows = rows.astype(F32)
-        inverse = lax.rsqrt(jnp.mean(rows * rows, axis=-1, keepdims=True) + EPSILON)
-        return inverse, (rows * inverse * gain_float).astype(BF16)
-
-    inverse_rms, normed = normalized(inputs)
-    _, window = normalized(jnp.concatenate([below, inputs, above], axis=1))
-    query = jnp.einsum(
-        "sti,iy->sty", normed, w_joint[:, :hidden_width], preferred_element_type=F32
-    ).astype(BF16) * jnp.asarray(HEAD_DIM**-0.5, BF16)
-    key_value = jnp.einsum(
-        "sti,iy->sty", window, w_joint[:, hidden_width:], preferred_element_type=F32
-    ).astype(BF16)
+        return lax.rsqrt(jnp.mean(rows * rows, axis=-1, keepdims=True) + EPSILON)
+
+    inverse_rms = inverse_of(inputs)
+    window = jnp.concatenate([below, inputs, above], axis=1)
+    normed = (window.astype(F32) * inverse_of(window) * gain_float).astype(BF16)
+    joint = jnp.einsum("sti,iy->sty", normed, w_joint, preferred_element_type=F32).astype(BF16)
     d_attention = jnp.einsum(
         "stz,yz->sty", output_cotangent, w_full_out, preferred_element_type=F32
     ).astype(BF16)
@@ -296,20 +335,31 @@
     bias = jnp.where(jnp.any(matches, axis=1).T, 0.0, MASKED).astype(F32)
     bias = jnp.tile(jnp.repeat(bias, block_len, axis=1), (1, 2))[:, None, :]
 
-    attended, stats = forward_attention(bias, query, key_value)
+    attended, stats = forward_attention(bias, joint)
     half = halved_gradient(attended, output_cotangent)
     half, d_attention = lax.optimization_barrier((half, d_attention))
     members = lax.axis_size(MEMBER)
     grad_wout = summed_gradient(half, samples * members)
-    d_query, low, own, high = backward_attention(bias, query, key_value, d_attention, stats)
-    from_below = lax.ppermute(high, DOMAIN, up)
-    from_above = lax.ppermute(low, DOMAIN, down)
-    attended, own = lax.optimization_barrier((attended, own))
+    grads = (lax.ppermute(d_attention, DOMAIN, up), lax.ppermute(d_attention, DOMAIN, down))
+    d_query, own, stats = query_gradient(bias, joint, d_attention, stats)
+    shape, flat = (stats.shape, (-1, stats.shape[-1]))
+    stats, attended = lax.optimization_barrier((stats, attended))
+
+    def message(third):
+        rows = bias[third * block_count : (third + 1) * block_count]
+        return jnp.concatenate([stats.reshape(flat), rows.reshape(flat)], axis=0)
+
+    received = (
+        lax.ppermute(message(2), DOMAIN, up),
+        lax.ppermute(message(0), DOMAIN, down),
+    )
     attn_out = jnp.einsum(
         "sty,yb->stb", attended, w_full_out, preferred_element_type=F32
     ).astype(BF16)
-    d_key_value = (own + from_below.astype(F32) + from_above.astype(F32)).astype(BF16)
-    d_joint = jnp.concatenate([d_query, d_key_value[0], d_key_value[1]], axis=-1)
+    side_stats = [rows[:-block_count].reshape(shape) for rows in received]
+    side_bias = [rows[-block_count:][:, None, :] for rows in received]
+    d_key, d_value = key_gradient(side_bias, joint, grads, side_stats, own)
+    d_joint = jnp.concatenate([d_query, d_key, d_value], axis=-1)
     d_normed = jnp.einsum("sty,iy->sti", d_joint, w_joint, preferred_element_type=F32)
     inputs_float = inputs.astype(F32)
     scaled = d_normed * gain_float

time: 225 us -> 232 us (1.031)
  waiting for transfers between devices: 64.6 us -> 47.3 us
  local copies, waits for them, and re-layouts: 7.26 us -> 19.8 us
  Pallas kernels: 19.6 us -> 25.1 us
  matrix products: 10.1 us -> 13.3 us
  starting transfers between devices: 73.8 us -> 76.9 us
    all_to_all x1, waiting for transfers between devices: 14.4 us -> 4.15 us  [summed_gradient(): part = lax.all_to_all(part, COLUMN, 0, 0, tiled=True)]
    all_to_all x1, waiting for transfers between devices: 8.92 us -> 0.01 us  [summed_gradient(): half = lax.all_to_all(half, (Y, X), 0, 0, tiled=True)]
    all_to_all x1, starting transfers between devices: 24.2 us -> 17.8 us  [summed_gradient(): part = lax.all_to_all(part, COLUMN, 0, 0, tiled=True)]
    unnamed x45 -> x51, local copies, waits for them, and re-layouts: 3.61 us -> 9.34 us
    pallas_call x2 -> x3, Pallas kernels: 17.6 us -> 23.1 us  [the longest x1 8.06 us: query_gradient(): plan.call(query_kernel, 4, given, *outs)]
    ppermute x2 -> x4, starting transfers between devices: 6.72 us -> 11.7 us  [the longest x1 3.6 us: shards(): lax.ppermute(d_attention, DOMAIN, up)]
    all_to_all x1, starting transfers between devices: 6.88 us -> 10.4 us  [plane_gather(): return lax.all_to_all(copies, PLANE, 0, 0, tiled=True)]
    dot_general x2 -> x1, matrix products: 3.49 us -> 6.64 us  [shards(): jnp.einsum('sti,iy->sty', normed, w_joint, preferred_element_type=F32)]
  transfers between devices with their start and end apart: 13 -> 15, of which waited for: 9 -> 9; matrix products, arithmetic and copies ran while one was open for 7% -> 9% of each run, Pallas kernels for 0% -> 7%
where the time goes in v3:
time: 232 us; the launch traced here: 231 us
  starting transfers between devices  76.9 us (33%)
  waiting for transfers between devices  47.3 us (20%)
  blocking collectives  33.6 us (14%)
  Pallas kernels  25.1 us (11%)
  local copies, waits for them, and re-layouts  19.8 us (9%)
  other arithmetic  13.4 us (6%)
  matrix products  13.3 us (6%)
    all_to_all x1, blocking collectives, plane_gather(): return lax.all_to_all(copies, PLANE, 0, 0, tiled=True)  33.6 us
    ppermute x1, waiting for transfers between devices, shards(): above = lax.ppermute(inputs, DOMAIN, down)  18.2 us
    all_to_all x1, starting transfers between devices, summed_gradient(): part = lax.all_to_all(part, COLUMN, 0, 0, tiled=True)  17.8 us
    ppermute x1, waiting for transfers between devices, shards(): below = lax.ppermute(inputs, DOMAIN, up)  11.9 us
    all_to_all x1, starting transfers between devices, plane_gather(): return lax.all_to_all(copies, PLANE, 0, 0, tiled=True)  10.4 us
    unnamed x51, local copies, waits for them, and re-layouts  9.34 us
    ppermute x1, starting transfers between devices, column_gather(): first = lax.ppermute(part, ZH, up)  9.08 us
    pallas_call x1, Pallas kernels, query_gradient(): plan.call(query_kernel, 4, given, *outs)  8.06 us
  transfers between devices with their start and end apart: 15, of which 9 were waited for; matrix products, arithmetic and copies ran while one was open for 9% of the time, Pallas kernels for 7%

profile of v3, /device:TPU:32, one launch (start us, length us, event | category | flops | bytes accessed | tf_op | source)
XLA Modules:
  0.0 230.6 jit_solution(5389095145071610795)
XLA Ops:
  1.3 2.0 shard_map.112
  3.3 9.1 %collective-permute-start.3 = (bf16[8,2176]{1,0:T(8,128)(2,1)}, bf16[8,2176]{1,0:T(8,128)(2,1)S(1)}, u32[]{:S(2)}, u32[]{:S(2)}) collective-permute-start(bf16[8,2176]{1,0:T(8,128)(2,1)} %shard_map.112), channel_id=1, source_target_pairs={{0,2},{2,4},{4,6},{6,0},{1,3},{3,5},{5,7},{7,1},{8,10},{10,12},{12... | collective-permute-start | bytes 104456 | tf_op jit(solution)/shard_map/ppermute | solution.py:226
  12.4 4.7 %collective-permute-start.2 = (bf16[8,2176]{1,0:T(8,128)(2,1)}, bf16[8,2176]{1,0:T(8,128)(2,1)S(1)}, u32[]{:S(2)}, u32[]{:S(2)}) collective-permute-start(bf16[8,2176]{1,0:T(8,128)(2,1)} %shard_map.112), channel_id=1, source_target_pairs={{2,0},{4,2},{6,4},{0,6},{3,1},{5,3},{7,5},{1,7},{10,8},{12,10},{14... | collective-permute-start | bytes 104456 | tf_op jit(solution)/shard_map/ppermute | solution.py:227
  17.4 6.4 %collective-permute-start.4 = (bf16[8,2176]{1,0:T(8,128)(2,1)S(1)}, bf16[8,2176]{1,0:T(8,128)(2,1)S(1)}, u32[]{:S(2)}, u32[]{:S(2)}) collective-permute-start(bf16[8,2176]{1,0:T(8,128)(2,1)S(1)} %collective-permute-done.3), channel_id=1, source_target_pairs={{0,2},{2,4},{4,6},{6,0},{1,3},{3,5},{5,7},{7,1},{8,10},{10,12},{12... | collective-permute-start | bytes 104456 | tf_op jit(solution)/shard_map/ppermute | solution.py:228
  23.8 3.3 %collective-permute-done.4 = bf16[8,2176]{1,0:T(8,128)(2,1)S(1)} collective-permute-done((bf16[8,2176]{1,0:T(8,128)(2,1)S(1)}, bf16[8,2176]{1,0:T(8,128)(2,1)S(1)}, u32[]{:S(2)}, u32[]{:S(2)}) %collective-permute-start.4) | collective-permute-done | bytes 34848 | tf_op jit(solution)/shard_map/ppermute | solution.py:228
  29.0 33.6 %all_to_all.20 = bf16[16,4,8,2048]{3,2,1,0:T(8,128)(2,1)S(1)} all-to-all(bf16[16,4,8,2048]{3,2,1,0:T(8,128)(2,1)S(1)} %broadcast_in_dim.54), channel_id=1, replica_groups=mesh['x'=4,'y'=4,'zl'=4,'zh'=4,'core'=2] {'x','y'}, dimensions={0} | all-to-all | bytes 4194304 | tf_op jit(solution)/shard_map/all_to_all | solution.py:246
  62.6 1.9 collective-permute-start.6
  64.5 2.8 %collective-permute-start = (bf16[2,192,1024]{2,1,0:T(8,128)(2,1)}, bf16[2,192,1024]{2,1,0:T(8,128)(2,1)}, u32[]{:S(2)}, u32[]{:S(2)}) collective-permute-start(bf16[2,192,1024]{2,1,0:T(8,128)(2,1)} %param.9), channel_id=1, source_target_pairs={{0,8},{8,16},{16,24},{24,32},{32,40},{40,48},{48,56},{56,64},{64,7... | collective-permute-start | bytes 2359304 | tf_op jit(solution)/shard_map/ppermute | solution.py:312
  67.3 3.9 %collective-permute-start.1 = (bf16[2,192,1024]{2,1,0:T(8,128)(2,1)}, bf16[2,192,1024]{2,1,0:T(8,128)(2,1)}, u32[]{:S(2)}, u32[]{:S(2)}) collective-permute-start(bf16[2,192,1024]{2,1,0:T(8,128)(2,1)} %param.9), channel_id=1, source_target_pairs={{8,0},{16,8},{24,16},{32,24},{40,32},{48,40},{56,48},{64,56},{72,6... | collective-permute-start | bytes 2359304 | tf_op jit(solution)/shard_map/ppermute | solution.py:313
  71.6 1.9 collective-permute-start.5
  74.7 11.9 %collective-permute-done = bf16[2,192,1024]{2,1,0:T(8,128)(2,1)} collective-permute-done((bf16[2,192,1024]{2,1,0:T(8,128)(2,1)}, bf16[2,192,1024]{2,1,0:T(8,128)(2,1)}, u32[]{:S(2)}, u32[]{:S(2)}) %collective-permute-start) | collective-permute-done | bytes 786464 | tf_op jit(solution)/shard_map/ppermute | solution.py:312
  86.7 18.2 %collective-permute-done.1 = bf16[2,192,1024]{2,1,0:T(8,128)(2,1)} collective-permute-done((bf16[2,192,1024]{2,1,0:T(8,128)(2,1)}, bf16[2,192,1024]{2,1,0:T(8,128)(2,1)}, u32[]{:S(2)}, u32[]{:S(2)}) %collective-permute-start.1) | collective-permute-done | bytes 786464 | tf_op jit(solution)/shard_map/ppermute | solution.py:313
  104.9 2.1 fusion
  109.6 6.6 %convolution_convert_fusion.q_ref.k_ref.v_ref.low_q_ref.high_q_ref = bf16[2,576,1536]{2,1,0:T(8,128)(2,1)S(1)} fusion(bf16[1024,1536,1]{1,0,2:T(8,128)(2,1)S(1)} %bitcast.107, f32[1024]{0:T(1024)S(1)} %bitcast.123, f32[2,576]{1,0:T(2,128)S(1)} %add_rsqrt_fusion, bf16[2,192,1024]{2,1,0:T(8,128)(2,1)} %collective-permute-done.1, ...), kind=kOutput, calls=%fused_computation.5 | convolution fusion | flops 3636264960 | bytes 9052672 | tf_op jit(solution)/shard_map/sti,iy->sty/dot_general | solution.py:324
  116.2 7.5 %shard_map.113 = (bf16[2,192,512]{2,1,0:T(8,128)(2,1)S(1)}, f32[2,4,2,384]{3,2,1,0:T(2,128)S(1)}) custom-call(f32[9,1,384]{2,1,0:T(1,128)S(1)} %tile.19.bias_ref, bf16[2,576,1536]{2,1,0:T(8,128)(2,1)S(1)} %convolution_convert_fusion.q_ref.k_ref.v_ref.low_q_ref.high_q_ref, ...), custom_call_target="tpu_custom_call" | custom-call | flops 452984832 | bytes 1179648 | tf_op jit(solution)/shard_map/pallas_call | solution.py:159
  124.7 2.0 collective-permute-start.7
  130.7 4.5 %all-to-all-start.1 = ((bf16[16,4,16,256]{3,2,1,0:T(8,128)(2,1)}), bf16[16,4,16,256]{3,2,1,0:T(8,128)(2,1)}, u32[]{:S(2)}, u32[]{:S(2)}) async-start(bf16[16,4,16,256]{3,2,1,0:T(8,128)(2,1)} %bitcast.45), calls=%async_computation.1 | async-start | bytes 1048576 | tf_op jit(solution)/shard_map/all_to_all | solution.py:293
  137.1 3.6 %collective-permute-start.10 = (bf16[2,192,512]{2,1,0:T(8,128)(2,1)S(1)}, bf16[2,192,512]{2,1,0:T(8,128)(2,1)S(1)}, u32[]{:S(2)}, u32[]{:S(2)}) collective-permute-start(bf16[2,192,512]{2,1,0:T(8,128)(2,1)S(1)} %fusion.12.g_ref), channel_id=1, source_target_pairs={{0,8},{8,16},{16,24},{24,32},{32,40},{40,48},{48,56},{56,64},{64,7... | collective-permute-start | bytes 1179656 | tf_op jit(solution)/shard_map/ppermute | solution.py:343
  140.7 2.3 collective-permute-start.11
  143.0 2.0 copy-done.2
  145.7 8.1 %shard_map.114 = (bf16[2,192,512]{2,1,0:T(8,128)(2,1)S(1)}, f32[2,2,192,512]{3,2,1,0:T(8,128)S(1)}, f32[2,4,3,384]{3,2,1,0:T(4,128)S(1)}) custom-call(f32[9,1,384]{2,1,0:T(1,128)S(1)} %tile.19.bias_ref, bf16[2,576,1536]{2,1,0:T(8,128)(2,1)S(1)} %copy-done.2, bf16[2,576,1536]{2,1,0:T(8,128)(2,1)S(1)} %copy-done.2, bf16[2,576,1536]{2,1,0:T(8,128)(2,1)S(1)} %copy-done.2, ...), custom_call_target="tpu_custom_call" | custom-call | flops 905969664 | bytes 2359296 | tf_op jit(solution)/shard_map/pallas_call | solution.py:171
  158.0 3.6 %collective-permute-start.8 = (f32[27,384]{1,0:T(8,128)S(1)}, f32[27,384]{1,0:T(8,128)S(1)}, u32[]{:S(2)}, u32[]{:S(2)}) collective-permute-start(f32[27,384]{1,0:T(8,128)S(1)} %get-tuple-element.48), channel_id=1, source_target_pairs={{0,8},{8,16},{16,24},{24,32},{32,40},{40,48},{48,56},{56,64},{64,7... | collective-permute-start | bytes 124424 | tf_op jit(solution)/shard_map/ppermute | solution.py:353
  161.6 2.2 collective-permute-start.9
  163.8 2.6 %convolution_convert_fusion.1 = bf16[2,192,1024]{2,1,0:T(8,128)(2,1)} fusion(bf16[2,192,512]{2,1,0:T(8,128)(2,1)S(1)} %get-tuple-element.18, bf16[512,256]{1,0:T(8,128)(2,1)} %bitcast.115, bf16[512,256]{1,0:T(8,128)(2,1)} %bitcast.117, bf16[512,256]{1,0:T(8,128)(2,1)} %bitcast.113, bf16[512,256]{1,0:T(8,128)(2,1)} %bitcast.111), kind=kOutput, calls=%fused_computation.22 | convolution fusion | flops 407240704 | bytes 2228224 | tf_op jit(solution)/shard_map/sty,yb->stb/dot_general | solution.py:356
  173.7 17.8 %all-to-all-start.2 = ((f32[16,16,256]{2,1,0:T(8,128)}), f32[16,16,256]{2,1,0:T(8,128)}, u32[]{:S(2)}, u32[]{:S(2)}) async-start(f32[16,16,256]{2,1,0:T(8,128)} %bitcast.46), calls=%async_computation.2 | async-start | bytes 524288 | tf_op jit(solution)/shard_map/all_to_all | solution.py:296
  191.5 2.0 copy-done.3
  194.9 7.5 %shard_map.115 = (bf16[2,192,512]{2,1,0:T(8,128)(2,1)S(1)}, bf16[2,192,512]{2,1,0:T(8,128)(2,1)S(1)}) custom-call(f32[3,1,384]{2,1,0:T(1,128)S(1)} %copy-done.7, f32[3,1,384]{2,1,0:T(1,128)S(1)} %copy-done.8, bf16[2,576,1536]{2,1,0:T(8,128)(2,1)S(1)} %copy-done.3, bf16[2,576,1536]{2,1,0:T(8,128)(2,1)S(1)} %copy-done.3, bf16[2,576,1536]{2,1,0:T(8,128)(2,1)S(1)} %copy-done.3, ...), custom_call_target="tpu_custom_call" | custom-call | flops 679477248 | bytes 1769472 | tf_op jit(solution)/shard_map/pallas_call | solution.py:181
  202.4 2.7 %fusion.7 = (f32[2,192]{1,0:T(2,128)S(1)}, f32[2,192]{1,0:T(2,128)S(1)}, f32[2,192,1024]{2,1,0:T(8,128)S(1)}) fusion(bf16[2,192,1024]{2,1,0:T(8,128)(2,1)} %param.9, f32[1024]{0:T(1024)S(1)} %bitcast.124, bf16[1024,1536,1]{1,0,2:T(8,128)(2,1)S(1)} %bitcast.108, bf16[2,192,512]{2,1,0:T(8,128)(2,1)S(1)} %get-tuple-element.23, ...), kind=kOutput, calls=%fused_computation.16 | convolution fusion | flops 1213857024 | bytes 6691840 | tf_op jit(solution)/shard_map/sty,iy->sti/dot_general | solution.py:363
  205.1 4.2 %all-to-all-done.2 = f32[16,16,256]{2,1,0:T(8,128)} async-done(((f32[16,16,256]{2,1,0:T(8,128)}), f32[16,16,256]{2,1,0:T(8,128)}, u32[]{:S(2)}, u32[]{:S(2)}) %all-to-all-start.2) | async-done | bytes 262176 | tf_op jit(solution)/shard_map/all_to_all | solution.py:296
  211.0 10.4 %all-to-all-start.3 = ((f32[16,16,256]{2,1,0:T(8,128)}), f32[16,16,256]{2,1,0:T(8,128)S(1)}, u32[]{:S(2)}, u32[]{:S(2)}) async-start(f32[16,16,256]{2,1,0:T(8,128)} %broadcast_in_dim.60), calls=%async_computation.3 | async-start | bytes 524288 | tf_op jit(solution)/shard_map/all_to_all | solution.py:246
  221.4 2.4 %fusion.10 = bf16[2,192,1024]{2,1,0:T(8,128)(2,1)} fusion(bf16[2,192,1024]{2,1,0:T(8,128)(2,1)} %param.9, f32[2,192,1024]{2,1,0:T(8,128)S(1)} %get-tuple-element.55, f32[2,192]{1,0:T(2,128)S(1)} %broadcast_multiply_fusion.1, f32[2,192]{1,0:T(2,128)S(1)} %get-tuple-element.52, f32[2,192]{1,0:T(2,128)S(1)} %get-tuple-element.51), kind=kLoop, calls=%fused_computation.19 | loop fusion | flops 2359296 | bytes 3150336 | tf_op jit(solution)/shard_map/convert_element_type | solution.py:368
  223.7 6.1 %all-to-all-done.3 = f32[16,16,256]{2,1,0:T(8,128)S(1)} async-done(((f32[16,16,256]{2,1,0:T(8,128)}), f32[16,16,256]{2,1,0:T(8,128)S(1)}, u32[]{:S(2)}, u32[]{:S(2)}) %all-to-all-start.3) | async-done | bytes 262176 | tf_op jit(solution)/shard_map/all_to_all | solution.py:246
  (123 shorter events, 29.5 us)
Async XLA Ops:
  0.6 123.2 %copy-start = (bf16[2,192,1024]{2,1,0:T(8,128)(2,1)S(1)}, bf16[2,192,1024]{2,1,0:T(8,128)(2,1)}, u32[]{:S(2)}) copy-start(bf16[2,192,1024]{2,1,0:T(8,128)(2,1)} %param.17) | copy-start | bytes 2359300
  3.3 14.1 %collective-permute-start.3 = (bf16[8,2176]{1,0:T(8,128)(2,1)}, bf16[8,2176]{1,0:T(8,128)(2,1)S(1)}, u32[]{:S(2)}, u32[]{:S(2)}) collective-permute-start(bf16[8,2176]{1,0:T(8,128)(2,1)} %shard_map.112), channel_id=1, source_target_pairs={{0,2},{2,4},{4,6},{6,0},{1,3},{3,5},{5,7},{7,1},{8,10},{10,12},{12... | collective-permute-start | bytes 104456 | tf_op jit(solution)/shard_map/ppermute | solution.py:226
  12.4 11.4 %collective-permute-start.2 = (bf16[8,2176]{1,0:T(8,128)(2,1)}, bf16[8,2176]{1,0:T(8,128)(2,1)S(1)}, u32[]{:S(2)}, u32[]{:S(2)}) collective-permute-start(bf16[8,2176]{1,0:T(8,128)(2,1)} %shard_map.112), channel_id=1, source_target_pairs={{2,0},{4,2},{6,4},{0,6},{3,1},{5,3},{7,5},{1,7},{10,8},{12,10},{14... | collective-permute-start | bytes 104456 | tf_op jit(solution)/shard_map/ppermute | solution.py:227
  17.4 9.7 %collective-permute-start.4 = (bf16[8,2176]{1,0:T(8,128)(2,1)S(1)}, bf16[8,2176]{1,0:T(8,128)(2,1)S(1)}, u32[]{:S(2)}, u32[]{:S(2)}) collective-permute-start(bf16[8,2176]{1,0:T(8,128)(2,1)S(1)} %collective-permute-done.3), channel_id=1, source_target_pairs={{0,2},{2,4},{4,6},{6,0},{1,3},{3,5},{5,7},{7,1},{8,10},{10,12},{12... | collective-permute-start | bytes 104456 | tf_op jit(solution)/shard_map/ppermute | solution.py:228
  29.0 42.3 %copy-start.21 = (s32[3,9]{1,0:T(4,128)S(1)}, s32[3,9]{1,0:T(4,128)}, u32[]{:S(2)}) copy-start(s32[3,9]{1,0:T(4,128)} %param.15) | copy-start | bytes 328
  29.0 42.4 %copy-start.20 = (s32[3,9]{1,0:T(4,128)S(1)}, s32[3,9]{1,0:T(4,128)}, u32[]{:S(2)}) copy-start(s32[3,9]{1,0:T(4,128)} %param.16) | copy-start | bytes 328
  62.6 44.4 %collective-permute-start.6 = (bf16[16,4,8,2048]{3,2,1,0:T(8,128)(2,1)S(1)}, bf16[16,4,8,2048]{3,2,1,0:T(8,128)(2,1)}, u32[]{:S(2)}, u32[]{:S(2)}) collective-permute-start(bf16[16,4,8,2048]{3,2,1,0:T(8,128)(2,1)S(1)} %all_to_all.20), channel_id=1, source_target_pairs={{0,1},{1,0},{2,3},{3,2},{4,5},{5,4},{6,7},{7,6},{8,9},{9,8},{10,11... | collective-permute-start | bytes 6291464 | tf_op jit(solution)/shard_map/ppermute | solution.py:234
  64.5 22.2 %collective-permute-start = (bf16[2,192,1024]{2,1,0:T(8,128)(2,1)}, bf16[2,192,1024]{2,1,0:T(8,128)(2,1)}, u32[]{:S(2)}, u32[]{:S(2)}) collective-permute-start(bf16[2,192,1024]{2,1,0:T(8,128)(2,1)} %param.9), channel_id=1, source_target_pairs={{0,8},{8,16},{16,24},{24,32},{32,40},{40,48},{48,56},{56,64},{64,7... | collective-permute-start | bytes 2359304 | tf_op jit(solution)/shard_map/ppermute | solution.py:312
  67.3 37.6 %collective-permute-start.1 = (bf16[2,192,1024]{2,1,0:T(8,128)(2,1)}, bf16[2,192,1024]{2,1,0:T(8,128)(2,1)}, u32[]{:S(2)}, u32[]{:S(2)}) collective-permute-start(bf16[2,192,1024]{2,1,0:T(8,128)(2,1)} %param.9), channel_id=1, source_target_pairs={{8,0},{16,8},{24,16},{32,24},{40,32},{48,40},{56,48},{64,56},{72,6... | collective-permute-start | bytes 2359304 | tf_op jit(solution)/shard_map/ppermute | solution.py:313
  71.6 3.1 %collective-permute-start.5 = (bf16[4,8,128]{2,1,0:T(8,128)(2,1)S(1)}, bf16[4,8,128]{2,1,0:T(8,128)(2,1)S(1)}, u32[]{:S(2)}, u32[]{:S(2)}) collective-permute-start(bf16[4,8,128]{2,1,0:T(8,128)(2,1)S(1)} %constant_dynamic-slice_fusion), channel_id=1, source_target_pairs={{0,1},{1,0},{2,3},{3,2},{4,5},{5,4},{6,7},{7,6},{8,9},{9,8},{10,11... | collective-permute-start | bytes 24584 | tf_op jit(solution)/shard_map/ppermute | solution.py:234
  74.7 34.8 %copy-start.18 = (f32[4,2,128]{2,1,0:T(2,128)}, f32[4,2,128]{2,1,0:T(2,128)S(1)}, u32[]{:S(2)}) copy-start(f32[4,2,128]{2,1,0:T(2,128)S(1)} %copy.42) | copy-start | bytes 12292
  109.5 6.7 %copy-start.11 = (bf16[4,2,16,8,1536]{4,3,2,1,0:T(8,128)(2,1)}, bf16[4,2,16,8,1536]{4,3,2,1,0:T(8,128)(2,1)S(1)}, u32[]{:S(2)}) copy-start(bf16[4,2,16,8,1536]{4,3,2,1,0:T(8,128)(2,1)S(1)} %copy.43) | copy-start | bytes 9437188
  116.2 7.6 %copy-start.1 = (bf16[2,576,1536]{2,1,0:T(8,128)(2,1)}, bf16[2,576,1536]{2,1,0:T(8,128)(2,1)S(1)}, u32[]{:S(2)}) copy-start(bf16[2,576,1536]{2,1,0:T(8,128)(2,1)S(1)} %convolution_convert_fusion.q_ref.k_ref.v_ref.low_q_ref.high_q_ref) | copy-start | bytes 10616836
  123.8 0.9 copy-start.5
  124.7 4.6 %collective-permute-start.7 = (f32[4,64,1024]{2,1,0:T(8,128)S(1)}, f32[4,64,1024]{2,1,0:T(8,128)S(1)}, u32[]{:S(2)}, u32[]{:S(2)}) collective-permute-start(f32[4,64,1024]{2,1,0:T(8,128)S(1)} %select_bitcast_fusion), channel_id=1, source_target_pairs={{0,1},{1,0},{2,3},{3,2},{4,5},{5,4},{6,7},{7,6},{8,9},{9,8},{10,11... | collective-permute-start | bytes 3145736 | tf_op jit(solution)/shard_map/ppermute | solution.py:234
  127.1 0.9 copy-start.14
  127.1 0.9 copy-start.15
  127.1 1.0 copy-start.16
  130.7 41.2 %all-to-all-start.1 = ((bf16[16,4,16,256]{3,2,1,0:T(8,128)(2,1)}), bf16[16,4,16,256]{3,2,1,0:T(8,128)(2,1)}, u32[]{:S(2)}, u32[]{:S(2)}) async-start(bf16[16,4,16,256]{3,2,1,0:T(8,128)(2,1)} %bitcast.45), calls=%async_computation.1 | async-start | bytes 1048576 | tf_op jit(solution)/shard_map/all_to_all | solution.py:293
  137.1 54.4 %collective-permute-start.10 = (bf16[2,192,512]{2,1,0:T(8,128)(2,1)S(1)}, bf16[2,192,512]{2,1,0:T(8,128)(2,1)S(1)}, u32[]{:S(2)}, u32[]{:S(2)}) collective-permute-start(bf16[2,192,512]{2,1,0:T(8,128)(2,1)S(1)} %fusion.12.g_ref), channel_id=1, source_target_pairs={{0,8},{8,16},{16,24},{24,32},{32,40},{40,48},{48,56},{56,64},{64,7... | collective-permute-start | bytes 1179656 | tf_op jit(solution)/shard_map/ppermute | solution.py:343
  140.7 50.8 %collective-permute-start.11 = (bf16[2,192,512]{2,1,0:T(8,128)(2,1)S(1)}, bf16[2,192,512]{2,1,0:T(8,128)(2,1)}, u32[]{:S(2)}, u32[]{:S(2)}) collective-permute-start(bf16[2,192,512]{2,1,0:T(8,128)(2,1)S(1)} %fusion.12.g_ref), channel_id=1, source_target_pairs={{8,0},{16,8},{24,16},{32,24},{40,32},{48,40},{56,48},{64,56},{72,6... | collective-permute-start | bytes 1179656 | tf_op jit(solution)/shard_map/ppermute | solution.py:343
  142.9 2.0 copy-start.2
  144.9 0.7 copy-start.6
  154.4 0.8 copy-start.9
  158.0 8.5 %collective-permute-start.8 = (f32[27,384]{1,0:T(8,128)S(1)}, f32[27,384]{1,0:T(8,128)S(1)}, u32[]{:S(2)}, u32[]{:S(2)}) collective-permute-start(f32[27,384]{1,0:T(8,128)S(1)} %get-tuple-element.48), channel_id=1, source_target_pairs={{0,8},{8,16},{16,24},{24,32},{32,40},{40,48},{48,56},{56,64},{64,7... | collective-permute-start | bytes 124424 | tf_op jit(solution)/shard_map/ppermute | solution.py:353
  161.6 6.8 %collective-permute-start.9 = (f32[27,384]{1,0:T(8,128)}, f32[27,384]{1,0:T(8,128)}, u32[]{:S(2)}, u32[]{:S(2)}) collective-permute-start(f32[27,384]{1,0:T(8,128)} %get-tuple-element.47), channel_id=1, source_target_pairs={{8,0},{16,8},{24,16},{32,24},{40,32},{48,40},{56,48},{64,56},{72,6... | collective-permute-start | bytes 124424 | tf_op jit(solution)/shard_map/ppermute | solution.py:354
  173.7 35.6 %all-to-all-start.2 = ((f32[16,16,256]{2,1,0:T(8,128)}), f32[16,16,256]{2,1,0:T(8,128)}, u32[]{:S(2)}, u32[]{:S(2)}) async-start(f32[16,16,256]{2,1,0:T(8,128)} %bitcast.46), calls=%async_computation.2 | async-start | bytes 524288 | tf_op jit(solution)/shard_map/all_to_all | solution.py:296
  191.5 2.0 copy-start.3
  194.9 7.5 %copy-start.10 = (bf16[2,192,512]{2,1,0:T(8,128)(2,1)S(1)}, bf16[2,192,512]{2,1,0:T(8,128)(2,1)}, u32[]{:S(2)}) copy-start(bf16[2,192,512]{2,1,0:T(8,128)(2,1)} %copy-done.9) | copy-start | bytes 1179652
  194.9 7.5 %copy-start.12 = (bf16[4,2,16,8,1536]{4,3,2,1,0:T(8,128)(2,1)S(1)}, bf16[4,2,16,8,1536]{4,3,2,1,0:T(8,128)(2,1)}, u32[]{:S(2)}) copy-start(bf16[4,2,16,8,1536]{4,3,2,1,0:T(8,128)(2,1)} %copy-done.11) | copy-start | bytes 9437188
  194.9 7.5 %copy-start.19 = (f32[4,2,128]{2,1,0:T(2,128)S(1)}, f32[4,2,128]{2,1,0:T(2,128)}, u32[]{:S(2)}) copy-start(f32[4,2,128]{2,1,0:T(2,128)} %copy-done.18) | copy-start | bytes 12292
  211.0 18.9 %all-to-all-start.3 = ((f32[16,16,256]{2,1,0:T(8,128)}), f32[16,16,256]{2,1,0:T(8,128)S(1)}, u32[]{:S(2)}, u32[]{:S(2)}) async-start(f32[16,16,256]{2,1,0:T(8,128)} %broadcast_in_dim.60), calls=%async_computation.3 | async-start | bytes 524288 | tf_op jit(solution)/shard_map/all_to_all | solution.py:246
  (5 other events, 3.3 us)

commit v4 on v3

--- a/solution.py
+++ b/solution.py
@@ -52,32 +52,36 @@
     scores = masked_scores(bias_ref[...], k_ref[0], stacked(q_ref[0], SCALE))
     row_max = jnp.max(scores, axis=0, keepdims=True)
     shifted = jnp.exp(scores - row_max)
-    inverse = 1.0 / jnp.sum(shifted, axis=0, keepdims=True)
-    prob_bf = (shifted * inverse).astype(BF16)
+    total = jnp.sum(shifted, axis=0, keepdims=True)
+    prob_bf = (shifted * (1.0 / total)).astype(BF16)
     att_ref[0] = merged(contract(v_ref[0], prob_bf, 0, 0)).astype(BF16)
-    stat_ref[0, 0, 0:1, :] = row_max
-    stat_ref[0, 0, 1:2, :] = inverse
-
-
-def query_kernel(bias_ref, q_ref, k_ref, v_ref, g_ref, stat_ref, dq_ref, own_ref, all_ref):
+    stat_ref[0, 0] = row_max + jnp.log(total)
+
+
+def probability(bias, key, query, stats):
+    return jnp.exp(masked_scores(bias, key, query) - stats[0:1])
+
+
+def query_kernel(bias_ref, q_ref, k_ref, v_ref, g_ref, stat_ref, dq_ref, own_ref, sent_ref):
     rows = q_ref.shape[1]
     query, key, value, grad = (stacked(q_ref[0], SCALE), k_ref[0], v_ref[0], stacked(g_ref[0]))
-    row_max, inverse = (stat_ref[0, 0, 0:1, :], stat_ref[0, 0, 1:2, :])
-    prob = jnp.exp(masked_scores(bias_ref[...], key, query) - row_max) * inverse
+    stats = stat_ref[0, 0]
+    prob = probability(bias_ref[...], key, query, stats)
     d_prob = contract(value, grad, 1, 1)
     delta = jnp.sum(prob * d_prob, axis=0, keepdims=True)
     d_score = (prob * (d_prob - delta)).astype(BF16)
     dq_ref[0] = (merged(contract(key, d_score, 0, 0)) * SCALE).astype(BF16)
     own_ref[0, 0] = contract(d_score[rows : 2 * rows], query, 1, 0)
     own_ref[1, 0] = contract(prob[rows : 2 * rows].astype(BF16), grad, 1, 0)
-    all_ref[0, 0, 0:1, :] = row_max
-    all_ref[0, 0, 1:2, :] = inverse
-    all_ref[0, 0, 2:3, :] = delta
+    third = bias_ref.shape[0] // 3
+    sent_ref[0, 0, 0:1, :] = stats
+    sent_ref[0, 0, 1:2, :] = delta
+    for i in range(third):
+        sent_ref[0, 0, 2 + i : 3 + i, :] = bias_ref[2 * third + i]
+        sent_ref[0, 0, 2 + third + i : 3 + third + i, :] = bias_ref[i]
 
 
 def key_kernel(
-    low_bias_ref,
-    high_bias_ref,
     low_q_ref,
     high_q_ref,
     k_ref,
@@ -92,18 +96,16 @@
 ):
     key, value = (k_ref[0], v_ref[0])
     d_key, d_value = (own_ref[0, 0], own_ref[1, 0])
-    sides = (
-        (low_bias_ref, low_q_ref, low_g_ref, low_stat_ref),
-        (high_bias_ref, high_q_ref, high_g_ref, high_stat_ref),
-    )
-    for bias_ref, q_ref, g_ref, stat_ref in sides:
-        query, grad = (stacked(q_ref[0], SCALE), stacked(g_ref[0]))
-        scores = masked_scores(bias_ref[...], key, query)
-        prob = jnp.exp(scores - stat_ref[0, 0, 0:1, :]) * stat_ref[0, 0, 1:2, :]
-        d_prob = contract(value, grad, 1, 1)
-        d_score = (prob * (d_prob - stat_ref[0, 0, 2:3, :])).astype(BF16)
-        d_key += contract(d_score, query, 1, 0)
-        d_value += contract(prob.astype(BF16), grad, 1, 0)
+    sides = ((low_q_ref, low_g_ref, low_stat_ref), (high_q_ref, high_g_ref, high_stat_ref))
+    for side, (q_ref, g_ref, stat_ref) in enumerate(sides):
+        query, grad, stats = (stacked(q_ref[0], SCALE), stacked(g_ref[0]), stat_ref[0, 0])
+        third = (stats.shape[0] - 2) // 2
+        first = 2 + side * third
+        bias = jnp.stack([stats[first + i : first + i + 1] for i in range(third)])
+        prob = probability(bias, key, query, stats)
+        d_score = (prob * (contract(value, grad, 1, 1) - stats[1:2])).astype(BF16)
+        d_key += contract(d_score, query, 1, 0).astype(BF16).astype(F32)
+        d_value += contract(prob.astype(BF16), grad, 1, 0).astype(BF16).astype(F32)
     dk_ref[0] = d_key.astype(BF16)
     dv_ref[0] = d_value.astype(BF16)
 
@@ -155,30 +157,30 @@
 def forward_attention(bias, joint):
     plan = Plan(joint)
     given = [plan.bias(bias), plan.joint(0, 1), plan.joint(1), plan.joint(2)]
-    outs = ([plan.narrow, plan.stat(2)], [plan.narrow_shape(), plan.stat_shape(2)])
+    outs = ([plan.narrow, plan.stat(1)], [plan.narrow_shape(), plan.stat_shape(1)])
     return plan.call(forward_kernel, 2, given, *outs)(bias, joint, joint, joint)
 
 
 def query_gradient(bias, joint, grad, stats):
     plan = Plan(joint)
+    count = 2 + 2 * (bias.shape[0] // 3)
     given = [plan.bias(bias), plan.joint(0, 1), plan.joint(1), plan.joint(2)]
-    given += [plan.narrow, plan.stat(2)]
+    given += [plan.narrow, plan.stat(1)]
     own = jax.ShapeDtypeStruct((2, plan.samples, plan.rows, plan.width), F32)
     outs = (
-        [plan.narrow, plan.split, plan.stat(3)],
-        [plan.narrow_shape(), own, plan.stat_shape(3)],
+        [plan.narrow, plan.split, plan.stat(count)],
+        [plan.narrow_shape(), own, plan.stat_shape(count)],
     )
     return plan.call(query_kernel, 4, given, *outs)(bias, joint, joint, joint, grad, stats)
 
 
-def key_gradient(biases, joint, grads, stats, own):
+def key_gradient(joint, grads, stats, own):
     plan = Plan(joint)
-    given = [plan.bias(biases[0]), plan.bias(biases[1]), plan.joint(0, 0), plan.joint(0, 2)]
-    given += [plan.joint(1, 1), plan.joint(2, 1), plan.narrow, plan.narrow]
-    given += [plan.stat(3), plan.stat(3), plan.split]
+    given = [plan.joint(0, 0), plan.joint(0, 2), plan.joint(1, 1), plan.joint(2, 1)]
+    given += [plan.narrow] * 2 + [plan.stat(stats[0].shape[2])] * 2 + [plan.split]
     outs = ([plan.narrow] * 2, [plan.narrow_shape()] * 2)
     call = plan.call(key_kernel, 3, given, *outs)
-    return call(*biases, joint, joint, joint, joint, *grads, *stats, own)
+    return call(joint, joint, joint, joint, *grads, *stats, own)
 
 
 def slice_kernel(place_ref, q_ref, k_ref, v_ref, out_ref, gain_ref, part_ref):
@@ -220,24 +222,16 @@
 
 def column_gather(part):
     count = lax.axis_size(ZH)
-    place = lax.axis_index(ZH)
     up = [(i, (i + 1) % count) for i in range(count)]
     down = [(j, i) for i, j in up]
     first = lax.ppermute(part, ZH, up)
     third = lax.ppermute(part, ZH, down)
     second = lax.ppermute(first, ZH, up)
-    turned = jnp.stack([third, second, first, part] * 2)
-    return lax.dynamic_slice_in_dim(turned, count - 1 - place, count, 0)
+    return jnp.stack([first, third, second])
 
 
 def other_core(value):
     return lax.ppermute(value, CORE, [(0, 1), (1, 0)])
-
-
-def both_cores(mine):
-    theirs = other_core(mine)
-    first = lax.axis_index(CORE) == 0
-    return jnp.stack([jnp.where(first, mine, theirs), jnp.where(first, theirs, mine)])
 
 
 def plane_gather(piece):
@@ -246,30 +240,111 @@
     return lax.all_to_all(copies, PLANE, 0, 0, tiled=True)
 
 
+def pack_kernel(q_ref, k_ref, v_ref, out_ref, gain_ref, mine_ref):
+    depth, width = q_ref.shape
+    out_depth, half = (out_ref.shape[0], out_ref.shape[1] // 2)
+    for i, ref in enumerate((q_ref, k_ref, v_ref)):
+        mine_ref[:, i * width : (i + 1) * width] = ref[...]
+    begin = 3 * width
+    mine_ref[:out_depth, begin : begin + half] = out_ref[:, :half]
+    mine_ref[out_depth:, begin : begin + half] = out_ref[:, half:]
+    mine_ref[:, begin + half :] = jnp.broadcast_to(gain_ref[...], (depth, gain_ref.shape[1]))
+
+
+def assembly_kernel(
+    place_ref, mine_ref, theirs_ref, far_ref, other_ref, joint_ref, out_ref, gain_ref
+):
+    step = pl.program_id(0)
+    width = joint_ref.shape[1]
+    half = out_ref.shape[1] // 2
+    depth, rows = (out_ref.shape[0], gain_ref.shape[1])
+    count = far_ref.shape[0]
+    columns = (far_ref.shape[3] - width - gain_ref.shape[2]) // 2
+    across = out_ref.shape[1] // columns
+
+    def near(ref):
+        joint_ref[...] = ref[:, :width]
+        out_ref[:, :half] = ref[:depth, width : width + half]
+        out_ref[:, half:] = ref[depth:, width : width + half]
+        gain_ref[0] = ref[:rows, width + half :]
+
+    def distant(ref):
+        for s in range(count):
+            joint_ref[s * rows : (s + 1) * rows, :] = ref[s, 0, :, :width]
+            top, left = (s // across * 2 * rows, s % across * columns)
+            for fold in range(2):
+                begin = width + fold * columns
+                place = slice(top + fold * rows, top + (fold + 1) * rows)
+                out_ref[place, left : left + columns] = ref[s, 0, :, begin : begin + columns]
+        gain_ref[0] = ref[0, 0, :, width + 2 * columns :]
+
+    pl.when(step == 0)(lambda: near(mine_ref))
+    pl.when(step == 1)(lambda: near(theirs_ref))
+    pl.when(jnp.logical_and(step > 1, step < 5))(lambda: distant(far_ref))
+    pl.when(step >= 5)(lambda: distant(other_ref))
+
+
+def assembled_weights(mine, theirs, far, other, width, out_shape):
+    nz = lax.axis_size(ZH)
+    zh, core = (lax.axis_index(ZH), lax.axis_index(CORE))
+    peers = [zh, (zh + nz - 1) % nz, (zh + 1) % nz, (zh + 2) % nz]
+    same = [2 * peer + core for peer in peers]
+    swapped = [2 * peer + 1 - core for peer in peers]
+    place = jnp.stack([same[0], swapped[0]] + same[1:] + swapped[1:])
+    count, _, rows, total = far.shape
+    depth = mine.shape[0]
+    out_depth, model_width = out_shape
+    gain_width = total - width - model_width // 2
+    whole = pl.BlockSpec(mine.shape, lambda i, place: (0, 0))
+
+    def distant(first):
+        return pl.BlockSpec(
+            (count, 1, rows, total),
+            lambda i, place: (0, jnp.clip(i - first, 0, 2), 0, 0),
+        )
+
+    shape = jax.ShapeDtypeStruct
+    return pl.pallas_call(
+        assembly_kernel,
+        grid_spec=pltpu.PrefetchScalarGridSpec(
+            num_scalar_prefetch=1,
+            grid=(2 * nz,),
+            in_specs=[whole, whole, distant(2), distant(5)],
+            out_specs=[
+                pl.BlockSpec((depth, width), lambda i, place: (place[i], 0)),
+                pl.BlockSpec((out_depth, model_width), lambda i, place: (place[i], 0)),
+                pl.BlockSpec((1, rows, gain_width), lambda i, place: (place[i], 0, 0)),
+            ],
+        ),
+        out_shape=[
+            shape((2 * nz * depth, width), BF16),
+            shape((2 * nz * out_depth, model_width), BF16),
+            shape((2 * nz, rows, gain_width), BF16),
+        ],
+        cost_estimate=pl.CostEstimate(flops=0, transcendentals=0, bytes_accessed=2**23),
+    )(place, mine, theirs, far, other)
+
+
 def gathered_weights(norm_gain, w_query, w_key, w_value, w_out):
-    nx, ny, nz = (lax.axis_size(X), lax.axis_size(Y), lax.axis_size(ZH))
+    nx, ny = (lax.axis_size(X), lax.axis_size(Y))
     depth, hidden_width = w_query.shape
     out_depth, model_width = w_out.shape
     rows = depth // (nx * ny)
     out_rows, out_columns = (out_depth // nx, model_width // ny)
-    folds = out_rows // rows
     part = own_slices(norm_gain, w_query, w_key, w_value, w_out, rows, out_rows, out_columns)
     part = column_gather(part)
-    width = 3 * hidden_width + folds * out_columns
-    gain = both_cores(part[:, :, width:])[:, :, 0]
-    gain = jnp.swapaxes(gain, 0, 1).reshape(-1)
-    whole = plane_gather(part[:, :, :width])
-    whole = both_cores(whole)
-    joint = jnp.transpose(whole[..., : 3 * hidden_width], (2, 0, 1, 3, 4))
-    joint = joint.reshape(2 * nz * depth, 3 * hidden_width)
-    whole = whole.reshape(2, nx, ny, nz, rows, width)
-    bands = []
-    for i in range(folds):
-        begin = 3 * hidden_width + i * out_columns
-        bands.append(jnp.transpose(whole[..., begin : begin + out_columns], (2, 3, 0, 1, 4, 5)))
-    bands = jnp.stack(bands, axis=4).reshape(ny, 2 * nz * out_depth, out_columns)
-    out_whole = jnp.concatenate([bands[i] for i in range(ny)], axis=1)
-    return gain, joint, out_whole
+    half = model_width // 2
+    far = plane_gather(part)
+    mine = pl.pallas_call(
+        pack_kernel,
+        out_shape=jax.ShapeDtypeStruct((depth, 3 * hidden_width + half + depth), BF16),
+    )(w_query, w_key, w_value, w_out, norm_gain[None])
+    theirs = other_core(mine)
+    other = other_core(far)
+    joint, out_whole, gain = assembled_weights(
+        mine, theirs, far, other, 3 * hidden_width, w_out.shape
+    )
+    return gain[:, 0, :].reshape(-1), joint, out_whole
 
 
 def halved_gradient(attended, cotangent):
@@ -322,6 +397,7 @@
     window = jnp.concatenate([below, inputs, above], axis=1)
     normed = (window.astype(F32) * inverse_of(window) * gain_float).astype(BF16)
     joint = jnp.einsum("sti,iy->sty", normed, w_joint, preferred_element_type=F32).astype(BF16)
+    joint = pltpu.with_memory_space_constraint(joint, pltpu.HBM)
     d_attention = jnp.einsum(
         "stz,yz->sty", output_cotangent, w_full_out, preferred_element_type=F32
     ).astype(BF16)
@@ -335,30 +411,17 @@
     bias = jnp.where(jnp.any(matches, axis=1).T, 0.0, MASKED).astype(F32)
     bias = jnp.tile(jnp.repeat(bias, block_len, axis=1), (1, 2))[:, None, :]
 
+    grads = (lax.ppermute(d_attention, DOMAIN, up), lax.ppermute(d_attention, DOMAIN, down))
     attended, stats = forward_attention(bias, joint)
     half = halved_gradient(attended, output_cotangent)
-    half, d_attention = lax.optimization_barrier((half, d_attention))
     members = lax.axis_size(MEMBER)
     grad_wout = summed_gradient(half, samples * members)
-    grads = (lax.ppermute(d_attention, DOMAIN, up), lax.ppermute(d_attention, DOMAIN, down))
     d_query, own, stats = query_gradient(bias, joint, d_attention, stats)
-    shape, flat = (stats.shape, (-1, stats.shape[-1]))
-    stats, attended = lax.optimization_barrier((stats, attended))
-
-    def message(third):
-        rows = bias[third * block_count : (third + 1) * block_count]
-        return jnp.concatenate([stats.reshape(flat), rows.reshape(flat)], axis=0)
-
-    received = (
-        lax.ppermute(message(2), DOMAIN, up),
-        lax.ppermute(message(0), DOMAIN, down),
-    )
+    side_stats = (lax.ppermute(stats, DOMAIN, up), lax.ppermute(stats, DOMAIN, down))
+    d_key, d_value = key_gradient(joint, grads, side_stats, own)
     attn_out = jnp.einsum(
         "sty,yb->stb", attended, w_full_out, preferred_element_type=F32
     ).astype(BF16)
-    side_stats = [rows[:-block_count].reshape(shape) for rows in received]
-    side_bias = [rows[-block_count:][:, None, :] for rows in received]
-    d_key, d_value = key_gradient(side_bias, joint, grads, side_stats, own)
     d_joint = jnp.concatenate([d_query, d_key, d_value], axis=-1)
     d_normed = jnp.einsum("sty,iy->sti", d_joint, w_joint, preferred_element_type=F32)
     inputs_float = inputs.astype(F32)

time: 232 us -> 220 us (0.948)
  waiting for transfers between devices: 47.3 us -> 31 us
  local copies, waits for them, and re-layouts: 19.8 us -> 4.46 us
  starting transfers between devices: 76.9 us -> 89.5 us
  Pallas kernels: 25.1 us -> 36.9 us
  blocking collectives: 33.6 us -> 28.9 us
  other arithmetic: 13.4 us -> 10.3 us
  matrix products: 13.3 us -> 15.9 us
    all_to_all x1, starting transfers between devices: 4.46 us -> 19.4 us  [summed_gradient(): half = lax.all_to_all(half, (Y, X), 0, 0, tiled=True)]
    pallas_call x1 -> x3, Pallas kernels: 7.5 us -> 17 us  [the longest x1 7.63 us: key_gradient(): return call(joint, joint, joint, joint, *grads, *stats, own)]
    ppermute x1, waiting for transfers between devices: 11.9 us -> 2.64 us  [shards(): below = lax.ppermute(inputs, DOMAIN, up)]
    unnamed x51 -> x28, local copies, waits for them, and re-layouts: 9.34 us -> 1.53 us
    ppermute x1, waiting for transfers between devices: 18.2 us -> 10.8 us  [shards(): above = lax.ppermute(inputs, DOMAIN, down)]
    all_to_all x1, blocking collectives: 33.6 us -> 28.9 us  [plane_gather(): return lax.all_to_all(copies, PLANE, 0, 0, tiled=True)]
    slice x11 -> x1, local copies, waits for them, and re-layouts: 2.65 us -> 0.05 us  [the longest x2 1.42 us: shards(): side_bias = [rows[-block_count:][:, None, :] for rows in received]]
  transfers between devices with their start and end apart: 15 -> 15, of which waited for: 9 -> 7; matrix products, arithmetic and copies ran while one was open for 9% -> 7% of each run, Pallas kernels for 7% -> 9%
where the time goes in v4:
time: 220 us; the launch traced here: 218 us
  starting transfers between devices  89.5 us (41%)
  Pallas kernels  36.9 us (17%)
  waiting for transfers between devices  31 us (14%)
  blocking collectives  28.9 us (13%)
  matrix products  15.9 us (7%)
  other arithmetic  10.3 us (5%)
  local copies, waits for them, and re-layouts  4.46 us (2%)
    all_to_all x1, blocking collectives, plane_gather(): return lax.all_to_all(copies, PLANE, 0, 0, tiled=True)  28.9 us
    all_to_all x1, starting transfers between devices, summed_gradient(): half = lax.all_to_all(half, (Y, X), 0, 0, tiled=True)  19.4 us
    all_to_all x1, starting transfers between devices, summed_gradient(): part = lax.all_to_all(part, COLUMN, 0, 0, tiled=True)  16 us
    all_to_all x1, starting transfers between devices, plane_gather(): return lax.all_to_all(copies, PLANE, 0, 0, tiled=True)  10.8 us
    ppermute x1, waiting for transfers between devices, shards(): above = lax.ppermute(inputs, DOMAIN, down)  10.8 us
    pallas_call x1, Pallas kernels, query_gradient(): plan.call(query_kernel, 4, given, *outs)  9.34 us
    ppermute x1, starting transfers between devices, column_gather(): first = lax.ppermute(part, ZH, up)  9.08 us
    pallas_call x1, Pallas kernels, forward_attention(): return plan.call(forward_kernel, 2, given, *outs)(bias, joint, joint, joint)  8.44 us
  transfers between devices with their start and end apart: 15, of which 7 were waited for; matrix products, arithmetic and copies ran while one was open for 7% of the time, Pallas kernels for 9%

profile of v4, /device:TPU:32, one launch (start us, length us, event | category | flops | bytes accessed | tf_op | source)
XLA Modules:
  0.0 218.1 jit_solution(2771737462906777076)
XLA Ops:
  1.2 2.0 shard_map.113
  3.3 9.1 %collective-permute-start.3 = (bf16[8,2176]{1,0:T(8,128)(2,1)}, bf16[8,2176]{1,0:T(8,128)(2,1)S(1)}, u32[]{:S(2)}, u32[]{:S(2)}) collective-permute-start(bf16[8,2176]{1,0:T(8,128)(2,1)} %shard_map.113), channel_id=1, source_target_pairs={{0,2},{2,4},{4,6},{6,0},{1,3},{3,5},{5,7},{7,1},{8,10},{10,12},{12... | collective-permute-start | bytes 104456 | tf_op jit(solution)/shard_map/ppermute | solution.py:227
  12.4 4.7 %collective-permute-start.4 = (bf16[8,2176]{1,0:T(8,128)(2,1)}, bf16[8,2176]{1,0:T(8,128)(2,1)S(1)}, u32[]{:S(2)}, u32[]{:S(2)}) collective-permute-start(bf16[8,2176]{1,0:T(8,128)(2,1)} %shard_map.113), channel_id=1, source_target_pairs={{2,0},{4,2},{6,4},{0,6},{3,1},{5,3},{7,5},{1,7},{10,8},{12,10},{14... | collective-permute-start | bytes 104456 | tf_op jit(solution)/shard_map/ppermute | solution.py:228
  17.3 6.4 %collective-permute-start.5 = (bf16[8,2176]{1,0:T(8,128)(2,1)S(1)}, bf16[8,2176]{1,0:T(8,128)(2,1)S(1)}, u32[]{:S(2)}, u32[]{:S(2)}) collective-permute-start(bf16[8,2176]{1,0:T(8,128)(2,1)S(1)} %collective-permute-done.3), channel_id=1, source_target_pairs={{0,2},{2,4},{4,6},{6,0},{1,3},{3,5},{5,7},{7,1},{8,10},{10,12},{12... | collective-permute-start | bytes 104456 | tf_op jit(solution)/shard_map/ppermute | solution.py:229
  23.7 3.3 %collective-permute-done.5 = bf16[8,2176]{1,0:T(8,128)(2,1)S(1)} collective-permute-done((bf16[8,2176]{1,0:T(8,128)(2,1)S(1)}, bf16[8,2176]{1,0:T(8,128)(2,1)S(1)}, u32[]{:S(2)}, u32[]{:S(2)}) %collective-permute-start.5) | collective-permute-done | bytes 34848 | tf_op jit(solution)/shard_map/ppermute | solution.py:229
  27.3 28.9 %all_to_all.20.far_ref = bf16[16,3,8,2176]{3,2,1,0:T(8,128)(2,1)S(1)} all-to-all(bf16[16,3,8,2176]{3,2,1,0:T(8,128)(2,1)S(1)} %broadcast_in_dim.22), channel_id=1, replica_groups=mesh['x'=4,'y'=4,'zl'=4,'zh'=4,'core'=2] {'x','y'}, dimensions={0} | all-to-all | bytes 3342336 | tf_op jit(solution)/shard_map/all_to_all | solution.py:240
  56.2 1.9 collective-permute-start.6
  58.1 2.9 %collective-permute-start.1 = (bf16[2,192,1024]{2,1,0:T(8,128)(2,1)S(1)}, bf16[2,192,1024]{2,1,0:T(8,128)(2,1)}, u32[]{:S(2)}, u32[]{:S(2)}) collective-permute-start(bf16[2,192,1024]{2,1,0:T(8,128)(2,1)S(1)} %copy-done.6), channel_id=1, source_target_pairs={{8,0},{16,8},{24,16},{32,24},{40,32},{48,40},{56,48},{64,56},{72,6... | collective-permute-start | bytes 2359304 | tf_op jit(solution)/shard_map/ppermute | solution.py:388
  61.1 2.9 %collective-permute-start = (bf16[2,192,1024]{2,1,0:T(8,128)(2,1)S(1)}, bf16[2,192,1024]{2,1,0:T(8,128)(2,1)}, u32[]{:S(2)}, u32[]{:S(2)}) collective-permute-start(bf16[2,192,1024]{2,1,0:T(8,128)(2,1)S(1)} %copy-done.6), channel_id=1, source_target_pairs={{0,8},{8,16},{16,24},{24,32},{32,40},{40,48},{48,56},{56,64},{64,7... | collective-permute-start | bytes 2359304 | tf_op jit(solution)/shard_map/ppermute | solution.py:387
  64.0 1.9 shard_map.112.mine_ref
  65.9 1.9 collective-permute-start.2
  69.3 10.8 %collective-permute-done.1 = bf16[2,192,1024]{2,1,0:T(8,128)(2,1)} collective-permute-done((bf16[2,192,1024]{2,1,0:T(8,128)(2,1)S(1)}, bf16[2,192,1024]{2,1,0:T(8,128)(2,1)}, u32[]{:S(2)}, u32[]{:S(2)}) %collective-permute-start.1) | collective-permute-done | bytes 786464 | tf_op jit(solution)/shard_map/ppermute | solution.py:388
  80.1 2.6 %collective-permute-done = bf16[2,192,1024]{2,1,0:T(8,128)(2,1)} collective-permute-done((bf16[2,192,1024]{2,1,0:T(8,128)(2,1)S(1)}, bf16[2,192,1024]{2,1,0:T(8,128)(2,1)}, u32[]{:S(2)}, u32[]{:S(2)}) %collective-permute-start) | collective-permute-done | bytes 786464 | tf_op jit(solution)/shard_map/ppermute | solution.py:387
  84.7 7.5 %shard_map.114 = (bf16[1024,1536]{1,0:T(8,128)(2,1)}, bf16[512,1024]{1,0:T(8,128)(2,1)}, bf16[8,8,128]{2,1,0:T(8,128)(2,1)}) custom-call(s32[8]{0:T(128)} %stack.74.place_ref, bf16[128,2176]{1,0:T(8,128)(2,1)} %shard_map.112.mine_ref, bf16[128,2176]{1,0:T(8,128)(2,1)} %collective-permute-done.2.theirs_ref, bf16[16,3,8,2176]{3,2,1,0:T(8,128)(2,1)} %copy-done.5, ...), custom_call_target="tpu_custom_call" | custom-call | bytes 8388608 | tf_op jit(solution)/shard_map/pallas_call | solution.py:307
  92.9 8.0 %convolution_convert_fusion.q_ref.k_ref.v_ref.low_q_ref.high_q_ref = bf16[2,576,1536]{2,1,0:T(8,128)(2,1)} fusion(bf16[1024,1536]{1,0:T(8,128)(2,1)} %get-tuple-element.14, f32[1024]{0:T(1024)S(1)} %bitcast.89, f32[2,576]{1,0:T(2,128)S(1)} %add_rsqrt_fusion, bf16[2,192,1024]{2,1,0:T(8,128)(2,1)} %collective-permute-done.1, ...), kind=kOutput, calls=%fused_computation.5 | convolution fusion | flops 3636264960 | bytes 9052672 | tf_op jit(solution)/shard_map/sti,iy->sty/dot_general | solution.py:399
  100.9 8.4 %shard_map.115 = (bf16[2,192,512]{2,1,0:T(8,128)(2,1)S(1)}, f32[2,4,1,384]{3,2,1,0:T(1,128)S(1)}) custom-call(f32[9,1,384]{2,1,0:T(1,128)S(1)} %tile.11.bias_ref, bf16[2,576,1536]{2,1,0:T(8,128)(2,1)} %convolution_convert_fusion.q_ref.k_ref.v_ref.low_q_ref.high_q_ref, bf16[2,576,1536]{2,1,0:T(8,128)(2,1)} %convolution_convert_fusion.q_ref.k_ref.v_ref.low_q_ref.high_q_ref, ...), custom_call_target="tpu_custom_call" | custom-call | flops 452984832 | bytes 1179648 | tf_op jit(solution)/shard_map/pallas_call | solution.py:161
  110.3 1.9 collective-permute-start.11
  112.2 2.6 %collective-permute-done.11 = f32[4,64,1024]{2,1,0:T(8,128)S(1)} collective-permute-done((f32[4,64,1024]{2,1,0:T(8,128)S(1)}, f32[4,64,1024]{2,1,0:T(8,128)S(1)}, u32[]{:S(2)}, u32[]{:S(2)}) %collective-permute-start.11) | collective-permute-done | bytes 1048608 | tf_op jit(solution)/shard_map/ppermute | solution.py:234
  116.3 19.4 %all-to-all-start.1 = ((bf16[16,4,16,256]{3,2,1,0:T(8,128)(2,1)}), bf16[16,4,16,256]{3,2,1,0:T(8,128)(2,1)}, u32[]{:S(2)}, u32[]{:S(2)}) async-start(bf16[16,4,16,256]{3,2,1,0:T(8,128)(2,1)} %bitcast.32), calls=%async_computation.1 | async-start | bytes 1048576 | tf_op jit(solution)/shard_map/all_to_all | solution.py:368
  137.5 3.0 %collective-permute-start.8 = (bf16[2,192,512]{2,1,0:T(8,128)(2,1)S(1)}, bf16[2,192,512]{2,1,0:T(8,128)(2,1)S(1)}, u32[]{:S(2)}, u32[]{:S(2)}) collective-permute-start(bf16[2,192,512]{2,1,0:T(8,128)(2,1)S(1)} %fusion.17.g_ref), channel_id=1, source_target_pairs={{8,0},{16,8},{24,16},{32,24},{40,32},{48,40},{56,48},{64,56},{72,6... | collective-permute-start | bytes 1179656 | tf_op jit(solution)/shard_map/ppermute | solution.py:414
  140.4 2.9 %collective-permute-start.7 = (bf16[2,192,512]{2,1,0:T(8,128)(2,1)S(1)}, bf16[2,192,512]{2,1,0:T(8,128)(2,1)}, u32[]{:S(2)}, u32[]{:S(2)}) collective-permute-start(bf16[2,192,512]{2,1,0:T(8,128)(2,1)S(1)} %fusion.17.g_ref), channel_id=1, source_target_pairs={{0,8},{8,16},{16,24},{24,32},{32,40},{40,48},{48,56},{56,64},{64,7... | collective-permute-start | bytes 1179656 | tf_op jit(solution)/shard_map/ppermute | solution.py:414
  144.0 9.3 %shard_map.116 = (bf16[2,192,512]{2,1,0:T(8,128)(2,1)S(1)}, f32[2,2,192,512]{3,2,1,0:T(8,128)S(1)}, f32[2,4,8,384]{3,2,1,0:T(8,128)}) custom-call(f32[9,1,384]{2,1,0:T(1,128)S(1)} %tile.11.bias_ref, bf16[2,576,1536]{2,1,0:T(8,128)(2,1)} %convolution_convert_fusion.q_ref.k_ref.v_ref.low_q_ref.high_q_ref, ...), custom_call_target="tpu_custom_call" | custom-call | flops 905969664 | bytes 2359296 | tf_op jit(solution)/shard_map/pallas_call | solution.py:174
  154.2 3.7 %collective-permute-start.10 = (f32[2,4,8,384]{3,2,1,0:T(8,128)}, f32[2,4,8,384]{3,2,1,0:T(8,128)}, u32[]{:S(2)}, u32[]{:S(2)}) collective-permute-start(f32[2,4,8,384]{3,2,1,0:T(8,128)} %get-tuple-element.19), channel_id=1, source_target_pairs={{8,0},{16,8},{24,16},{32,24},{40,32},{48,40},{56,48},{64,56},{72,6... | collective-permute-start | bytes 294920 | tf_op jit(solution)/shard_map/ppermute | solution.py:420
  157.9 2.1 collective-permute-start.9
  161.9 16.0 %all-to-all-start.2 = ((f32[16,16,256]{2,1,0:T(8,128)}), f32[16,16,256]{2,1,0:T(8,128)}, u32[]{:S(2)}, u32[]{:S(2)}) async-start(f32[16,16,256]{2,1,0:T(8,128)} %bitcast.80), calls=%async_computation.2 | async-start | bytes 524288 | tf_op jit(solution)/shard_map/all_to_all | solution.py:371
  177.9 2.7 %convolution_convert_fusion.1 = bf16[2,192,1024]{2,1,0:T(8,128)(2,1)} fusion(bf16[2,192,512]{2,1,0:T(8,128)(2,1)S(1)} %get-tuple-element.15, bf16[512,1024]{1,0:T(8,128)(2,1)} %get-tuple-element.16), kind=kOutput, calls=%fused_computation.21 | convolution fusion | flops 403046400 | bytes 2228224 | tf_op jit(solution)/shard_map/sty,yb->stb/dot_general | solution.py:422
  180.6 7.6 %shard_map.117 = (bf16[2,192,512]{2,1,0:T(8,128)(2,1)S(1)}, bf16[2,192,512]{2,1,0:T(8,128)(2,1)S(1)}) custom-call(bf16[2,576,1536]{2,1,0:T(8,128)(2,1)} %convolution_convert_fusion.q_ref.k_ref.v_ref.low_q_ref.high_q_ref, bf16[2,576,1536]{2,1,0:T(8,128)(2,1)} %convolution_convert_fusion.q_ref.k_ref.v_ref.low_q_ref.high_q_ref, ...), custom_call_target="tpu_custom_call" | custom-call | flops 679477248 | bytes 1769472 | tf_op jit(solution)/shard_map/pallas_call | solution.py:183
  188.3 2.6 %fusion.9 = (f32[2,192]{1,0:T(2,128)S(1)}, f32[2,192]{1,0:T(2,128)S(1)}, f32[2,192,1024]{2,1,0:T(8,128)}) fusion(bf16[2,192,1024]{2,1,0:T(8,128)(2,1)S(1)} %copy-done.7, f32[1024]{0:T(1024)S(1)} %bitcast.90, bf16[1024,1536]{1,0:T(8,128)(2,1)S(1)} %copy-done.13, bf16[2,192,512]{2,1,0:T(8,128)(2,1)S(1)} %get-tuple-element.22, ...), kind=kOutput, calls=%fused_computation.15 | convolution fusion | flops 1213857024 | bytes 6691840 | tf_op jit(solution)/shard_map/sty,iy->sti/dot_general | solution.py:426
  191.0 5.5 %all-to-all-done.2 = f32[16,16,256]{2,1,0:T(8,128)} async-done(((f32[16,16,256]{2,1,0:T(8,128)}), f32[16,16,256]{2,1,0:T(8,128)}, u32[]{:S(2)}, u32[]{:S(2)}) %all-to-all-start.2) | async-done | bytes 262176 | tf_op jit(solution)/shard_map/all_to_all | solution.py:371
  198.1 10.8 %all-to-all-start.3 = ((f32[16,16,256]{2,1,0:T(8,128)}), f32[16,16,256]{2,1,0:T(8,128)S(1)}, u32[]{:S(2)}, u32[]{:S(2)}) async-start(f32[16,16,256]{2,1,0:T(8,128)} %broadcast_in_dim.24), calls=%async_computation.3 | async-start | bytes 524288 | tf_op jit(solution)/shard_map/all_to_all | solution.py:240
  208.9 2.6 %fusion.12 = bf16[2,192,1024]{2,1,0:T(8,128)(2,1)} fusion(bf16[2,192,1024]{2,1,0:T(8,128)(2,1)S(1)} %copy-done.8, f32[2,192,1024]{2,1,0:T(8,128)} %get-tuple-element.39, f32[2,192]{1,0:T(2,128)S(1)} %get-tuple-element.40, f32[2,192]{1,0:T(2,128)S(1)} %get-tuple-element.38, f32[2,192]{1,0:T(2,128)S(1)} %get-tuple-element.37), kind=kLoop, calls=%fused_computation.18 | loop fusion | flops 2359296 | bytes 3150336 | tf_op jit(solution)/shard_map/convert_element_type | solution.py:431
  211.6 5.8 %all-to-all-done.3 = f32[16,16,256]{2,1,0:T(8,128)S(1)} async-done(((f32[16,16,256]{2,1,0:T(8,128)}), f32[16,16,256]{2,1,0:T(8,128)S(1)}, u32[]{:S(2)}, u32[]{:S(2)}) %all-to-all-start.3) | async-done | bytes 262176 | tf_op jit(solution)/shard_map/all_to_all | solution.py:240
  (71 shorter events, 15.0 us)
Async XLA Ops:
  0.6 108.8 %copy-start = (bf16[2,192,1024]{2,1,0:T(8,128)(2,1)S(1)}, bf16[2,192,1024]{2,1,0:T(8,128)(2,1)}, u32[]{:S(2)}) copy-start(bf16[2,192,1024]{2,1,0:T(8,128)(2,1)} %param.17) | copy-start | bytes 2359300
  3.3 14.1 %collective-permute-start.3 = (bf16[8,2176]{1,0:T(8,128)(2,1)}, bf16[8,2176]{1,0:T(8,128)(2,1)S(1)}, u32[]{:S(2)}, u32[]{:S(2)}) collective-permute-start(bf16[8,2176]{1,0:T(8,128)(2,1)} %shard_map.113), channel_id=1, source_target_pairs={{0,2},{2,4},{4,6},{6,0},{1,3},{3,5},{5,7},{7,1},{8,10},{10,12},{12... | collective-permute-start | bytes 104456 | tf_op jit(solution)/shard_map/ppermute | solution.py:227
  12.4 11.4 %collective-permute-start.4 = (bf16[8,2176]{1,0:T(8,128)(2,1)}, bf16[8,2176]{1,0:T(8,128)(2,1)S(1)}, u32[]{:S(2)}, u32[]{:S(2)}) collective-permute-start(bf16[8,2176]{1,0:T(8,128)(2,1)} %shard_map.113), channel_id=1, source_target_pairs={{2,0},{4,2},{6,4},{0,6},{3,1},{5,3},{7,5},{1,7},{10,8},{12,10},{14... | collective-permute-start | bytes 104456 | tf_op jit(solution)/shard_map/ppermute | solution.py:228
  17.3 9.7 %collective-permute-start.5 = (bf16[8,2176]{1,0:T(8,128)(2,1)S(1)}, bf16[8,2176]{1,0:T(8,128)(2,1)S(1)}, u32[]{:S(2)}, u32[]{:S(2)}) collective-permute-start(bf16[8,2176]{1,0:T(8,128)(2,1)S(1)} %collective-permute-done.3), channel_id=1, source_target_pairs={{0,2},{2,4},{4,6},{6,0},{1,3},{3,5},{5,7},{7,1},{8,10},{10,12},{12... | collective-permute-start | bytes 104456 | tf_op jit(solution)/shard_map/ppermute | solution.py:229
  27.1 31.0 %copy-start.6 = (bf16[2,192,1024]{2,1,0:T(8,128)(2,1)S(1)}, bf16[2,192,1024]{2,1,0:T(8,128)(2,1)}, u32[]{:S(2)}) copy-start(bf16[2,192,1024]{2,1,0:T(8,128)(2,1)} %param.9) | copy-start | bytes 2359300
  27.2 40.7 %copy-start.11 = (s32[3,9]{1,0:T(4,128)S(1)}, s32[3,9]{1,0:T(4,128)}, u32[]{:S(2)}) copy-start(s32[3,9]{1,0:T(4,128)} %param.16) | copy-start | bytes 328
  27.3 40.8 %copy-start.12 = (s32[3,9]{1,0:T(4,128)S(1)}, s32[3,9]{1,0:T(4,128)}, u32[]{:S(2)}) copy-start(s32[3,9]{1,0:T(4,128)} %param.15) | copy-start | bytes 328
  56.2 28.5 %copy-start.5 = (bf16[16,3,8,2176]{3,2,1,0:T(8,128)(2,1)}, bf16[16,3,8,2176]{3,2,1,0:T(8,128)(2,1)S(1)}, u32[]{:S(2)}) copy-start(bf16[16,3,8,2176]{3,2,1,0:T(8,128)(2,1)S(1)} %all_to_all.20.far_ref) | copy-start | bytes 5013508
  56.2 28.5 %collective-permute-start.6 = (bf16[16,3,8,2176]{3,2,1,0:T(8,128)(2,1)S(1)}, bf16[16,3,8,2176]{3,2,1,0:T(8,128)(2,1)}, u32[]{:S(2)}, u32[]{:S(2)}) collective-permute-start(bf16[16,3,8,2176]{3,2,1,0:T(8,128)(2,1)S(1)} %all_to_all.20.far_ref), channel_id=1, source_target_pairs={{0,1},{1,0},{2,3},{3,2},{4,5},{5,4},{6,7},{7,6},{8,9},{9,8},{10,11... | collective-permute-start | bytes 5013512 | tf_op jit(solution)/shard_map/ppermute | solution.py:234
  58.1 21.9 %collective-permute-start.1 = (bf16[2,192,1024]{2,1,0:T(8,128)(2,1)S(1)}, bf16[2,192,1024]{2,1,0:T(8,128)(2,1)}, u32[]{:S(2)}, u32[]{:S(2)}) collective-permute-start(bf16[2,192,1024]{2,1,0:T(8,128)(2,1)S(1)} %copy-done.6), channel_id=1, source_target_pairs={{8,0},{16,8},{24,16},{32,24},{40,32},{48,40},{56,48},{64,56},{72,6... | collective-permute-start | bytes 2359304 | tf_op jit(solution)/shard_map/ppermute | solution.py:388
  61.1 21.7 %collective-permute-start = (bf16[2,192,1024]{2,1,0:T(8,128)(2,1)S(1)}, bf16[2,192,1024]{2,1,0:T(8,128)(2,1)}, u32[]{:S(2)}, u32[]{:S(2)}) collective-permute-start(bf16[2,192,1024]{2,1,0:T(8,128)(2,1)S(1)} %copy-done.6), channel_id=1, source_target_pairs={{0,8},{8,16},{16,24},{24,32},{32,40},{40,48},{48,56},{56,64},{64,7... | collective-permute-start | bytes 2359304 | tf_op jit(solution)/shard_map/ppermute | solution.py:387
  65.9 18.7 %collective-permute-start.2 = (bf16[128,2176]{1,0:T(8,128)(2,1)}, bf16[128,2176]{1,0:T(8,128)(2,1)}, u32[]{:S(2)}, u32[]{:S(2)}) collective-permute-start(bf16[128,2176]{1,0:T(8,128)(2,1)} %shard_map.112.mine_ref), channel_id=1, source_target_pairs={{0,1},{1,0},{2,3},{3,2},{4,5},{5,4},{6,7},{7,6},{8,9},{9,8},{10,11... | collective-permute-start | bytes 1671176 | tf_op jit(solution)/shard_map/ppermute | solution.py:234
  92.9 8.0 %copy-start.9 = (f32[8,1,128]{2,1,0:T(1,128)}, f32[8,1,128]{2,1,0:T(1,128)S(1)}, u32[]{:S(2)}) copy-start(f32[8,1,128]{2,1,0:T(1,128)S(1)} %slice_convert_fusion) | copy-start | bytes 12292
  109.4 0.9 copy-start.1
  110.3 4.6 %collective-permute-start.11 = (f32[4,64,1024]{2,1,0:T(8,128)S(1)}, f32[4,64,1024]{2,1,0:T(8,128)S(1)}, u32[]{:S(2)}, u32[]{:S(2)}) collective-permute-start(f32[4,64,1024]{2,1,0:T(8,128)S(1)} %select_bitcast_fusion), channel_id=1, source_target_pairs={{0,1},{1,0},{2,3},{3,2},{4,5},{5,4},{6,7},{7,6},{8,9},{9,8},{10,11... | collective-permute-start | bytes 3145736 | tf_op jit(solution)/shard_map/ppermute | solution.py:234
  116.3 43.7 %all-to-all-start.1 = ((bf16[16,4,16,256]{3,2,1,0:T(8,128)(2,1)}), bf16[16,4,16,256]{3,2,1,0:T(8,128)(2,1)}, u32[]{:S(2)}, u32[]{:S(2)}) async-start(bf16[16,4,16,256]{3,2,1,0:T(8,128)(2,1)} %bitcast.32), calls=%async_computation.1 | async-start | bytes 1048576 | tf_op jit(solution)/shard_map/all_to_all | solution.py:368
  137.5 43.1 %collective-permute-start.8 = (bf16[2,192,512]{2,1,0:T(8,128)(2,1)S(1)}, bf16[2,192,512]{2,1,0:T(8,128)(2,1)S(1)}, u32[]{:S(2)}, u32[]{:S(2)}) collective-permute-start(bf16[2,192,512]{2,1,0:T(8,128)(2,1)S(1)} %fusion.17.g_ref), channel_id=1, source_target_pairs={{8,0},{16,8},{24,16},{32,24},{40,32},{48,40},{56,48},{64,56},{72,6... | collective-permute-start | bytes 1179656 | tf_op jit(solution)/shard_map/ppermute | solution.py:414
  140.4 40.1 %collective-permute-start.7 = (bf16[2,192,512]{2,1,0:T(8,128)(2,1)S(1)}, bf16[2,192,512]{2,1,0:T(8,128)(2,1)}, u32[]{:S(2)}, u32[]{:S(2)}) collective-permute-start(bf16[2,192,512]{2,1,0:T(8,128)(2,1)S(1)} %fusion.17.g_ref), channel_id=1, source_target_pairs={{0,8},{8,16},{16,24},{24,32},{32,40},{40,48},{48,56},{56,64},{64,7... | collective-permute-start | bytes 1179656 | tf_op jit(solution)/shard_map/ppermute | solution.py:414
  143.3 0.7 copy-start.2
  153.4 0.8 copy-start.3
  154.2 26.4 %collective-permute-start.10 = (f32[2,4,8,384]{3,2,1,0:T(8,128)}, f32[2,4,8,384]{3,2,1,0:T(8,128)}, u32[]{:S(2)}, u32[]{:S(2)}) collective-permute-start(f32[2,4,8,384]{3,2,1,0:T(8,128)} %get-tuple-element.19), channel_id=1, source_target_pairs={{8,0},{16,8},{24,16},{32,24},{40,32},{48,40},{56,48},{64,56},{72,6... | collective-permute-start | bytes 294920 | tf_op jit(solution)/shard_map/ppermute | solution.py:420
  157.9 22.7 %collective-permute-start.9 = (f32[2,4,8,384]{3,2,1,0:T(8,128)}, f32[2,4,8,384]{3,2,1,0:T(8,128)}, u32[]{:S(2)}, u32[]{:S(2)}) collective-permute-start(f32[2,4,8,384]{3,2,1,0:T(8,128)} %get-tuple-element.19), channel_id=1, source_target_pairs={{0,8},{8,16},{16,24},{24,32},{32,40},{40,48},{48,56},{56,64},{64,7... | collective-permute-start | bytes 294920 | tf_op jit(solution)/shard_map/ppermute | solution.py:420
  161.9 34.6 %all-to-all-start.2 = ((f32[16,16,256]{2,1,0:T(8,128)}), f32[16,16,256]{2,1,0:T(8,128)}, u32[]{:S(2)}, u32[]{:S(2)}) async-start(f32[16,16,256]{2,1,0:T(8,128)} %bitcast.80), calls=%async_computation.2 | async-start | bytes 524288 | tf_op jit(solution)/shard_map/all_to_all | solution.py:371
  180.6 7.7 %copy-start.4 = (bf16[2,192,512]{2,1,0:T(8,128)(2,1)S(1)}, bf16[2,192,512]{2,1,0:T(8,128)(2,1)}, u32[]{:S(2)}) copy-start(bf16[2,192,512]{2,1,0:T(8,128)(2,1)} %copy-done.3) | copy-start | bytes 1179652
  180.6 7.7 %copy-start.7 = (bf16[2,192,1024]{2,1,0:T(8,128)(2,1)S(1)}, bf16[2,192,1024]{2,1,0:T(8,128)(2,1)}, u32[]{:S(2)}) copy-start(bf16[2,192,1024]{2,1,0:T(8,128)(2,1)} %param.9) | copy-start | bytes 2359300
  180.6 7.7 %copy-start.10 = (f32[8,1,128]{2,1,0:T(1,128)S(1)}, f32[8,1,128]{2,1,0:T(1,128)}, u32[]{:S(2)}) copy-start(f32[8,1,128]{2,1,0:T(1,128)} %copy-done.9) | copy-start | bytes 12292
  180.6 7.7 %copy-start.13 = (bf16[1024,1536]{1,0:T(8,128)(2,1)S(1)}, bf16[1024,1536]{1,0:T(8,128)(2,1)}, u32[]{:S(2)}) copy-start(bf16[1024,1536]{1,0:T(8,128)(2,1)} %get-tuple-element.14) | copy-start | bytes 9437188
  188.3 20.6 %copy-start.8 = (bf16[2,192,1024]{2,1,0:T(8,128)(2,1)S(1)}, bf16[2,192,1024]{2,1,0:T(8,128)(2,1)}, u32[]{:S(2)}) copy-start(bf16[2,192,1024]{2,1,0:T(8,128)(2,1)} %param.9) | copy-start | bytes 2359300
  198.1 19.3 %all-to-all-start.3 = ((f32[16,16,256]{2,1,0:T(8,128)}), f32[16,16,256]{2,1,0:T(8,128)S(1)}, u32[]{:S(2)}, u32[]{:S(2)}) async-start(f32[16,16,256]{2,1,0:T(8,128)} %broadcast_in_dim.24), calls=%async_computation.3 | async-start | bytes 524288 | tf_op jit(solution)/shard_map/all_to_all | solution.py:240

commit v5 on v4

--- a/solution.py
+++ b/solution.py
@@ -185,23 +185,33 @@
 
 def slice_kernel(place_ref, q_ref, k_ref, v_ref, out_ref, gain_ref, part_ref):
     rows, width = q_ref.shape
+    half = width // 2
     columns = out_ref.shape[1]
-    folds = out_ref.shape[0] // rows
-    for i, ref in enumerate((q_ref, k_ref, v_ref)):
-        part_ref[:, i * width : (i + 1) * width] = ref[...]
-    for i in range(folds):
-        begin = 3 * width + i * columns
-        part_ref[:, begin : begin + columns] = out_ref[i * rows : (i + 1) * rows, :]
-    begin = 3 * width + folds * columns
-    part_ref[:, begin:] = jnp.broadcast_to(gain_ref[...], (rows, gain_ref.shape[1]))
-
-
-def own_slices(norm_gain, w_query, w_key, w_value, w_out, rows, out_rows, out_columns):
+
+    @pl.when(place_ref[1] == 0)
+    def _():
+        part_ref[:, :width] = q_ref[...]
+        part_ref[:, width : width + half] = k_ref[:, :half]
+
+    @pl.when(place_ref[1] != 0)
+    def _():
+        part_ref[:, :half] = k_ref[:, half:]
+        part_ref[:, half : half + width] = v_ref[...]
+
+    begin = width + half
+    part_ref[:, begin : begin + columns] = out_ref[...]
+    part_ref[:, begin + columns :] = jnp.broadcast_to(gain_ref[...], (rows, gain_ref.shape[1]))
+
+
+def own_slices(norm_gain, w_query, w_key, w_value, w_out):
+    nx, ny = (lax.axis_size(X), lax.axis_size(Y))
+    xi, yi = (lax.axis_index(X), lax.axis_index(Y))
     depth, width = w_query.shape
-    xi, yi = (lax.axis_index(X), lax.axis_index(Y))
-    place = jnp.stack([xi * lax.axis_size(Y) + yi, xi, yi])
+    rows, columns = (w_out.shape[0] // nx, w_out.shape[1] // ny)
+    number = xi * ny + yi
+    place = jnp.stack([number // 2, number % 2, xi, yi])
     band = pl.BlockSpec((rows, width), lambda i, place: (place[0], 0))
-    total = 3 * width + out_rows // rows * out_columns + depth
+    total = width + width // 2 + columns + depth
     return pl.pallas_call(
         slice_kernel,
         grid_spec=pltpu.PrefetchScalarGridSpec(
@@ -211,7 +221,7 @@
                 band,
                 band,
                 band,
-                pl.BlockSpec((out_rows, out_columns), lambda i, place: (place[1], place[2])),
+                pl.BlockSpec((rows, columns), lambda i, place: (place[2], place[3])),
                 pl.BlockSpec((1, depth), lambda i, place: (0, 0)),
             ],
             out_specs=pl.BlockSpec((rows, total), lambda i, place: (0, 0)),
@@ -259,7 +269,7 @@
     half = out_ref.shape[1] // 2
     depth, rows = (out_ref.shape[0], gain_ref.shape[1])
     count = far_ref.shape[0]
-    columns = (far_ref.shape[3] - width - gain_ref.shape[2]) // 2
+    columns = far_ref.shape[3] - width // 2 - gain_ref.shape[2]
     across = out_ref.shape[1] // columns
 
     def near(ref):
@@ -270,13 +280,13 @@
 
     def distant(ref):
         for s in range(count):
-            joint_ref[s * rows : (s + 1) * rows, :] = ref[s, 0, :, :width]
-            top, left = (s // across * 2 * rows, s % across * columns)
-            for fold in range(2):
-                begin = width + fold * columns
-                place = slice(top + fold * rows, top + (fold + 1) * rows)
-                out_ref[place, left : left + columns] = ref[s, 0, :, begin : begin + columns]
-        gain_ref[0] = ref[0, 0, :, width + 2 * columns :]
+            top, left = (s // 2 * rows, s % 2 * (width // 2))
+            joint_ref[top : top + rows, left : left + width // 2] = ref[s, 0, :, : width // 2]
+            top, left = (s // across * rows, s % across * columns)
+            out_ref[top : top + rows, left : left + columns] = ref[
+                s, 0, :, width // 2 : width // 2 + columns
+            ]
+        gain_ref[0] = ref[0, 0, :, width // 2 + columns :]
 
     pl.when(step == 0)(lambda: near(mine_ref))
     pl.when(step == 1)(lambda: near(theirs_ref))
@@ -294,7 +304,7 @@
     count, _, rows, total = far.shape
     depth = mine.shape[0]
     out_depth, model_width = out_shape
-    gain_width = total - width - model_width // 2
+    gain_width = mine.shape[1] - width - model_width // 2
     whole = pl.BlockSpec(mine.shape, lambda i, place: (0, 0))
 
     def distant(first):
@@ -326,14 +336,9 @@
 
 
 def gathered_weights(norm_gain, w_query, w_key, w_value, w_out):
-    nx, ny = (lax.axis_size(X), lax.axis_size(Y))
     depth, hidden_width = w_query.shape
-    out_depth, model_width = w_out.shape
-    rows = depth // (nx * ny)
-    out_rows, out_columns = (out_depth // nx, model_width // ny)
-    part = own_slices(norm_gain, w_query, w_key, w_value, w_out, rows, out_rows, out_columns)
-    part = column_gather(part)
-    half = model_width // 2
+    half = w_out.shape[1] // 2
+    part = column_gather(own_slices(norm_gain, w_query, w_key, w_value, w_out))
     far = plane_gather(part)
     mine = pl.pallas_call(
         pack_kernel,

time: 220 us -> 221 us (level)
  no operation moved by 1% of the time
where the time goes in v5:
time: 221 us; the launch traced here: 219 us
  starting transfers between devices  89.5 us (40%)
  Pallas kernels  37 us (17%)
  waiting for transfers between devices  31 us (14%)
  blocking collectives  29.8 us (13%)
  matrix products  15.9 us (7%)
  other arithmetic  10.3 us (5%)
  local copies, waits for them, and re-layouts  4.42 us (2%)
    all_to_all x1, blocking collectives, plane_gather(): return lax.all_to_all(copies, PLANE, 0, 0, tiled=True)  29.8 us
    all_to_all x1, starting transfers between devices, summed_gradient(): half = lax.all_to_all(half, (Y, X), 0, 0, tiled=True)  19.3 us
    all_to_all x1, starting transfers between devices, summed_gradient(): part = lax.all_to_all(part, COLUMN, 0, 0, tiled=True)  16 us
    ppermute x1, waiting for transfers between devices, shards(): above = lax.ppermute(inputs, DOMAIN, down)  10.8 us
    all_to_all x1, starting transfers between devices, plane_gather(): return lax.all_to_all(copies, PLANE, 0, 0, tiled=True)  10.8 us
    pallas_call x1, Pallas kernels, query_gradient(): plan.call(query_kernel, 4, given, *outs)  9.34 us
    ppermute x1, starting transfers between devices, column_gather(): first = lax.ppermute(part, ZH, up)  9.08 us
    pallas_call x1, Pallas kernels, forward_attention(): return plan.call(forward_kernel, 2, given, *outs)(bias, joint, joint, joint)  8.44 us
  transfers between devices with their start and end apart: 15, of which 7 were waited for; matrix products, arithmetic and copies ran while one was open for 7% of the time, Pallas kernels for 9%

profile of v5, /device:TPU:32, one launch (start us, length us, event | category | flops | bytes accessed | tf_op | source)
XLA Modules:
  0.0 219.2 jit_solution(17866315597333102018)
XLA Ops:
  1.3 2.1 shard_map.113
  3.4 9.1 %collective-permute-start.3 = (bf16[16,1152]{1,0:T(8,128)(2,1)}, bf16[16,1152]{1,0:T(8,128)(2,1)S(1)}, u32[]{:S(2)}, u32[]{:S(2)}) collective-permute-start(bf16[16,1152]{1,0:T(8,128)(2,1)} %shard_map.113), channel_id=1, source_target_pairs={{0,2},{2,4},{4,6},{6,0},{1,3},{3,5},{5,7},{7,1},{8,10},{10,12},{12... | collective-permute-start | bytes 110600 | tf_op jit(solution)/shard_map/ppermute | solution.py:237
  12.5 4.7 %collective-permute-start.4 = (bf16[16,1152]{1,0:T(8,128)(2,1)}, bf16[16,1152]{1,0:T(8,128)(2,1)S(1)}, u32[]{:S(2)}, u32[]{:S(2)}) collective-permute-start(bf16[16,1152]{1,0:T(8,128)(2,1)} %shard_map.113), channel_id=1, source_target_pairs={{2,0},{4,2},{6,4},{0,6},{3,1},{5,3},{7,5},{1,7},{10,8},{12,10},{14... | collective-permute-start | bytes 110600 | tf_op jit(solution)/shard_map/ppermute | solution.py:238
  17.5 6.5 %collective-permute-start.5 = (bf16[16,1152]{1,0:T(8,128)(2,1)S(1)}, bf16[16,1152]{1,0:T(8,128)(2,1)S(1)}, u32[]{:S(2)}, u32[]{:S(2)}) collective-permute-start(bf16[16,1152]{1,0:T(8,128)(2,1)S(1)} %collective-permute-done.3), channel_id=1, source_target_pairs={{0,2},{2,4},{4,6},{6,0},{1,3},{3,5},{5,7},{7,1},{8,10},{10,12},{12... | collective-permute-start | bytes 110600 | tf_op jit(solution)/shard_map/ppermute | solution.py:239
  24.0 3.2 %collective-permute-done.5 = bf16[16,1152]{1,0:T(8,128)(2,1)S(1)} collective-permute-done((bf16[16,1152]{1,0:T(8,128)(2,1)S(1)}, bf16[16,1152]{1,0:T(8,128)(2,1)S(1)}, u32[]{:S(2)}, u32[]{:S(2)}) %collective-permute-start.5) | collective-permute-done | bytes 36896 | tf_op jit(solution)/shard_map/ppermute | solution.py:239
  27.5 29.8 %all_to_all.20.far_ref = bf16[16,3,16,1152]{3,2,1,0:T(8,128)(2,1)S(1)} all-to-all(bf16[16,3,16,1152]{3,2,1,0:T(8,128)(2,1)S(1)} %broadcast_in_dim.22), channel_id=1, replica_groups=mesh['x'=4,'y'=4,'zl'=4,'zh'=4,'core'=2] {'x','y'}, dimensions={0} | all-to-all | bytes 3538944 | tf_op jit(solution)/shard_map/all_to_all | solution.py:250
  57.3 1.9 collective-permute-start.6
  59.2 2.9 %collective-permute-start.1 = (bf16[2,192,1024]{2,1,0:T(8,128)(2,1)S(1)}, bf16[2,192,1024]{2,1,0:T(8,128)(2,1)}, u32[]{:S(2)}, u32[]{:S(2)}) collective-permute-start(bf16[2,192,1024]{2,1,0:T(8,128)(2,1)S(1)} %copy-done.6), channel_id=1, source_target_pairs={{8,0},{16,8},{24,16},{32,24},{40,32},{48,40},{56,48},{64,56},{72,6... | collective-permute-start | bytes 2359304 | tf_op jit(solution)/shard_map/ppermute | solution.py:393
  62.2 2.9 %collective-permute-start = (bf16[2,192,1024]{2,1,0:T(8,128)(2,1)S(1)}, bf16[2,192,1024]{2,1,0:T(8,128)(2,1)}, u32[]{:S(2)}, u32[]{:S(2)}) collective-permute-start(bf16[2,192,1024]{2,1,0:T(8,128)(2,1)S(1)} %copy-done.6), channel_id=1, source_target_pairs={{0,8},{8,16},{16,24},{24,32},{32,40},{40,48},{48,56},{56,64},{64,7... | collective-permute-start | bytes 2359304 | tf_op jit(solution)/shard_map/ppermute | solution.py:392
  65.1 1.9 shard_map.112.mine_ref
  67.0 1.9 collective-permute-start.2
  70.4 10.8 %collective-permute-done.1 = bf16[2,192,1024]{2,1,0:T(8,128)(2,1)} collective-permute-done((bf16[2,192,1024]{2,1,0:T(8,128)(2,1)S(1)}, bf16[2,192,1024]{2,1,0:T(8,128)(2,1)}, u32[]{:S(2)}, u32[]{:S(2)}) %collective-permute-start.1) | collective-permute-done | bytes 786464 | tf_op jit(solution)/shard_map/ppermute | solution.py:393
  81.2 2.6 %collective-permute-done = bf16[2,192,1024]{2,1,0:T(8,128)(2,1)} collective-permute-done((bf16[2,192,1024]{2,1,0:T(8,128)(2,1)S(1)}, bf16[2,192,1024]{2,1,0:T(8,128)(2,1)}, u32[]{:S(2)}, u32[]{:S(2)}) %collective-permute-start) | collective-permute-done | bytes 786464 | tf_op jit(solution)/shard_map/ppermute | solution.py:392
  85.8 7.5 %shard_map.114 = (bf16[1024,1536]{1,0:T(8,128)(2,1)}, bf16[512,1024]{1,0:T(8,128)(2,1)}, bf16[8,16,128]{2,1,0:T(8,128)(2,1)}) custom-call(s32[8]{0:T(128)} %stack.77.place_ref, bf16[128,2176]{1,0:T(8,128)(2,1)} %shard_map.112.mine_ref, bf16[128,2176]{1,0:T(8,128)(2,1)} %collective-permute-done.2.theirs_ref, bf16[16,3,16,1152]{3,2,1,0:T(8,128)(2,1)} %copy-done.5, ...), custom_call_target="tpu_custom_call" | custom-call | bytes 8388608 | tf_op jit(solution)/shard_map/pallas_call | solution.py:317
  94.1 8.0 %convolution_convert_fusion.q_ref.k_ref.v_ref.low_q_ref.high_q_ref = bf16[2,576,1536]{2,1,0:T(8,128)(2,1)} fusion(bf16[1024,1536]{1,0:T(8,128)(2,1)} %get-tuple-element.14, f32[1024]{0:T(1024)S(1)} %bitcast.90, f32[2,576]{1,0:T(2,128)S(1)} %add_rsqrt_fusion, bf16[2,192,1024]{2,1,0:T(8,128)(2,1)} %collective-permute-done.1, ...), kind=kOutput, calls=%fused_computation.5 | convolution fusion | flops 3636264960 | bytes 9052672 | tf_op jit(solution)/shard_map/sti,iy->sty/dot_general | solution.py:404
  102.1 8.4 %shard_map.115 = (bf16[2,192,512]{2,1,0:T(8,128)(2,1)S(1)}, f32[2,4,1,384]{3,2,1,0:T(1,128)S(1)}) custom-call(f32[9,1,384]{2,1,0:T(1,128)S(1)} %tile.11.bias_ref, bf16[2,576,1536]{2,1,0:T(8,128)(2,1)} %convolution_convert_fusion.q_ref.k_ref.v_ref.low_q_ref.high_q_ref, bf16[2,576,1536]{2,1,0:T(8,128)(2,1)} %convolution_convert_fusion.q_ref.k_ref.v_ref.low_q_ref.high_q_ref, ...), custom_call_target="tpu_custom_call" | custom-call | flops 452984832 | bytes 1179648 | tf_op jit(solution)/shard_map/pallas_call | solution.py:161
  111.5 1.9 collective-permute-start.11
  113.4 2.6 %collective-permute-done.11 = f32[4,64,1024]{2,1,0:T(8,128)S(1)} collective-permute-done((f32[4,64,1024]{2,1,0:T(8,128)S(1)}, f32[4,64,1024]{2,1,0:T(8,128)S(1)}, u32[]{:S(2)}, u32[]{:S(2)}) %collective-permute-start.11) | collective-permute-done | bytes 1048608 | tf_op jit(solution)/shard_map/ppermute | solution.py:244
  117.4 19.3 %all-to-all-start.1 = ((bf16[16,4,16,256]{3,2,1,0:T(8,128)(2,1)}), bf16[16,4,16,256]{3,2,1,0:T(8,128)(2,1)}, u32[]{:S(2)}, u32[]{:S(2)}) async-start(bf16[16,4,16,256]{3,2,1,0:T(8,128)(2,1)} %bitcast.33), calls=%async_computation.1 | async-start | bytes 1048576 | tf_op jit(solution)/shard_map/all_to_all | solution.py:373
  138.5 3.0 %collective-permute-start.8 = (bf16[2,192,512]{2,1,0:T(8,128)(2,1)S(1)}, bf16[2,192,512]{2,1,0:T(8,128)(2,1)S(1)}, u32[]{:S(2)}, u32[]{:S(2)}) collective-permute-start(bf16[2,192,512]{2,1,0:T(8,128)(2,1)S(1)} %fusion.17.g_ref), channel_id=1, source_target_pairs={{8,0},{16,8},{24,16},{32,24},{40,32},{48,40},{56,48},{64,56},{72,6... | collective-permute-start | bytes 1179656 | tf_op jit(solution)/shard_map/ppermute | solution.py:419
  141.5 2.9 %collective-permute-start.7 = (bf16[2,192,512]{2,1,0:T(8,128)(2,1)S(1)}, bf16[2,192,512]{2,1,0:T(8,128)(2,1)}, u32[]{:S(2)}, u32[]{:S(2)}) collective-permute-start(bf16[2,192,512]{2,1,0:T(8,128)(2,1)S(1)} %fusion.17.g_ref), channel_id=1, source_target_pairs={{0,8},{8,16},{16,24},{24,32},{32,40},{40,48},{48,56},{56,64},{64,7... | collective-permute-start | bytes 1179656 | tf_op jit(solution)/shard_map/ppermute | solution.py:419
  145.1 9.3 %shard_map.116 = (bf16[2,192,512]{2,1,0:T(8,128)(2,1)S(1)}, f32[2,2,192,512]{3,2,1,0:T(8,128)S(1)}, f32[2,4,8,384]{3,2,1,0:T(8,128)}) custom-call(f32[9,1,384]{2,1,0:T(1,128)S(1)} %tile.11.bias_ref, bf16[2,576,1536]{2,1,0:T(8,128)(2,1)} %convolution_convert_fusion.q_ref.k_ref.v_ref.low_q_ref.high_q_ref, ...), custom_call_target="tpu_custom_call" | custom-call | flops 905969664 | bytes 2359296 | tf_op jit(solution)/shard_map/pallas_call | solution.py:174
  155.2 3.8 %collective-permute-start.10 = (f32[2,4,8,384]{3,2,1,0:T(8,128)}, f32[2,4,8,384]{3,2,1,0:T(8,128)}, u32[]{:S(2)}, u32[]{:S(2)}) collective-permute-start(f32[2,4,8,384]{3,2,1,0:T(8,128)} %get-tuple-element.19), channel_id=1, source_target_pairs={{8,0},{16,8},{24,16},{32,24},{40,32},{48,40},{56,48},{64,56},{72,6... | collective-permute-start | bytes 294920 | tf_op jit(solution)/shard_map/ppermute | solution.py:425
  159.0 2.1 collective-permute-start.9
  162.9 16.0 %all-to-all-start.2 = ((f32[16,16,256]{2,1,0:T(8,128)}), f32[16,16,256]{2,1,0:T(8,128)}, u32[]{:S(2)}, u32[]{:S(2)}) async-start(f32[16,16,256]{2,1,0:T(8,128)} %bitcast.81), calls=%async_computation.2 | async-start | bytes 524288 | tf_op jit(solution)/shard_map/all_to_all | solution.py:376
  178.9 2.7 %convolution_convert_fusion.1 = bf16[2,192,1024]{2,1,0:T(8,128)(2,1)} fusion(bf16[2,192,512]{2,1,0:T(8,128)(2,1)S(1)} %get-tuple-element.15, bf16[512,1024]{1,0:T(8,128)(2,1)} %get-tuple-element.16), kind=kOutput, calls=%fused_computation.21 | convolution fusion | flops 403046400 | bytes 2228224 | tf_op jit(solution)/shard_map/sty,yb->stb/dot_general | solution.py:427
  181.6 7.6 %shard_map.117 = (bf16[2,192,512]{2,1,0:T(8,128)(2,1)S(1)}, bf16[2,192,512]{2,1,0:T(8,128)(2,1)S(1)}) custom-call(bf16[2,576,1536]{2,1,0:T(8,128)(2,1)} %convolution_convert_fusion.q_ref.k_ref.v_ref.low_q_ref.high_q_ref, bf16[2,576,1536]{2,1,0:T(8,128)(2,1)} %convolution_convert_fusion.q_ref.k_ref.v_ref.low_q_ref.high_q_ref, ...), custom_call_target="tpu_custom_call" | custom-call | flops 679477248 | bytes 1769472 | tf_op jit(solution)/shard_map/pallas_call | solution.py:183
  189.3 2.6 %fusion.9 = (f32[2,192]{1,0:T(2,128)S(1)}, f32[2,192]{1,0:T(2,128)S(1)}, f32[2,192,1024]{2,1,0:T(8,128)}) fusion(bf16[2,192,1024]{2,1,0:T(8,128)(2,1)S(1)} %copy-done.7, f32[1024]{0:T(1024)S(1)} %bitcast.91, bf16[1024,1536]{1,0:T(8,128)(2,1)S(1)} %copy-done.13, bf16[2,192,512]{2,1,0:T(8,128)(2,1)S(1)} %get-tuple-element.22, ...), kind=kOutput, calls=%fused_computation.15 | convolution fusion | flops 1213857024 | bytes 6691840 | tf_op jit(solution)/shard_map/sty,iy->sti/dot_general | solution.py:431
  192.0 5.5 %all-to-all-done.2 = f32[16,16,256]{2,1,0:T(8,128)} async-done(((f32[16,16,256]{2,1,0:T(8,128)}), f32[16,16,256]{2,1,0:T(8,128)}, u32[]{:S(2)}, u32[]{:S(2)}) %all-to-all-start.2) | async-done | bytes 262176 | tf_op jit(solution)/shard_map/all_to_all | solution.py:376
  199.2 10.8 %all-to-all-start.3 = ((f32[16,16,256]{2,1,0:T(8,128)}), f32[16,16,256]{2,1,0:T(8,128)S(1)}, u32[]{:S(2)}, u32[]{:S(2)}) async-start(f32[16,16,256]{2,1,0:T(8,128)} %broadcast_in_dim.24), calls=%async_computation.3 | async-start | bytes 524288 | tf_op jit(solution)/shard_map/all_to_all | solution.py:250
  210.0 2.6 %fusion.12 = bf16[2,192,1024]{2,1,0:T(8,128)(2,1)} fusion(bf16[2,192,1024]{2,1,0:T(8,128)(2,1)S(1)} %copy-done.8, f32[2,192,1024]{2,1,0:T(8,128)} %get-tuple-element.39, f32[2,192]{1,0:T(2,128)S(1)} %get-tuple-element.40, f32[2,192]{1,0:T(2,128)S(1)} %get-tuple-element.38, f32[2,192]{1,0:T(2,128)S(1)} %get-tuple-element.37), kind=kLoop, calls=%fused_computation.18 | loop fusion | flops 2359296 | bytes 3150336 | tf_op jit(solution)/shard_map/convert_element_type | solution.py:436
  212.6 5.8 %all-to-all-done.3 = f32[16,16,256]{2,1,0:T(8,128)S(1)} async-done(((f32[16,16,256]{2,1,0:T(8,128)}), f32[16,16,256]{2,1,0:T(8,128)S(1)}, u32[]{:S(2)}, u32[]{:S(2)}) %all-to-all-start.3) | async-done | bytes 262176 | tf_op jit(solution)/shard_map/all_to_all | solution.py:250
  (71 shorter events, 15.1 us)
Async XLA Ops:
  0.6 109.9 %copy-start = (bf16[2,192,1024]{2,1,0:T(8,128)(2,1)S(1)}, bf16[2,192,1024]{2,1,0:T(8,128)(2,1)}, u32[]{:S(2)}) copy-start(bf16[2,192,1024]{2,1,0:T(8,128)(2,1)} %param.17) | copy-start | bytes 2359300
  3.4 14.1 %collective-permute-start.3 = (bf16[16,1152]{1,0:T(8,128)(2,1)}, bf16[16,1152]{1,0:T(8,128)(2,1)S(1)}, u32[]{:S(2)}, u32[]{:S(2)}) collective-permute-start(bf16[16,1152]{1,0:T(8,128)(2,1)} %shard_map.113), channel_id=1, source_target_pairs={{0,2},{2,4},{4,6},{6,0},{1,3},{3,5},{5,7},{7,1},{8,10},{10,12},{12... | collective-permute-start | bytes 110600 | tf_op jit(solution)/shard_map/ppermute | solution.py:237
  12.5 11.6 %collective-permute-start.4 = (bf16[16,1152]{1,0:T(8,128)(2,1)}, bf16[16,1152]{1,0:T(8,128)(2,1)S(1)}, u32[]{:S(2)}, u32[]{:S(2)}) collective-permute-start(bf16[16,1152]{1,0:T(8,128)(2,1)} %shard_map.113), channel_id=1, source_target_pairs={{2,0},{4,2},{6,4},{0,6},{3,1},{5,3},{7,5},{1,7},{10,8},{12,10},{14... | collective-permute-start | bytes 110600 | tf_op jit(solution)/shard_map/ppermute | solution.py:238
  17.5 9.7 %collective-permute-start.5 = (bf16[16,1152]{1,0:T(8,128)(2,1)S(1)}, bf16[16,1152]{1,0:T(8,128)(2,1)S(1)}, u32[]{:S(2)}, u32[]{:S(2)}) collective-permute-start(bf16[16,1152]{1,0:T(8,128)(2,1)S(1)} %collective-permute-done.3), channel_id=1, source_target_pairs={{0,2},{2,4},{4,6},{6,0},{1,3},{3,5},{5,7},{7,1},{8,10},{10,12},{12... | collective-permute-start | bytes 110600 | tf_op jit(solution)/shard_map/ppermute | solution.py:239
  27.3 31.9 %copy-start.6 = (bf16[2,192,1024]{2,1,0:T(8,128)(2,1)S(1)}, bf16[2,192,1024]{2,1,0:T(8,128)(2,1)}, u32[]{:S(2)}) copy-start(bf16[2,192,1024]{2,1,0:T(8,128)(2,1)} %param.9) | copy-start | bytes 2359300
  27.4 41.6 %copy-start.11 = (s32[3,9]{1,0:T(4,128)S(1)}, s32[3,9]{1,0:T(4,128)}, u32[]{:S(2)}) copy-start(s32[3,9]{1,0:T(4,128)} %param.16) | copy-start | bytes 328
  27.4 41.7 %copy-start.12 = (s32[3,9]{1,0:T(4,128)S(1)}, s32[3,9]{1,0:T(4,128)}, u32[]{:S(2)}) copy-start(s32[3,9]{1,0:T(4,128)} %param.15) | copy-start | bytes 328
  57.3 28.5 %copy-start.5 = (bf16[16,3,16,1152]{3,2,1,0:T(8,128)(2,1)}, bf16[16,3,16,1152]{3,2,1,0:T(8,128)(2,1)S(1)}, u32[]{:S(2)}) copy-start(bf16[16,3,16,1152]{3,2,1,0:T(8,128)(2,1)S(1)} %all_to_all.20.far_ref) | copy-start | bytes 5308420
  57.3 28.5 %collective-permute-start.6 = (bf16[16,3,16,1152]{3,2,1,0:T(8,128)(2,1)S(1)}, bf16[16,3,16,1152]{3,2,1,0:T(8,128)(2,1)}, u32[]{:S(2)}, u32[]{:S(2)}) collective-permute-start(bf16[16,3,16,1152]{3,2,1,0:T(8,128)(2,1)S(1)} %all_to_all.20.far_ref), channel_id=1, source_target_pairs={{0,1},{1,0},{2,3},{3,2},{4,5},{5,4},{6,7},{7,6},{8,9},{9,8},{10,11... | collective-permute-start | bytes 5308424 | tf_op jit(solution)/shard_map/ppermute | solution.py:244
  59.2 21.9 %collective-permute-start.1 = (bf16[2,192,1024]{2,1,0:T(8,128)(2,1)S(1)}, bf16[2,192,1024]{2,1,0:T(8,128)(2,1)}, u32[]{:S(2)}, u32[]{:S(2)}) collective-permute-start(bf16[2,192,1024]{2,1,0:T(8,128)(2,1)S(1)} %copy-done.6), channel_id=1, source_target_pairs={{8,0},{16,8},{24,16},{32,24},{40,32},{48,40},{56,48},{64,56},{72,6... | collective-permute-start | bytes 2359304 | tf_op jit(solution)/shard_map/ppermute | solution.py:393
  62.2 21.7 %collective-permute-start = (bf16[2,192,1024]{2,1,0:T(8,128)(2,1)S(1)}, bf16[2,192,1024]{2,1,0:T(8,128)(2,1)}, u32[]{:S(2)}, u32[]{:S(2)}) collective-permute-start(bf16[2,192,1024]{2,1,0:T(8,128)(2,1)S(1)} %copy-done.6), channel_id=1, source_target_pairs={{0,8},{8,16},{16,24},{24,32},{32,40},{40,48},{48,56},{56,64},{64,7... | collective-permute-start | bytes 2359304 | tf_op jit(solution)/shard_map/ppermute | solution.py:392
  67.0 18.7 %collective-permute-start.2 = (bf16[128,2176]{1,0:T(8,128)(2,1)}, bf16[128,2176]{1,0:T(8,128)(2,1)}, u32[]{:S(2)}, u32[]{:S(2)}) collective-permute-start(bf16[128,2176]{1,0:T(8,128)(2,1)} %shard_map.112.mine_ref), channel_id=1, source_target_pairs={{0,1},{1,0},{2,3},{3,2},{4,5},{5,4},{6,7},{7,6},{8,9},{9,8},{10,11... | collective-permute-start | bytes 1671176 | tf_op jit(solution)/shard_map/ppermute | solution.py:244
  94.0 8.0 %copy-start.9 = (f32[8,1,128]{2,1,0:T(1,128)}, f32[8,1,128]{2,1,0:T(1,128)S(1)}, u32[]{:S(2)}) copy-start(f32[8,1,128]{2,1,0:T(1,128)S(1)} %slice_convert_fusion) | copy-start | bytes 12292
  110.5 0.9 copy-start.1
  111.5 4.6 %collective-permute-start.11 = (f32[4,64,1024]{2,1,0:T(8,128)S(1)}, f32[4,64,1024]{2,1,0:T(8,128)S(1)}, u32[]{:S(2)}, u32[]{:S(2)}) collective-permute-start(f32[4,64,1024]{2,1,0:T(8,128)S(1)} %select_bitcast_fusion), channel_id=1, source_target_pairs={{0,1},{1,0},{2,3},{3,2},{4,5},{5,4},{6,7},{7,6},{8,9},{9,8},{10,11... | collective-permute-start | bytes 3145736 | tf_op jit(solution)/shard_map/ppermute | solution.py:244
  117.4 43.6 %all-to-all-start.1 = ((bf16[16,4,16,256]{3,2,1,0:T(8,128)(2,1)}), bf16[16,4,16,256]{3,2,1,0:T(8,128)(2,1)}, u32[]{:S(2)}, u32[]{:S(2)}) async-start(bf16[16,4,16,256]{3,2,1,0:T(8,128)(2,1)} %bitcast.33), calls=%async_computation.1 | async-start | bytes 1048576 | tf_op jit(solution)/shard_map/all_to_all | solution.py:373
  138.5 43.0 %collective-permute-start.8 = (bf16[2,192,512]{2,1,0:T(8,128)(2,1)S(1)}, bf16[2,192,512]{2,1,0:T(8,128)(2,1)S(1)}, u32[]{:S(2)}, u32[]{:S(2)}) collective-permute-start(bf16[2,192,512]{2,1,0:T(8,128)(2,1)S(1)} %fusion.17.g_ref), channel_id=1, source_target_pairs={{8,0},{16,8},{24,16},{32,24},{40,32},{48,40},{56,48},{64,56},{72,6... | collective-permute-start | bytes 1179656 | tf_op jit(solution)/shard_map/ppermute | solution.py:419
  141.5 40.1 %collective-permute-start.7 = (bf16[2,192,512]{2,1,0:T(8,128)(2,1)S(1)}, bf16[2,192,512]{2,1,0:T(8,128)(2,1)}, u32[]{:S(2)}, u32[]{:S(2)}) collective-permute-start(bf16[2,192,512]{2,1,0:T(8,128)(2,1)S(1)} %fusion.17.g_ref), channel_id=1, source_target_pairs={{0,8},{8,16},{16,24},{24,32},{32,40},{40,48},{48,56},{56,64},{64,7... | collective-permute-start | bytes 1179656 | tf_op jit(solution)/shard_map/ppermute | solution.py:419
  144.4 0.7 copy-start.2
  154.5 0.8 copy-start.3
  155.2 26.3 %collective-permute-start.10 = (f32[2,4,8,384]{3,2,1,0:T(8,128)}, f32[2,4,8,384]{3,2,1,0:T(8,128)}, u32[]{:S(2)}, u32[]{:S(2)}) collective-permute-start(f32[2,4,8,384]{3,2,1,0:T(8,128)} %get-tuple-element.19), channel_id=1, source_target_pairs={{8,0},{16,8},{24,16},{32,24},{40,32},{48,40},{56,48},{64,56},{72,6... | collective-permute-start | bytes 294920 | tf_op jit(solution)/shard_map/ppermute | solution.py:425
  159.0 22.6 %collective-permute-start.9 = (f32[2,4,8,384]{3,2,1,0:T(8,128)}, f32[2,4,8,384]{3,2,1,0:T(8,128)}, u32[]{:S(2)}, u32[]{:S(2)}) collective-permute-start(f32[2,4,8,384]{3,2,1,0:T(8,128)} %get-tuple-element.19), channel_id=1, source_target_pairs={{0,8},{8,16},{16,24},{24,32},{32,40},{40,48},{48,56},{56,64},{64,7... | collective-permute-start | bytes 294920 | tf_op jit(solution)/shard_map/ppermute | solution.py:425
  162.9 34.5 %all-to-all-start.2 = ((f32[16,16,256]{2,1,0:T(8,128)}), f32[16,16,256]{2,1,0:T(8,128)}, u32[]{:S(2)}, u32[]{:S(2)}) async-start(f32[16,16,256]{2,1,0:T(8,128)} %bitcast.81), calls=%async_computation.2 | async-start | bytes 524288 | tf_op jit(solution)/shard_map/all_to_all | solution.py:376
  181.6 7.7 %copy-start.4 = (bf16[2,192,512]{2,1,0:T(8,128)(2,1)S(1)}, bf16[2,192,512]{2,1,0:T(8,128)(2,1)}, u32[]{:S(2)}) copy-start(bf16[2,192,512]{2,1,0:T(8,128)(2,1)} %copy-done.3) | copy-start | bytes 1179652
  181.6 7.7 %copy-start.7 = (bf16[2,192,1024]{2,1,0:T(8,128)(2,1)S(1)}, bf16[2,192,1024]{2,1,0:T(8,128)(2,1)}, u32[]{:S(2)}) copy-start(bf16[2,192,1024]{2,1,0:T(8,128)(2,1)} %param.9) | copy-start | bytes 2359300
  181.6 7.7 %copy-start.10 = (f32[8,1,128]{2,1,0:T(1,128)S(1)}, f32[8,1,128]{2,1,0:T(1,128)}, u32[]{:S(2)}) copy-start(f32[8,1,128]{2,1,0:T(1,128)} %copy-done.9) | copy-start | bytes 12292
  181.6 7.7 %copy-start.13 = (bf16[1024,1536]{1,0:T(8,128)(2,1)S(1)}, bf16[1024,1536]{1,0:T(8,128)(2,1)}, u32[]{:S(2)}) copy-start(bf16[1024,1536]{1,0:T(8,128)(2,1)} %get-tuple-element.14) | copy-start | bytes 9437188
  189.3 20.6 %copy-start.8 = (bf16[2,192,1024]{2,1,0:T(8,128)(2,1)S(1)}, bf16[2,192,1024]{2,1,0:T(8,128)(2,1)}, u32[]{:S(2)}) copy-start(bf16[2,192,1024]{2,1,0:T(8,128)(2,1)} %param.9) | copy-start | bytes 2359300
  199.2 19.3 %all-to-all-start.3 = ((f32[16,16,256]{2,1,0:T(8,128)}), f32[16,16,256]{2,1,0:T(8,128)S(1)}, u32[]{:S(2)}, u32[]{:S(2)}) async-start(f32[16,16,256]{2,1,0:T(8,128)} %broadcast_in_dim.24), calls=%async_computation.3 | async-start | bytes 524288 | tf_op jit(solution)/shard_map/all_to_all | solution.py:250
